TPU v7x, 512 devices: a whole 4x4x16 slice. The times are simulated.
512 devices in a mesh: dom: 64 (over y, z_lo, core), cls: 8 (over z_hi, x).
Axes of the slice: x: 4, y: 4, z: 16 (z_hi: 2, z_lo: 8; z = z_hi * 8 + z_lo), core: 2. Of those that a mesh axis runs over, the one named last changes fastest.
Arguments:
- particles: bfloat16 [36864, 4096], P('dom'), may hold values from -6 to 6
- shift_index: int32 [36864], P('dom'), may hold values from 0 to 24
- prev_class: int32 [36864], P('dom'), may hold values from 0 to 63
- prev_rotation: int32 [36864], P('dom'), may hold values from 0 to 23
- precision: float32 [36864], P('dom'), may hold values from 0.25 to 300
- references: bfloat16 [64, 98304], P('cls', 'dom')
Outputs:
- new_references: float32 [64, 98304], P('cls', 'dom')
- log_evidence: float32 [36864], P('dom')
All inputs are finite; a program needn't handle non-finite values.
Results may differ from a plain program's by a relative error of at most 0.0039.
Values may be sent and summed in bfloat16 or wider, within the bound.
No kernel may reach another device: no remote copies, remote signals or barrier semaphores. Data moves between devices by JAX's collectives and lax.ppermute only.
A program may use at most 64 MiB of HBM per device.

v0:
```python
import math

import jax
import jax.numpy as jnp
from jax import lax
from jax.sharding import PartitionSpec as P

BOX = 64
F = 4096
R = 24


two_pi = 2.0 * math.pi
shift_side = 5
class_reward = 1.0
prior_mass = 1.0


def shift_particles(particles, shift_index, box_side):
    half_width = particles.shape[1] // 2
    frequency = jnp.arange(half_width, dtype=jnp.int32)
    freq_x = frequency % box_side - box_side // 2
    freq_y = frequency // box_side
    step_x = shift_index % shift_side - 2
    step_y = shift_index // shift_side - 2
    phase_int = (freq_x[None, :] * step_x[:, None] + freq_y[None, :] * step_y[:, None]) % box_side
    phase_angle = phase_int.astype(jnp.float32) * (two_pi / box_side)
    cosine_values = jnp.cos(phase_angle)
    sine_values = jnp.sin(phase_angle)
    real_part = particles[:, :half_width].astype(jnp.float32)
    imag_part = particles[:, half_width:].astype(jnp.float32)
    out_real = real_part * cosine_values + imag_part * sine_values
    out_imag = imag_part * cosine_values - real_part * sine_values
    return jnp.concatenate([out_real, out_imag], axis=1).astype(jnp.bfloat16)


def prior_term(prev_class, prev_rotation, class_ids, rotation_ids, rotations):
    rotation_distance = jnp.abs(rotation_ids[None, :] - prev_rotation[:, None])
    rotation_distance = jnp.minimum(rotation_distance, rotations - rotation_distance).astype(
        jnp.float32
    )
    prior_spread_width = rotations / 8.0
    match_flags = (class_ids[None, :] == prev_class[:, None]).astype(jnp.float32)
    return (
        -rotation_distance * rotation_distance / (2.0 * prior_spread_width * prior_spread_width)
        + class_reward * match_flags
    )


def on_device(particles, shift_index, prev_class, prev_rotation, precision, references):
    local_classes = references.shape[0]
    columns = references.shape[1]
    gathered = lax.all_gather(references, "dom", axis=1, tiled=True)
    table = gathered.reshape(local_classes * R, F)
    half_norm = 0.5 * jnp.sum(jnp.square(table.astype(jnp.float32)), axis=1)
    candidate = jnp.arange(local_classes * R, dtype=jnp.int32)
    class_ids = lax.axis_index("cls") * local_classes + candidate // R
    rotation_ids = candidate % R
    shifted = shift_particles(particles, shift_index, BOX)
    correlation = lax.dot_general(
        shifted, table, (((1,), (1,)), ((), ())), preferred_element_type=jnp.float32
    )
    scores = precision[:, None] * (correlation - half_norm[None, :])
    scores = scores + prior_term(prev_class, prev_rotation, class_ids, rotation_ids, R)
    local_top = jnp.max(scores, axis=1)
    top_score = lax.pmax(local_top, "cls")
    exponent = jnp.exp(scores - top_score[:, None])
    total_mass = lax.psum(jnp.sum(exponent, axis=1), "cls")
    probs = exponent / total_mass[:, None]
    weights = probs.astype(jnp.bfloat16)
    numerator = lax.dot_general(
        weights, shifted, (((0,), (0,)), ((), ())), preferred_element_type=jnp.float32
    )
    numerator = numerator.reshape(local_classes, R * F)
    occupancy = jnp.sum(probs, axis=0).reshape(local_classes, R)
    start = lax.axis_index("dom") * columns
    summed, occupancy = lax.psum((numerator, occupancy), "dom")
    mine = lax.dynamic_slice_in_dim(summed, start, columns, 1)
    spread = jnp.broadcast_to(occupancy[:, :, None], (local_classes, R, F)).reshape(
        local_classes, R * F
    )
    mass_columns = lax.dynamic_slice_in_dim(spread, start, columns, 1)
    refreshed_references = mine / (mass_columns + prior_mass)
    evidence = top_score + jnp.log(total_mass)
    return (refreshed_references, evidence)


def solution(mesh):
    return jax.shard_map(
        on_device,
        mesh=mesh,
        in_specs=(P("dom", None), P("dom"), P("dom"), P("dom"), P("dom"), P("cls", "dom")),
        out_specs=(P("cls", "dom"), P("dom")),
        check_vma=False,
    )
```

profile of v0, /device:TPU:1, one launch (start us, length us, event | category | flops | bytes accessed | tf_op | source)
XLA Modules:
  0.0 1063.9 jit_solution(16293794462568525287)
XLA Ops:
  7.2 0.0 all-gather.2.cloned.1.call-start
  7.2 0.7 all-gather.2.cloned.1.call-update
  7.9 0.0 all-reduce.2.cloned.1.call-start
  8.0 0.7 fusion.28
  8.7 23.3 %fusion.1 = (bf16[576,2048]{1,0:T(8,128)(2,1)}, bf16[576,2048]{1,0:T(8,128)(2,1)}) fusion(s32[576]{0:T(1024)S(1)} %get-tuple-element.5, s32[2048]{0:T(1024)S(1)} %get-tuple-element.8, s32[576]{0:T(1024)S(1)} %get-tuple-element.4, s32[2048]{0:T(1024)S(1)} %get-tuple-element.9, bf16[576,4096]{1,0:T(8,128)(2,1)} %param.6), kind=kLoop, calls=%fused_computation.8 | loop fusion | flops 30670848 | bytes 9458176 | tf_op jit(solution)/shard_map/convert
  32.0 0.0 copy-start.1
  32.0 0.0 copy-start.2
  32.0 0.0 copy-start.3
  32.0 104.3 %all-gather.2.cloned.1.call-done = bf16[8,98304]{1,0:T(8,128)(2,1)} async-done(((bf16[8,1536]{1,0:T(8,128)(2,1)}), bf16[8,98304]{1,0:T(8,128)(2,1)}) %all-gather.2.cloned.1.call-update) | async-done | bytes 1572880 | tf_op jit(solution)/shard_map/all_gather | solution.py:53
  136.3 2.1 reshape.71
  138.4 0.4 multiply_reduce_fusion
  138.8 0.0 copy-done.1
  138.8 0.0 copy-done.2
  138.8 0.0 copy-done.3
  138.8 4.3 fusion.35
  143.1 0.0 copy-start
  143.1 38.3 %pmax.7 = f32[576]{0:T(1024)S(1)} all-reduce(f32[576]{0:T(1024)S(1)} %get-tuple-element.6), channel_id=1, replica_groups=mesh['dom'=64,'cls'=8] {'cls'}, use_global_device_ids=true, to_apply=%region_2.3 | all-reduce | flops 576 | bytes 4608 | tf_op jit(solution)/shard_map/pmax | solution.py:66
  181.5 0.1 fusion.18
  181.6 0.0 copy-done
  181.6 29.9 %psum.21 = f32[576]{0:T(1024)S(1)} all-reduce(f32[576]{0:T(1024)S(1)} %fusion.18), channel_id=1, replica_groups=mesh['dom'=64,'cls'=8] {'cls'}, use_global_device_ids=true, to_apply=%region_4.5 | all-reduce | flops 576 | bytes 4608 | tf_op jit(solution)/shard_map/psum | solution.py:68
  211.5 3.9 fusion.7
  215.5 2.3 reshape.72
  217.7 0.0 all-reduce.2.cloned.1.call-update
  217.7 1.2 fusion.20
  218.9 0.1 reshape.73
  219.0 217.7 %psum.23 = f32[8,24]{1,0:T(8,128)S(1)} all-reduce(f32[8,24]{1,0:T(8,128)S(1)} %reshape.73), channel_id=1, replica_groups=mesh['dom'=64,'cls'=8] {'dom'}, use_global_device_ids=true, to_apply=%region_7.8 | all-reduce | flops 192 | bytes 1536 | tf_op jit(solution)/shard_map/psum | solution.py:77
  436.7 0.1 copy.8
  436.8 0.6 log_add_fusion
  437.4 618.0 %all-reduce.2.cloned.1.call-done = f32[8,98304]{1,0:T(8,128)} async-done(((f32[8,98304]{1,0:T(8,128)}), f32[8,98304]{1,0:T(8,128)}) %all-reduce.2.cloned.1.call-update) | async-done | bytes 3145744 | tf_op jit(solution)/shard_map/psum | solution.py:77
  1055.3 0.3 broadcast_in_dim.2
  1055.6 1.4 add_divide_fusion
  (3 shorter events, 0.0 us)
Async XLA Ops:
  7.2 129.1 %all-gather.2.cloned.1.call-start = ((), (), s32[]{:S(2)}) async-start(), calls=%async_computation | async-start | bytes 1597440 | tf_op jit(solution)/shard_map/all_gather | solution.py:53
  7.9 1047.4 %all-reduce.2.cloned.1.call-start = ((), (), s32[]{:S(2)}) async-start(), calls=%async_computation.1 | async-start | bytes 6291456 | tf_op jit(solution)/shard_map/psum | solution.py:77
  32.0 106.8 %copy-start.1 = (s32[576]{0:T(1024)S(1)}, s32[576]{0:T(1024)}, u32[]{:S(2)}) copy-start(s32[576]{0:T(1024)} %param.8) | copy-start | bytes 6916
  32.0 106.8 %copy-start.2 = (s32[576]{0:T(1024)S(1)}, s32[576]{0:T(1024)}, u32[]{:S(2)}) copy-start(s32[576]{0:T(1024)} %param.9) | copy-start | bytes 6916
  32.0 106.8 %copy-start.3 = (f32[576]{0:T(1024)S(1)}, f32[576]{0:T(1024)}, u32[]{:S(2)}) copy-start(f32[576]{0:T(1024)} %param.10) | copy-start | bytes 6916
  143.1 38.4 %copy-start = (f32[576,192]{0,1:T(8,128)}, f32[576,192]{0,1:T(8,128)S(1)}, u32[]{:S(2)}) copy-start(f32[576,192]{0,1:T(8,128)S(1)} %get-tuple-element.7) | copy-start | bytes 1327108
Sparse Core Ops, SparseCore 0:
  10.1 126.0 all-gather.1
  217.9 837.4 all-reduce.1
where the time goes:
time: 1060 us
  waiting for transfers between devices  723 us (68%)
  blocking collectives  286 us (27%)
  other arithmetic  27.7 us (3%)
  between operations  14.1 us (1%)
    psum x1, waiting for transfers between devices, on_device(): summed, occupancy = lax.psum((numerator, occupancy), 'dom')  618 us
    psum x1, blocking collectives, on_device(): summed, occupancy = lax.psum((numerator, occupancy), 'dom')  218 us
    all_gather x1, waiting for transfers between devices, on_device(): gathered = lax.all_gather(references, 'dom', axis=1, tiled=True)  104 us
    pmax x1, blocking collectives, on_device(): top_score = lax.pmax(local_top, 'cls')  38.3 us
    psum x1, blocking collectives, on_device(): total_mass = lax.psum(jnp.sum(exponent, axis=1), 'cls')  29.9 us
    another operation x1, other arithmetic  23.3 us
  transfers between devices with their start and end apart: 2, of which 2 were waited for; matrix products, arithmetic and copies ran while one was open for 2% of the time, Pallas kernels for 0%

commit v1 on v0

v1 whole, which is shorter than its diff:
```python
import math

import jax
import jax.numpy as jnp
from jax import lax
from jax.experimental import pallas as pl
from jax.experimental.pallas import tpu as pltpu
from jax.sharding import Mesh
from jax.sharding import PartitionSpec as P

BOX = 64
F = 4096
H = F // 2
R = 24
K = 8
ROWS = K * R
SHIFTS = 25
SIDE = 5
P_DEV = 576
ROW_BLOCK = 96
TILES = 12

bf16 = jnp.bfloat16
f32 = jnp.float32

Z = ("za", "zb")
CLS = ("zh", "x")
DOM = ("y", "za", "zb", "c")


def phase_table():
    frequency = jnp.arange(H, dtype=jnp.int32)
    freq_x = frequency % BOX - BOX // 2
    freq_y = frequency // BOX
    shift = jnp.arange(SHIFTS, dtype=jnp.int32)
    step_x = shift % SIDE - 2
    step_y = shift // SIDE - 2
    phase = (freq_x[None, :] * step_x[:, None] + freq_y[None, :] * step_y[:, None]) % BOX
    angle = phase.astype(f32) * (2.0 * math.pi / BOX)
    exact = jnp.concatenate([jnp.cos(angle), jnp.sin(angle)], axis=1)
    high = lax.reduce_precision(exact, 8, 7)
    rest = exact - high
    middle = lax.reduce_precision(rest, 8, 7)
    low = rest - middle
    return jnp.concatenate([high, middle, low, jnp.zeros((128 - 3 * SHIFTS, F), f32)], axis=0).astype(bf16)


def shift_kernel(index_ref, table_ref, image_ref, out_ref):
    index = index_ref[...]
    lane = lax.broadcasted_iota(jnp.int32, (ROW_BLOCK, 128), 1)
    chosen = (lane == index) | (lane == index + SHIFTS) | (lane == index + 2 * SHIFTS)
    chosen = jnp.where(chosen, 1.0, 0.0).astype(bf16)
    for at in range(0, H, 512):
        cosine = jnp.dot(chosen, table_ref[:, at : at + 512], preferred_element_type=f32)
        sine = jnp.dot(chosen, table_ref[:, H + at : H + at + 512], preferred_element_type=f32)
        real = image_ref[:, at : at + 512].astype(f32)
        imag = image_ref[:, H + at : H + at + 512].astype(f32)
        out_ref[:, at : at + 512] = (real * cosine + imag * sine).astype(bf16)
        out_ref[:, H + at : H + at + 512] = (imag * cosine - real * sine).astype(bf16)


def shift_particles(particles, shift_index):
    return pl.pallas_call(
        shift_kernel,
        grid=(P_DEV // ROW_BLOCK,),
        in_specs=[
            pl.BlockSpec((ROW_BLOCK, 1), lambda i: (i, 0)),
            pl.BlockSpec((128, F), lambda i: (0, 0)),
            pl.BlockSpec((ROW_BLOCK, F), lambda i: (i, 0)),
        ],
        out_specs=pl.BlockSpec((ROW_BLOCK, F), lambda i: (i, 0)),
        out_shape=jax.ShapeDtypeStruct((P_DEV, F), bf16),
        compiler_params=pltpu.CompilerParams(vmem_limit_bytes=24 << 20),
        name="shift",
    )(shift_index[:, None], phase_table(), particles)


def exchange(array, axis):
    return lax.all_to_all(array, axis, 0, 0, tiled=True)


def gather_table(references):
    mine = references.reshape(K, TILES, 128).transpose(1, 0, 2)
    along_z = exchange(jnp.broadcast_to(mine, (8, TILES, K, 128)), Z)
    along_y = exchange(jnp.broadcast_to(along_z, (4, 8, TILES, K, 128)), "y")
    both = lax.all_gather(along_y, "c", axis=0)
    both = both.reshape(2, 4, 2, 4, TILES, K, 128)
    both = both.transpose(1, 2, 3, 0, 4, 5, 6).reshape(8, 3, 32, K, 128)
    return both.transpose(0, 1, 3, 2, 4).reshape(ROWS, F)


def scatter_sums(numerator, occupancy):
    pieces = numerator.reshape(8, 3, K, 32, 128).transpose(0, 1, 3, 2, 4)
    pieces = pieces.reshape(4, 2, 4, 2, TILES, K, 128).transpose(3, 0, 1, 2, 4, 5, 6)
    spread = jnp.broadcast_to(occupancy.reshape(8, 3, 1, K), (8, 3, 8, K))
    spread = spread.reshape(4, 2, 4, 2, 3, K).transpose(3, 0, 1, 2, 5, 4)
    high = lax.reduce_precision(spread, 8, 7)
    extra = jnp.concatenate([high, spread - high, jnp.zeros((2, 4, 2, 4, K, 122), f32)], axis=-1)
    pieces = jnp.concatenate([pieces, extra[:, :, :, :, None]], axis=4).astype(bf16)
    pieces = exchange(pieces, "c").astype(f32)
    pieces = jnp.sum(pieces, axis=0).astype(bf16)
    pieces = exchange(pieces, "y").astype(f32)
    pieces = jnp.sum(pieces, axis=0).astype(bf16)
    pieces = pieces.reshape(8, TILES + 1, K, 128)
    pieces = exchange(pieces, Z).astype(f32)
    pieces = jnp.sum(pieces, axis=0)
    summed = pieces[:TILES].reshape(3, 4, K, 128).transpose(2, 0, 1, 3)
    mass = pieces[TILES, :, 0:3] + pieces[TILES, :, 3:6]
    return summed, mass


def on_device(particles, shift_index, prev_class, prev_rotation, precision, references):
    table = gather_table(references)
    shifted = shift_particles(particles, shift_index)
    half_norm = 0.5 * jnp.sum(jnp.square(table.astype(f32)), axis=1)
    row = jnp.arange(ROWS, dtype=jnp.int32)
    class_ids = lax.axis_index(CLS) * K + row % K
    rotation_ids = row // K
    correlation = lax.dot_general(table, shifted, (((1,), (1,)), ((), ())), preferred_element_type=f32)
    scores = precision[None, :] * (correlation - half_norm[:, None])
    distance = jnp.abs(rotation_ids[:, None] - prev_rotation[None, :])
    distance = jnp.minimum(distance, R - distance).astype(f32)
    width = R / 8.0
    match = (class_ids[:, None] == prev_class[None, :]).astype(f32)
    scores = scores + (-distance * distance / (2.0 * width * width) + match)
    local_top = jnp.max(scores, axis=0)
    local_mass = jnp.sum(jnp.exp(scores - local_top[None, :]), axis=0)
    stats = jnp.stack([local_top, local_mass])
    stats = exchange(jnp.broadcast_to(stats, (8, 2, P_DEV)), CLS)
    top_score = jnp.max(stats[:, 0], axis=0)
    total_mass = jnp.sum(stats[:, 1] * jnp.exp(stats[:, 0] - top_score[None, :]), axis=0)
    probs = jnp.exp(scores - top_score[None, :]) / total_mass[None, :]
    weights = probs.astype(bf16)
    numerator = lax.dot_general(weights, shifted, (((1,), (0,)), ((), ())), preferred_element_type=f32)
    summed, mass = scatter_sums(numerator, jnp.sum(probs, axis=1))
    refreshed = summed / (mass[:, :, None, None] + 1.0)
    evidence = top_score + jnp.log(total_mass)
    return (refreshed.reshape(K, TILES * 128), evidence)


def solution(mesh):
    split = Mesh(mesh.devices.reshape(4, 2, 4, 2, 2, 4), DOM + CLS)
    return jax.shard_map(
        on_device,
        mesh=split,
        in_specs=(P(DOM, None), P(DOM), P(DOM), P(DOM), P(DOM), P(CLS, DOM)),
        out_specs=(P(CLS, DOM), P(DOM)),
        check_vma=False,
    )
```

time: 1060 us -> 157 us (0.15)
  the two profiles are of different devices: /device:TPU:1 before, /device:TPU:32 now
where the time goes in v1:
time: 157 us; the launch traced here: 156 us
  blocking collectives  48.5 us (31%)
  waiting for transfers between devices  43.2 us (28%)
  starting transfers between devices  22.8 us (15%)
  between operations  14.3 us (9%)
  local copies, waits for them, and re-layouts  10.6 us (7%)
  matrix products  8.02 us (5%)
  other arithmetic  5.35 us (3%)
  Pallas kernels  3.57 us (2%)
    all_to_all x3, blocking collectives, exchange(): return lax.all_to_all(array, axis, 0, 0, tiled=True)  48.5 us
    all_to_all x3, waiting for transfers between devices, exchange(): return lax.all_to_all(array, axis, 0, 0, tiled=True)  37.5 us
    all_to_all x3, starting transfers between devices, exchange(): return lax.all_to_all(array, axis, 0, 0, tiled=True)  22.8 us
    all_gather x1, waiting for transfers between devices, gather_table(): both = lax.all_gather(along_y, 'c', axis=0)  5.69 us
    unnamed x14, local copies, waits for them, and re-layouts  5.36 us
    dot_general x1, matrix products, on_device(): lax.dot_general(table, shifted, (((1,), (1,)), ((), ())), preferred_eleme...  4.28 us
    dot_general x1, matrix products, on_device(): lax.dot_general(weights, shifted, (((1,), (0,)), ((), ())), preferred_ele...  3.74 us
    pallas_call x1, Pallas kernels, shift_particles(): pl.pallas_call(shift_kernel, grid=(P_DEV // ROW_BLOCK,), in_specs=[pl.Blo...  3.57 us
  transfers between devices with their start and end apart: 4, of which 4 were waited for; matrix products, arithmetic and copies ran while one was open for 2% of the time, Pallas kernels for 2%

profile of v1, /device:TPU:32, one launch (start us, length us, event | category | flops | bytes accessed | tf_op | source)
XLA Modules:
  0.0 156.3 jit_solution(15482700913709956621)
XLA Ops:
  7.2 0.8 broadcast_in_dim.21
  7.9 26.0 %all_to_all.30 = bf16[8,12,8,128]{3,2,1,0:T(8,128)(2,1)S(1)} all-to-all(bf16[8,12,8,128]{3,2,1,0:T(8,128)(2,1)S(1)} %broadcast_in_dim.21), channel_id=1, replica_groups=mesh['y'=4,'za'=2,'zb'=4,'c'=2,'zh'=2,'x'=4] {'za','zb'}, dimensions={0} | all-to-all | bytes 393216 | tf_op jit(solution)/shard_map/all_to_all | solution.py:79
  34.0 1.0 broadcast_in_dim.22
  35.0 4.5 %all-to-all-start.1 = ((bf16[4,8,12,8,128]{4,3,2,1,0:T(8,128)(2,1)}), bf16[4,8,12,8,128]{4,3,2,1,0:T(8,128)(2,1)S(1)}, u32[]{:S(2)}, u32[]{:S(2)}) async-start(bf16[4,8,12,8,128]{4,3,2,1,0:T(8,128)(2,1)} %broadcast_in_dim.22), calls=%async_computation.1 | async-start | bytes 1572864 | tf_op jit(solution)/shard_map/all_to_all | solution.py:79
  39.5 9.5 %all-to-all-done.1 = bf16[4,8,12,8,128]{4,3,2,1,0:T(8,128)(2,1)S(1)} async-done(((bf16[4,8,12,8,128]{4,3,2,1,0:T(8,128)(2,1)}), bf16[4,8,12,8,128]{4,3,2,1,0:T(8,128)(2,1)S(1)}, u32[]{:S(2)}, u32[]{:S(2)}) %all-to-all-start.1) | async-done | bytes 786464 | tf_op jit(solution)/shard_map/all_to_all | solution.py:79
  48.9 0.9 copy-done.2
  49.8 1.1 fusion.13
  51.0 0.1 broadcast_in_dim.53.index_ref
  51.3 0.3 maximum_maximum_fusion.table_ref
  51.6 2.3 %copy-done = bf16[576,4096]{1,0:T(8,128)(2,1)S(1)} copy-done((bf16[576,4096]{1,0:T(8,128)(2,1)S(1)}, bf16[576,4096]{1,0:T(8,128)(2,1)}, u32[]{:S(2)}) %copy-start) | copy-done | bytes 4718616
  53.9 3.6 %shift.1 = bf16[576,4096]{1,0:T(8,128)(2,1)S(1)} custom-call(s32[576,1]{1,0:T(8,128)S(1)} %broadcast_in_dim.53.index_ref, bf16[128,4096]{1,0:T(8,128)(2,1)S(1)} %maximum_maximum_fusion.table_ref, bf16[576,4096]{1,0:T(8,128)(2,1)S(1)} %copy-done), custom_call_target="tpu_custom_call" | custom-call | tf_op jit(solution)/shard_map/shift/pallas_call | solution.py:63
  57.5 2.1 %copy-done.1 = bf16[576,4096]{1,0:T(8,128)(2,1)} copy-done((bf16[576,4096]{1,0:T(8,128)(2,1)}, bf16[576,4096]{1,0:T(8,128)(2,1)S(1)}, u32[]{:S(2)}) %copy-start.1) | copy-done | bytes 4718616
  59.6 5.7 %all-gather.3.cloned.1.call-done = bf16[8,8,12,8,128]{4,3,2,1,0:T(8,128)(2,1)} async-done(((bf16[4,8,12,8,128]{4,3,2,1,0:T(8,128)(2,1)}), bf16[8,8,12,8,128]{4,3,2,1,0:T(8,128)(2,1)}) %all-gather.3.cloned.1.call-update) | async-done | bytes 1572880 | tf_op jit(solution)/shard_map/all_gather | solution.py:86
  65.3 1.6 %copy.44 = bf16[4,2,4,2,12,8,128]{6,5,4,3,2,1,0:T(8,128)(2,1)S(1)} copy(bf16[4,2,4,2,12,8,128]{6,5,4,2,1,0,3:T(8,128)(2,1)} %bitcast.51) | data formatting | bytes 3145728 | tf_op jit(solution)/shard_map/transpose | solution.py:88
  67.0 0.4 multiply_reduce_fusion
  67.5 4.3 %fusion.31 = (f32[576]{0:T(1024)S(1)}, f32[192,576]{1,0:T(8,128)S(1)}) fusion(s32[576]{0:T(1024)S(1)} %copy-done.4, s32[192]{0:T(256)S(1)} %get-tuple-element.19, s32[576]{0:T(1024)S(1)} %copy-done.5, s32[192]{0:T(256)S(1)} %get-tuple-element.18, f32[192]{0:T(256)S(1)} %mul.93, bf16[576,4096]{1,0:T(8,128)(2,1)} %copy-done.1, ...), kind=kOutput, calls=%fused_computation.74 | convolution fusion | flops 907627968 | bytes 6745344 | tf_op jit(solution)/shard_map/dot_general | solution.py:119
  71.9 0.6 broadcast_in_dim.23
  72.6 13.7 %all-to-all-start.2 = ((f32[8,2,576]{2,1,0:T(2,128)}), f32[8,2,576]{2,1,0:T(2,128)S(1)}, u32[]{:S(2)}, u32[]{:S(2)}) async-start(f32[8,2,576]{2,1,0:T(2,128)} %broadcast_in_dim.23), calls=%async_computation.2 | async-start | bytes 81920 | tf_op jit(solution)/shard_map/all_to_all | solution.py:79
  86.3 14.9 %all-to-all-done.2 = f32[8,2,576]{2,1,0:T(2,128)S(1)} async-done(((f32[8,2,576]{2,1,0:T(2,128)}), f32[8,2,576]{2,1,0:T(2,128)S(1)}, u32[]{:S(2)}, u32[]{:S(2)}) %all-to-all-start.2) | async-done | bytes 36896 | tf_op jit(solution)/shard_map/all_to_all | solution.py:79
  101.3 0.2 fusion.14
  101.5 3.7 %convolution_convert_fusion = bf16[192,4096]{1,0:T(8,128)(2,1)S(1)} fusion(bf16[576,4096]{1,0:T(8,128)(2,1)} %copy-done.1, f32[192,576]{1,0:T(8,128)S(1)} %get-tuple-element.13, f32[576]{0:T(1024)S(1)} %fusion.18, f32[576]{0:T(1024)S(1)} %get-tuple-element.7), kind=kOutput, calls=%fused_computation | convolution fusion | flops 907087872 | bytes 6738432 | tf_op jit(solution)/shard_map/dot_general | solution.py:134
  105.4 0.4 copy.47
  106.0 0.2 pad_maximum_fusion
  106.2 0.2 copy.48
  106.4 5.1 %all_to_all.31 = bf16[2,4,2,4,13,8,128]{6,5,4,3,2,1,0:T(8,128)(2,1)S(1)} all-to-all(bf16[2,4,2,4,13,8,128]{6,5,4,3,2,1,0:T(8,128)(2,1)S(1)} %copy.48), channel_id=1, replica_groups=mesh['y'=4,'za'=2,'zb'=4,'c'=2,'zh'=2,'x'=4] {'c'}, dimensions={0} | all-to-all | bytes 3407872 | tf_op jit(solution)/shard_map/all_to_all | solution.py:79
  111.5 0.5 reduce_sum.73
  112.0 17.4 %all_to_all.32 = bf16[4,2,4,13,8,128]{5,4,3,2,1,0:T(8,128)(2,1)S(1)} all-to-all(bf16[4,2,4,13,8,128]{5,4,3,2,1,0:T(8,128)(2,1)S(1)} %reduce_sum.73), channel_id=1, replica_groups=mesh['y'=4,'za'=2,'zb'=4,'c'=2,'zh'=2,'x'=4] {'y'}, dimensions={0} | all-to-all | bytes 1703936 | tf_op jit(solution)/shard_map/all_to_all | solution.py:79
  129.4 0.8 reduce_sum.74
  130.2 4.7 %all-to-all-start.5 = ((bf16[8,13,8,128]{3,2,1,0:T(8,128)(2,1)}), bf16[8,13,8,128]{3,2,1,0:T(8,128)(2,1)S(1)}, u32[]{:S(2)}, u32[]{:S(2)}) async-start(bf16[8,13,8,128]{3,2,1,0:T(8,128)(2,1)} %bitcast.17), calls=%async_computation.5 | async-start | bytes 425984 | tf_op jit(solution)/shard_map/all_to_all | solution.py:79
  134.9 0.6 log_add_fusion
  135.5 13.1 %all-to-all-done.5 = bf16[8,13,8,128]{3,2,1,0:T(8,128)(2,1)S(1)} async-done(((bf16[8,13,8,128]{3,2,1,0:T(8,128)(2,1)}), bf16[8,13,8,128]{3,2,1,0:T(8,128)(2,1)S(1)}, u32[]{:S(2)}, u32[]{:S(2)}) %all-to-all-start.5) | async-done | bytes 213024 | tf_op jit(solution)/shard_map/all_to_all | solution.py:79
  148.8 0.7 broadcast_divide_fusion
  (38 shorter events, 1.1 us)
Async XLA Ops:
  7.9 43.0 %copy-start.3 = (s32[576]{0:T(1024)S(1)}, s32[576]{0:T(1024)}, u32[]{:S(2)}) copy-start(s32[576]{0:T(1024)} %param.7) | copy-start | bytes 6916
  35.0 14.0 %all-to-all-start.1 = ((bf16[4,8,12,8,128]{4,3,2,1,0:T(8,128)(2,1)}), bf16[4,8,12,8,128]{4,3,2,1,0:T(8,128)(2,1)S(1)}, u32[]{:S(2)}, u32[]{:S(2)}) async-start(bf16[4,8,12,8,128]{4,3,2,1,0:T(8,128)(2,1)} %broadcast_in_dim.22), calls=%async_computation.1 | async-start | bytes 1572864 | tf_op jit(solution)/shard_map/all_to_all | solution.py:79
  39.4 25.9 %all-gather.3.cloned.1.call-start = ((), (), s32[]{:S(2)}) async-start(), calls=%async_computation.6 | async-start | bytes 2359296 | tf_op jit(solution)/shard_map/all_gather | solution.py:86
  48.9 0.9 copy-start.2
  51.6 2.3 %copy-start = (bf16[576,4096]{1,0:T(8,128)(2,1)S(1)}, bf16[576,4096]{1,0:T(8,128)(2,1)}, u32[]{:S(2)}) copy-start(bf16[576,4096]{1,0:T(8,128)(2,1)} %image_ref.1) | copy-start | bytes 14155780
  57.5 2.1 %copy-start.1 = (bf16[576,4096]{1,0:T(8,128)(2,1)}, bf16[576,4096]{1,0:T(8,128)(2,1)S(1)}, u32[]{:S(2)}) copy-start(bf16[576,4096]{1,0:T(8,128)(2,1)S(1)} %shift.1) | copy-start | bytes 14155780
  65.3 2.2 %copy-start.4 = (s32[576]{0:T(1024)S(1)}, s32[576]{0:T(1024)}, u32[]{:S(2)}) copy-start(s32[576]{0:T(1024)} %param.8) | copy-start | bytes 6916
  65.3 2.2 %copy-start.5 = (s32[576]{0:T(1024)S(1)}, s32[576]{0:T(1024)}, u32[]{:S(2)}) copy-start(s32[576]{0:T(1024)} %param.9) | copy-start | bytes 6916
  65.3 2.2 %copy-start.6 = (f32[576]{0:T(1024)S(1)}, f32[576]{0:T(1024)}, u32[]{:S(2)}) copy-start(f32[576]{0:T(1024)} %param.10) | copy-start | bytes 6916
  72.6 28.7 %all-to-all-start.2 = ((f32[8,2,576]{2,1,0:T(2,128)}), f32[8,2,576]{2,1,0:T(2,128)S(1)}, u32[]{:S(2)}, u32[]{:S(2)}) async-start(f32[8,2,576]{2,1,0:T(2,128)} %broadcast_in_dim.23), calls=%async_computation.2 | async-start | bytes 81920 | tf_op jit(solution)/shard_map/all_to_all | solution.py:79
  130.2 18.4 %all-to-all-start.5 = ((bf16[8,13,8,128]{3,2,1,0:T(8,128)(2,1)}), bf16[8,13,8,128]{3,2,1,0:T(8,128)(2,1)S(1)}, u32[]{:S(2)}, u32[]{:S(2)}) async-start(bf16[8,13,8,128]{3,2,1,0:T(8,128)(2,1)} %bitcast.17), calls=%async_computation.5 | async-start | bytes 425984 | tf_op jit(solution)/shard_map/all_to_all | solution.py:79
Sparse Core Ops, SparseCore 0:
  50.0 15.3 all-gather.2

commit v2 on v1

v2 whole, which is shorter than its diff:
```python
import math

import jax
import jax.numpy as jnp
from jax import lax
from jax.experimental import pallas as pl
from jax.experimental.pallas import tpu as pltpu
from jax.sharding import Mesh
from jax.sharding import PartitionSpec as P

BOX = 64
F = 4096
H = F // 2
R = 24
K = 8
ROWS = K * R
SHIFTS = 25
SIDE = 5
P_DEV = 576
ROW_BLOCK = 96
TILES = 12

bf16 = jnp.bfloat16
f32 = jnp.float32

Z = ("za", "zb")
CLS = ("zh", "x")
DOM = ("y", "za", "zb", "c")


def phase_table():
    frequency = jnp.arange(H, dtype=jnp.int32)
    freq_x = frequency % BOX - BOX // 2
    freq_y = frequency // BOX
    shift = jnp.arange(SHIFTS, dtype=jnp.int32)
    step_x = shift % SIDE - 2
    step_y = shift // SIDE - 2
    phase = (freq_x[None, :] * step_x[:, None] + freq_y[None, :] * step_y[:, None]) % BOX
    angle = phase.astype(f32) * (2.0 * math.pi / BOX)
    exact = jnp.concatenate([jnp.cos(angle), jnp.sin(angle)], axis=1)
    high = lax.reduce_precision(exact, 8, 7)
    rest = exact - high
    middle = lax.reduce_precision(rest, 8, 7)
    low = rest - middle
    return jnp.concatenate([high, middle, low, jnp.zeros((128 - 3 * SHIFTS, F), f32)], axis=0).astype(bf16)


def shift_kernel(index_ref, table_ref, image_ref, out_ref):
    index = index_ref[...]
    lane = lax.broadcasted_iota(jnp.int32, (ROW_BLOCK, 128), 1)
    chosen = (lane == index) | (lane == index + SHIFTS) | (lane == index + 2 * SHIFTS)
    chosen = jnp.where(chosen, 1.0, 0.0).astype(bf16)
    for at in range(0, H, 512):
        cosine = jnp.dot(chosen, table_ref[:, at : at + 512], preferred_element_type=f32)
        sine = jnp.dot(chosen, table_ref[:, H + at : H + at + 512], preferred_element_type=f32)
        real = image_ref[:, at : at + 512].astype(f32)
        imag = image_ref[:, H + at : H + at + 512].astype(f32)
        out_ref[:, at : at + 512] = (real * cosine + imag * sine).astype(bf16)
        out_ref[:, H + at : H + at + 512] = (imag * cosine - real * sine).astype(bf16)


def shift_particles(particles, shift_index):
    return pl.pallas_call(
        shift_kernel,
        grid=(P_DEV // ROW_BLOCK,),
        in_specs=[
            pl.BlockSpec((ROW_BLOCK, 1), lambda i: (i, 0)),
            pl.BlockSpec((128, F), lambda i: (0, 0)),
            pl.BlockSpec((ROW_BLOCK, F), lambda i: (i, 0)),
        ],
        out_specs=pl.BlockSpec((ROW_BLOCK, F), lambda i: (i, 0)),
        out_shape=pltpu.HBM((P_DEV, F), bf16),
        compiler_params=pltpu.CompilerParams(vmem_limit_bytes=16 << 20),
        name="shift",
    )(shift_index[:, None], phase_table(), particles)


def exchange(array, axis):
    return lax.all_to_all(array, axis, 0, 0, tiled=True)


def gather_table(references, shifted_of):
    mine = references.reshape(K, TILES, 128).transpose(1, 0, 2)
    along_z = exchange(jnp.broadcast_to(mine, (8, TILES, K, 128)), Z)
    along_z, shifted = lax.optimization_barrier((along_z, shifted_of()))
    along_y = exchange(jnp.broadcast_to(along_z, (4, 8, TILES, K, 128)), "y")
    other = lax.ppermute(along_y, "c", [(0, 1), (1, 0)])
    return along_y.reshape(8, 4, TILES, K, 128), other.reshape(8, 4, TILES, K, 128), shifted


def column_copies(source_ref, target_ref, arrived):
    copies = []
    for q in range(8):
        columns = pl.ds(q * 512, 512)
        copies.append(pltpu.make_async_copy(source_ref.at[:, columns], target_ref.at[:, columns], arrived.at[q]))
        copies[-1].start()
    return copies


def score_kernel(place_ref, own_ref, other_ref, shifted_ref, class_ref, rotation_ref, precision_ref, scores_ref, stats_ref, table_ref, images_ref, arrived):
    copies = column_copies(shifted_ref, images_ref, arrived)
    core = place_ref[0]
    for source, at in ((own_ref, core), (other_ref, 1 - core)):
        for zb in range(4):
            for b in range(3):
                part = 6 * zb + 3 * at + b
                turn = part // 8
                column = (part - 8 * turn) * 512
                rows = pl.ds(pl.multiple_of(turn * 64, 64), 64)
                for lanes in range(4):
                    tiles = source[:, zb, 4 * b + lanes].reshape(64, 128)
                    table_ref[rows, pl.ds(pl.multiple_of(column + lanes * 128, 128), 128)] = tiles
    half_norm = jnp.zeros((ROWS, 128), f32)
    for at in range(0, F, 128):
        piece = table_ref[:, at : at + 128].astype(f32)
        half_norm = half_norm + piece * piece
    half_norm = 0.5 * jnp.sum(half_norm, axis=1, keepdims=True)
    for copy in copies:
        copy.wait()
    correlation = lax.dot_general(table_ref[...], images_ref[...], (((1,), (1,)), ((), ())), preferred_element_type=f32)
    row = lax.broadcasted_iota(jnp.int32, (ROWS, 1), 0)
    class_ids = place_ref[1] + row % K
    rotation_ids = (row // K) % 8 * 3 + row // 64
    distance = jnp.abs(rotation_ids - rotation_ref[...])
    distance = jnp.minimum(distance, R - distance).astype(f32)
    width = R / 8.0
    match = jnp.where(class_ids == class_ref[...], 1.0, 0.0)
    scores = precision_ref[...] * (correlation - half_norm) + (-distance * distance / (2.0 * width * width) + match)
    scores_ref[...] = scores
    top = jnp.max(scores, axis=0, keepdims=True)
    mass = jnp.sum(jnp.exp(scores - top), axis=0, keepdims=True)
    for at in range(8):
        stats_ref[at, 0:1, :] = top
        stats_ref[at, 1:2, :] = mass


def local_scores(own, other, shifted, prev_class, prev_rotation, precision):
    place = jnp.stack([lax.axis_index("c"), lax.axis_index(CLS) * K]).astype(jnp.int32)
    vmem = pl.BlockSpec(memory_space=pltpu.VMEM)
    return pl.pallas_call(
        score_kernel,
        in_specs=[pl.BlockSpec(memory_space=pltpu.SMEM), vmem, vmem, pl.BlockSpec(memory_space=pltpu.HBM)] + [vmem] * 3,
        out_specs=[vmem, vmem],
        out_shape=[jax.ShapeDtypeStruct((ROWS, P_DEV), f32), jax.ShapeDtypeStruct((8, 2, P_DEV), f32)],
        scratch_shapes=[pltpu.VMEM((ROWS, F), bf16), pltpu.VMEM((P_DEV, F), bf16), pltpu.SemaphoreType.DMA((8,))],
        compiler_params=pltpu.CompilerParams(vmem_limit_bytes=16 << 20),
        name="scores",
    )(place, own, other, shifted, prev_class[None, :], prev_rotation[None, :], precision[None, :])


def sum_kernel(stats_ref, scores_ref, shifted_ref, pieces_ref, evidence_ref, images_ref, arrived):
    copies = column_copies(shifted_ref, images_ref, arrived)
    tops = [stats_ref[i, 0:1, :] for i in range(8)]
    top = tops[0]
    for i in range(1, 8):
        top = jnp.maximum(top, tops[i])
    mass = jnp.zeros_like(top)
    for i in range(8):
        mass = mass + stats_ref[i, 1:2, :] * jnp.exp(tops[i] - top)
    evidence_ref[...] = top + jnp.log(mass)
    probs = jnp.exp(scores_ref[...] - top) * (1.0 / mass)
    weights = probs.astype(bf16)
    occupancy = jnp.sum(probs, axis=1, keepdims=True)
    high = occupancy.astype(bf16).astype(f32)
    low = occupancy - high
    lane = lax.broadcasted_iota(jnp.int32, (8, K, 128), 2)
    high = [high[64 * turn : 64 * turn + 64].reshape(8, K, 1) for turn in range(3)]
    low = [low[64 * turn : 64 * turn + 64].reshape(8, K, 1) for turn in range(3)]
    for j in range(8):
        tile = jnp.zeros((8, K, 128), f32)
        for b in range(3):
            turn = (3 * j + b) // 8
            tile = jnp.where(lane == b, high[turn], tile)
            tile = jnp.where(lane == 3 + b, low[turn], tile)
        pieces_ref[j % 2, :, j // 2, TILES] = tile.astype(bf16)
    for q in range(8):
        copies[q].wait()
        numerator = jnp.dot(weights, images_ref[:, q * 512 : q * 512 + 512], preferred_element_type=f32)
        for turn in range(3):
            part = 8 * turn + q
            j, b = part // 3, part % 3
            for lanes in range(4):
                tile = numerator[64 * turn : 64 * turn + 64, 128 * lanes : 128 * lanes + 128]
                pieces_ref[j % 2, :, j // 2, 4 * b + lanes] = tile.reshape(8, K, 128).astype(bf16)


def local_sums(stats, scores, shifted):
    vmem = pl.BlockSpec(memory_space=pltpu.VMEM)
    return pl.pallas_call(
        sum_kernel,
        in_specs=[vmem, vmem, pl.BlockSpec(memory_space=pltpu.HBM)],
        out_specs=[vmem, vmem],
        out_shape=[
            jax.ShapeDtypeStruct((2, 8, 4, TILES + 1, K, 128), bf16),
            jax.ShapeDtypeStruct((1, P_DEV), f32),
        ],
        scratch_shapes=[pltpu.VMEM((P_DEV, F), bf16), pltpu.SemaphoreType.DMA((8,))],
        compiler_params=pltpu.CompilerParams(vmem_limit_bytes=16 << 20),
        name="sums",
    )(stats, scores, shifted)


def scatter_sums(pieces):
    pieces = exchange(pieces, "c").astype(f32)
    pieces = jnp.sum(pieces, axis=0).astype(bf16)
    pieces = pieces.reshape(4, 8, TILES + 1, K, 128)
    pieces = exchange(pieces, "y").astype(f32)
    pieces = jnp.sum(pieces, axis=0).astype(bf16)
    pieces = exchange(pieces, Z).astype(f32)
    pieces = jnp.sum(pieces, axis=0)
    summed = pieces[:TILES].reshape(3, 4, K, 128).transpose(2, 0, 1, 3)
    mass = pieces[TILES, :, 0:3] + pieces[TILES, :, 3:6]
    return summed, mass


def on_device(particles, shift_index, prev_class, prev_rotation, precision, references):
    own, other, shifted = gather_table(references, lambda: shift_particles(particles, shift_index))
    shifted = pltpu.with_memory_space_constraint(shifted, pltpu.HBM)
    scores, stats = local_scores(own, other, shifted, prev_class, prev_rotation, precision)
    stats = exchange(stats, CLS)
    pieces, evidence = local_sums(stats, scores, shifted)
    summed, mass = scatter_sums(pieces)
    refreshed = summed / (mass[:, :, None, None] + 1.0)
    return (refreshed.reshape(K, TILES * 128), evidence.reshape(P_DEV))


def solution(mesh):
    split = Mesh(mesh.devices.reshape(4, 2, 4, 2, 2, 4), DOM + CLS)
    return jax.shard_map(
        on_device,
        mesh=split,
        in_specs=(P(DOM, None), P(DOM), P(DOM), P(DOM), P(DOM), P(CLS, DOM)),
        out_specs=(P(CLS, DOM), P(DOM)),
        check_vma=False,
    )
```

time: 157 us -> 126 us (0.80)
  waiting for transfers between devices: 43.2 us -> 18.7 us
  between operations: 14.3 us -> 0.79 us
  blocking collectives: 48.5 us -> 59.7 us
  Pallas kernels: 3.57 us -> 14.3 us
  matrix products: 8.02 us -> 0 us
  local copies, waits for them, and re-layouts: 10.6 us -> 4.88 us
    all_to_all x3 -> x2, waiting for transfers between devices: 37.5 us -> 16.6 us  [exchange(): return lax.all_to_all(array, axis, 0, 0, tiled=True)]
    all_to_all x3 -> x4, blocking collectives: 48.5 us -> 59.7 us  [exchange(): return lax.all_to_all(array, axis, 0, 0, tiled=True)]
    pallas_call x0 -> x2, Pallas kernels: none -> 9.2 us  [the longest x1 5.33 us: local_scores(): pl.pallas_call(score_kernel, in_specs=[pl.BlockSpec(memory_space=pltpu.SM...]
    dot_general x2 -> x0, matrix products: 8.02 us -> none  [the longest x1 4.28 us: on_device(): lax.dot_general(table, shifted, (((1,), (1,)), ((), ())), preferred_eleme...]
    all_gather x1 -> x0, waiting for transfers between devices: 5.69 us -> none  [gather_table(): both = lax.all_gather(along_y, 'c', axis=0)]
    unnamed x14 -> x8, local copies, waits for them, and re-layouts: 5.36 us -> 2.34 us
    ppermute x0 -> x1, waiting for transfers between devices: none -> 2.09 us  [gather_table(): other = lax.ppermute(along_y, 'c', [(0, 1), (1, 0)])]
    ppermute x0 -> x1, starting transfers between devices: none -> 1.91 us  [gather_table(): other = lax.ppermute(along_y, 'c', [(0, 1), (1, 0)])]
  transfers between devices with their start and end apart: 4 -> 3, of which waited for: 4 -> 3; matrix products, arithmetic and copies ran while one was open for 2% -> 2% of each run, Pallas kernels for 2% -> 4%
where the time goes in v2:
time: 126 us
  blocking collectives  59.7 us (47%)
  starting transfers between devices  22.9 us (18%)
  waiting for transfers between devices  18.7 us (15%)
  Pallas kernels  14.3 us (11%)
  local copies, waits for them, and re-layouts  4.88 us (4%)
  other arithmetic  4.4 us (3%)
    all_to_all x4, blocking collectives, exchange(): return lax.all_to_all(array, axis, 0, 0, tiled=True)  59.7 us
    all_to_all x2, starting transfers between devices, exchange(): return lax.all_to_all(array, axis, 0, 0, tiled=True)  21 us
    all_to_all x2, waiting for transfers between devices, exchange(): return lax.all_to_all(array, axis, 0, 0, tiled=True)  16.6 us
    pallas_call x1, Pallas kernels, local_scores(): pl.pallas_call(score_kernel, in_specs=[pl.BlockSpec(memory_space=pltpu.SM...  5.33 us
    pallas_call x1, Pallas kernels, shift_particles(): pl.pallas_call(shift_kernel, grid=(P_DEV // ROW_BLOCK,), in_specs=[pl.Blo...  5.06 us
    pallas_call x1, Pallas kernels, local_sums(): pl.pallas_call(sum_kernel, in_specs=[vmem, vmem, pl.BlockSpec(memory_spac...  3.86 us
  transfers between devices with their start and end apart: 3, of which 3 were waited for; matrix products, arithmetic and copies ran while one was open for 2% of the time, Pallas kernels for 4%

profile of v2, /device:TPU:32, one launch (start us, length us, event | category | flops | bytes accessed | tf_op | source)
XLA Modules:
  0.0 125.6 jit_solution(11644385994674412710)
XLA Ops:
  0.6 1.4 %broadcast_in_dim.26 = bf16[8,12,8,128]{3,2,1,0:T(8,128)(2,1)} broadcast(bf16[12,8,128]{2,1,0:T(8,128)(2,1)} %bitcast.18), dimensions={1,2,3} | broadcast | bytes 221184 | tf_op jit(solution)/shard_map/broadcast_in_dim | solution.py:84
  2.1 12.6 %all-to-all-start = ((bf16[8,12,8,128]{3,2,1,0:T(8,128)(2,1)}), bf16[8,12,8,128]{3,2,1,0:T(8,128)(2,1)S(1)}, u32[]{:S(2)}, u32[]{:S(2)}) async-start(bf16[8,12,8,128]{3,2,1,0:T(8,128)(2,1)} %broadcast_in_dim.26), calls=%async_computation | async-start | bytes 393216 | tf_op jit(solution)/shard_map/all_to_all | solution.py:79
  14.7 0.8 broadcast_in_dim.33.index_ref
  15.6 0.1 pad.3.clone
  15.6 1.1 fusion.5
  16.7 0.1 reduce-precision_convert_fusion.1
  16.9 0.3 maximum_maximum_fusion.table_ref
  17.1 0.0 copy-start
  17.1 2.3 %copy-done = bf16[576,4096]{1,0:T(8,128)(2,1)S(1)} copy-done((bf16[576,4096]{1,0:T(8,128)(2,1)S(1)}, bf16[576,4096]{1,0:T(8,128)(2,1)}, u32[]{:S(2)}) %copy-start) | copy-done | bytes 4718616
  19.5 5.1 %shift.1.shifted_ref = bf16[576,4096]{1,0:T(8,128)(2,1)} custom-call(s32[576,1]{1,0:T(8,128)S(1)} %broadcast_in_dim.33.index_ref, bf16[128,4096]{1,0:T(8,128)(2,1)S(1)} %maximum_maximum_fusion.table_ref, bf16[576,4096]{1,0:T(8,128)(2,1)S(1)} %copy-done), custom_call_target="tpu_custom_call" | custom-call | tf_op jit(solution)/shard_map/shift/pallas_call | solution.py:63
  24.5 3.8 %all-to-all-done = bf16[8,12,8,128]{3,2,1,0:T(8,128)(2,1)S(1)} async-done(((bf16[8,12,8,128]{3,2,1,0:T(8,128)(2,1)}), bf16[8,12,8,128]{3,2,1,0:T(8,128)(2,1)S(1)}, u32[]{:S(2)}, u32[]{:S(2)}) %all-to-all-start) | async-done | bytes 196640 | tf_op jit(solution)/shard_map/all_to_all | solution.py:79
  28.3 0.1 broadcast_in_dim.29
  28.4 13.8 %all_to_all.30 = bf16[4,8,12,8,128]{4,3,2,1,0:T(8,128)(2,1)S(1)} all-to-all(bf16[4,8,12,8,128]{4,3,2,1,0:T(8,128)(2,1)S(1)} %broadcast_in_dim.29), channel_id=1, replica_groups=mesh['y'=4,'za'=2,'zb'=4,'c'=2,'zh'=2,'x'=4] {'y'}, dimensions={0} | all-to-all | bytes 1572864 | tf_op jit(solution)/shard_map/all_to_all | solution.py:79
  42.2 1.9 %collective-permute-start = (bf16[4,8,12,8,128]{4,3,2,1,0:T(8,128)(2,1)S(1)}, bf16[4,8,12,8,128]{4,3,2,1,0:T(8,128)(2,1)S(1)}, u32[]{:S(2)}, u32[]{:S(2)}) collective-permute-start(bf16[4,8,12,8,128]{4,3,2,1,0:T(8,128)(2,1)S(1)} %all_to_all.30), channel_id=1, source_target_pairs={{0,8},{8,0},{1,9},{9,1},{2,10},{10,2},{3,11},{11,3},{4,12},{12,4},... | collective-permute-start | bytes 2359304 | tf_op jit(solution)/shard_map/ppermute | solution.py:87
  44.1 0.0 copy-done.1
  44.1 0.0 copy-done.2
  44.1 0.0 copy-done.3
  44.2 0.1 pad_add_fusion.place_ref
  44.2 2.1 %collective-permute-done = bf16[4,8,12,8,128]{4,3,2,1,0:T(8,128)(2,1)S(1)} collective-permute-done((bf16[4,8,12,8,128]{4,3,2,1,0:T(8,128)(2,1)S(1)}, bf16[4,8,12,8,128]{4,3,2,1,0:T(8,128)(2,1)S(1)}, u32[]{:S(2)}, u32[]{:S(2)}) %collective-permute-start) | collective-permute-done | bytes 786464 | tf_op jit(solution)/shard_map/ppermute | solution.py:87
  46.3 5.3 %scores.1 = (f32[192,576]{1,0:T(8,128)S(1)}, f32[8,2,576]{2,1,0:T(2,128)S(1)}) custom-call(s32[2]{0:T(128)S(1)} %pad_add_fusion.place_ref, bf16[8,4,12,8,128]{4,3,2,1,0:T(8,128)(2,1)S(1)} %bitcast.13, bf16[8,4,12,8,128]{4,3,2,1,0:T(8,128)(2,1)S(1)} %bitcast.14, bf16[576,4096]{1,0:T(8,128)(2,1)} %shift.1.shifted_ref, ...), custom_call_target="tpu_custom_call" | custom-call | tf_op jit(solution)/shard_map/scores/pallas_call | solution.py:140
  51.7 24.8 %all_to_all.31.stats_ref = f32[8,2,576]{2,1,0:T(2,128)S(1)} all-to-all(f32[8,2,576]{2,1,0:T(2,128)S(1)} %get-tuple-element.10), channel_id=1, replica_groups=mesh['y'=4,'za'=2,'zb'=4,'c'=2,'zh'=2,'x'=4] {'zh','x'}, dimensions={0} | all-to-all | bytes 73728 | tf_op jit(solution)/shard_map/all_to_all | solution.py:79
  76.5 3.9 %sums.1 = (bf16[2,8,4,13,8,128]{5,4,3,2,1,0:T(8,128)(2,1)S(1)}, f32[1,576]{1,0:T(1,128)S(1)}) custom-call(f32[8,2,576]{2,1,0:T(2,128)S(1)} %all_to_all.31.stats_ref, f32[192,576]{1,0:T(8,128)S(1)} %get-tuple-element.11.scores_ref, bf16[576,4096]{1,0:T(8,128)(2,1)} %shift.1.shifted_ref), custom_call_target="tpu_custom_call" | custom-call | tf_op jit(solution)/shard_map/sums/pallas_call | solution.py:189
  80.4 5.1 %all_to_all.32 = bf16[2,8,4,13,8,128]{5,4,3,2,1,0:T(8,128)(2,1)S(1)} all-to-all(bf16[2,8,4,13,8,128]{5,4,3,2,1,0:T(8,128)(2,1)S(1)} %get-tuple-element.12), channel_id=1, replica_groups=mesh['y'=4,'za'=2,'zb'=4,'c'=2,'zh'=2,'x'=4] {'c'}, dimensions={0} | all-to-all | bytes 3407872 | tf_op jit(solution)/shard_map/all_to_all | solution.py:79
  85.5 0.6 reduce_sum.33
  86.1 16.0 %all_to_all.33 = bf16[4,8,13,8,128]{4,3,2,1,0:T(8,128)(2,1)S(1)} all-to-all(bf16[4,8,13,8,128]{4,3,2,1,0:T(8,128)(2,1)S(1)} %bitcast.15), channel_id=1, replica_groups=mesh['y'=4,'za'=2,'zb'=4,'c'=2,'zh'=2,'x'=4] {'y'}, dimensions={0} | all-to-all | bytes 1703936 | tf_op jit(solution)/shard_map/all_to_all | solution.py:79
  102.0 0.8 reduce_sum.34
  102.9 8.4 %all-to-all-start.5 = ((bf16[8,13,8,128]{3,2,1,0:T(8,128)(2,1)}), bf16[8,13,8,128]{3,2,1,0:T(8,128)(2,1)S(1)}, u32[]{:S(2)}, u32[]{:S(2)}) async-start(bf16[8,13,8,128]{3,2,1,0:T(8,128)(2,1)} %reduce_sum.34), calls=%async_computation.5 | async-start | bytes 425984 | tf_op jit(solution)/shard_map/all_to_all | solution.py:79
  111.3 0.6 reduce.2
  111.9 12.8 %all-to-all-done.5 = bf16[8,13,8,128]{3,2,1,0:T(8,128)(2,1)S(1)} async-done(((bf16[8,13,8,128]{3,2,1,0:T(8,128)(2,1)}), bf16[8,13,8,128]{3,2,1,0:T(8,128)(2,1)S(1)}, u32[]{:S(2)}, u32[]{:S(2)}) %all-to-all-start.5) | async-done | bytes 213024 | tf_op jit(solution)/shard_map/all_to_all | solution.py:79
  124.8 0.1 fusion.12
  124.8 0.1 copy.12
  124.9 0.7 broadcast_divide_fusion
  (11 shorter events, 0.1 us)
Async XLA Ops:
  2.1 26.2 %all-to-all-start = ((bf16[8,12,8,128]{3,2,1,0:T(8,128)(2,1)}), bf16[8,12,8,128]{3,2,1,0:T(8,128)(2,1)S(1)}, u32[]{:S(2)}, u32[]{:S(2)}) async-start(bf16[8,12,8,128]{3,2,1,0:T(8,128)(2,1)} %broadcast_in_dim.26), calls=%async_computation | async-start | bytes 393216 | tf_op jit(solution)/shard_map/all_to_all | solution.py:79
  17.1 2.3 %copy-start = (bf16[576,4096]{1,0:T(8,128)(2,1)S(1)}, bf16[576,4096]{1,0:T(8,128)(2,1)}, u32[]{:S(2)}) copy-start(bf16[576,4096]{1,0:T(8,128)(2,1)} %image_ref.1) | copy-start | bytes 14155780
  24.5 19.6 %copy-start.1 = (s32[576]{0:T(1024)S(1)}, s32[576]{0:T(1024)}, u32[]{:S(2)}) copy-start(s32[576]{0:T(1024)} %param.8) | copy-start | bytes 6916
  24.5 19.6 %copy-start.2 = (s32[576]{0:T(1024)S(1)}, s32[576]{0:T(1024)}, u32[]{:S(2)}) copy-start(s32[576]{0:T(1024)} %param.9) | copy-start | bytes 6916
  24.5 19.6 %copy-start.3 = (f32[576]{0:T(1024)S(1)}, f32[576]{0:T(1024)}, u32[]{:S(2)}) copy-start(f32[576]{0:T(1024)} %param.10) | copy-start | bytes 6916
  42.2 4.2 %collective-permute-start = (bf16[4,8,12,8,128]{4,3,2,1,0:T(8,128)(2,1)S(1)}, bf16[4,8,12,8,128]{4,3,2,1,0:T(8,128)(2,1)S(1)}, u32[]{:S(2)}, u32[]{:S(2)}) collective-permute-start(bf16[4,8,12,8,128]{4,3,2,1,0:T(8,128)(2,1)S(1)} %all_to_all.30), channel_id=1, source_target_pairs={{0,8},{8,0},{1,9},{9,1},{2,10},{10,2},{3,11},{11,3},{4,12},{12,4},... | collective-permute-start | bytes 2359304 | tf_op jit(solution)/shard_map/ppermute | solution.py:87
  102.9 21.8 %all-to-all-start.5 = ((bf16[8,13,8,128]{3,2,1,0:T(8,128)(2,1)}), bf16[8,13,8,128]{3,2,1,0:T(8,128)(2,1)S(1)}, u32[]{:S(2)}, u32[]{:S(2)}) async-start(bf16[8,13,8,128]{3,2,1,0:T(8,128)(2,1)} %reduce_sum.34), calls=%async_computation.5 | async-start | bytes 425984 | tf_op jit(solution)/shard_map/all_to_all | solution.py:79

commit v3 on v2

--- a/solution.py
+++ b/solution.py
@@ -59,7 +59,7 @@
         out_ref[:, H + at : H + at + 512] = (imag * cosine - real * sine).astype(bf16)
 
 
-def shift_particles(particles, shift_index):
+def shift_particles(particles, shift_index, table):
     return pl.pallas_call(
         shift_kernel,
         grid=(P_DEV // ROW_BLOCK,),
@@ -72,18 +72,19 @@
         out_shape=pltpu.HBM((P_DEV, F), bf16),
         compiler_params=pltpu.CompilerParams(vmem_limit_bytes=16 << 20),
         name="shift",
-    )(shift_index[:, None], phase_table(), particles)
+    )(shift_index, table, particles)
 
 
 def exchange(array, axis):
     return lax.all_to_all(array, axis, 0, 0, tiled=True)
 
 
-def gather_table(references, shifted_of):
+def gather_table(references, particles, shift_index):
     mine = references.reshape(K, TILES, 128).transpose(1, 0, 2)
     along_z = exchange(jnp.broadcast_to(mine, (8, TILES, K, 128)), Z)
-    along_z, shifted = lax.optimization_barrier((along_z, shifted_of()))
+    along_z, index, phases = lax.optimization_barrier((along_z, shift_index[:, None], phase_table()))
     along_y = exchange(jnp.broadcast_to(along_z, (4, 8, TILES, K, 128)), "y")
+    along_y, shifted = lax.optimization_barrier((along_y, shift_particles(particles, index, phases)))
     other = lax.ppermute(along_y, "c", [(0, 1), (1, 0)])
     return along_y.reshape(8, 4, TILES, K, 128), other.reshape(8, 4, TILES, K, 128), shifted
 
@@ -200,28 +201,40 @@
     )(stats, scores, shifted)
 
 
+def finish_kernel(pieces_ref, out_ref):
+    total = pieces_ref[0].astype(f32)
+    for i in range(1, 8):
+        total = total + pieces_ref[i].astype(f32)
+    mass = total[TILES]
+    for b in range(3):
+        scale = 1.0 / (mass[:, b : b + 1] + mass[:, 3 + b : 4 + b] + 1.0)
+        for lanes in range(4):
+            at = 4 * b + lanes
+            out_ref[:, at * 128 : at * 128 + 128] = total[at] * scale
+
+
 def scatter_sums(pieces):
     pieces = exchange(pieces, "c").astype(f32)
     pieces = jnp.sum(pieces, axis=0).astype(bf16)
     pieces = pieces.reshape(4, 8, TILES + 1, K, 128)
     pieces = exchange(pieces, "y").astype(f32)
     pieces = jnp.sum(pieces, axis=0).astype(bf16)
-    pieces = exchange(pieces, Z).astype(f32)
-    pieces = jnp.sum(pieces, axis=0)
-    summed = pieces[:TILES].reshape(3, 4, K, 128).transpose(2, 0, 1, 3)
-    mass = pieces[TILES, :, 0:3] + pieces[TILES, :, 3:6]
-    return summed, mass
+    pieces = exchange(pieces, Z)
+    return pl.pallas_call(
+        finish_kernel,
+        out_shape=jax.ShapeDtypeStruct((K, TILES * 128), f32),
+        compiler_params=pltpu.CompilerParams(vmem_limit_bytes=16 << 20),
+        name="finish",
+    )(pieces.reshape(8, TILES + 1, K, 128))
 
 
 def on_device(particles, shift_index, prev_class, prev_rotation, precision, references):
-    own, other, shifted = gather_table(references, lambda: shift_particles(particles, shift_index))
+    own, other, shifted = gather_table(references, particles, shift_index)
     shifted = pltpu.with_memory_space_constraint(shifted, pltpu.HBM)
     scores, stats = local_scores(own, other, shifted, prev_class, prev_rotation, precision)
     stats = exchange(stats, CLS)
     pieces, evidence = local_sums(stats, scores, shifted)
-    summed, mass = scatter_sums(pieces)
-    refreshed = summed / (mass[:, :, None, None] + 1.0)
-    return (refreshed.reshape(K, TILES * 128), evidence.reshape(P_DEV))
+    return (scatter_sums(pieces), evidence.reshape(P_DEV))
 
 
 def solution(mesh):

time: 126 us -> 127 us (level)
  blocking collectives: 59.7 us -> 46.1 us
  waiting for transfers between devices: 18.7 us -> 28.2 us
  starting transfers between devices: 22.9 us -> 27 us
    all_to_all x4 -> x3, blocking collectives: 59.7 us -> 46.1 us  [exchange(): return lax.all_to_all(array, axis, 0, 0, tiled=True)]
    all_to_all x2 -> x3, waiting for transfers between devices: 16.6 us -> 26.1 us  [exchange(): return lax.all_to_all(array, axis, 0, 0, tiled=True)]
    all_to_all x2 -> x3, starting transfers between devices: 21 us -> 25.1 us  [exchange(): return lax.all_to_all(array, axis, 0, 0, tiled=True)]
  transfers between devices with their start and end apart: 3 -> 4, of which waited for: 3 -> 4; matrix products, arithmetic and copies ran while one was open for 2% -> 2% of each run, Pallas kernels for 4% -> 4%
where the time goes in v3:
time: 127 us; the launch traced here: 126 us
  blocking collectives  46.1 us (36%)
  waiting for transfers between devices  28.2 us (22%)
  starting transfers between devices  27 us (21%)
  Pallas kernels  15 us (12%)
  local copies, waits for them, and re-layouts  5.76 us (5%)
  other arithmetic  3.6 us (3%)
    all_to_all x3, blocking collectives, exchange(): return lax.all_to_all(array, axis, 0, 0, tiled=True)  46.1 us
    all_to_all x3, waiting for transfers between devices, exchange(): return lax.all_to_all(array, axis, 0, 0, tiled=True)  26.1 us
    all_to_all x3, starting transfers between devices, exchange(): return lax.all_to_all(array, axis, 0, 0, tiled=True)  25.1 us
    pallas_call x1, Pallas kernels, local_scores(): pl.pallas_call(score_kernel, in_specs=[pl.BlockSpec(memory_space=pltpu.SM...  5.34 us
    pallas_call x1, Pallas kernels, shift_particles(): pl.pallas_call(shift_kernel, grid=(P_DEV // ROW_BLOCK,), in_specs=[pl.Blo...  5.03 us
    pallas_call x1, Pallas kernels, local_sums(): pl.pallas_call(sum_kernel, in_specs=[vmem, vmem, pl.BlockSpec(memory_spac...  3.86 us
  transfers between devices with their start and end apart: 4, of which 4 were waited for; matrix products, arithmetic and copies ran while one was open for 2% of the time, Pallas kernels for 4%

profile of v3, /device:TPU:32, one launch (start us, length us, event | category | flops | bytes accessed | tf_op | source)
XLA Modules:
  0.0 126.4 jit_solution(5155719096593567810)
XLA Ops:
  0.6 1.4 %broadcast_in_dim.25 = bf16[8,12,8,128]{3,2,1,0:T(8,128)(2,1)} broadcast(bf16[12,8,128]{2,1,0:T(8,128)(2,1)} %bitcast.11), dimensions={1,2,3} | broadcast | bytes 221184 | tf_op jit(solution)/shard_map/broadcast_in_dim | solution.py:84
  2.1 12.6 %all-to-all-start = ((bf16[8,12,8,128]{3,2,1,0:T(8,128)(2,1)}), bf16[8,12,8,128]{3,2,1,0:T(8,128)(2,1)S(1)}, u32[]{:S(2)}, u32[]{:S(2)}) async-start(bf16[8,12,8,128]{3,2,1,0:T(8,128)(2,1)} %broadcast_in_dim.25), calls=%async_computation | async-start | bytes 393216 | tf_op jit(solution)/shard_map/all_to_all | solution.py:79
  14.7 0.7 broadcast_in_dim.26
  15.4 0.1 pad.3.clone
  15.5 1.1 fusion.5
  16.6 0.1 reduce-precision_convert_fusion.1
  16.7 0.3 maximum_maximum_fusion.table_ref
  17.0 11.3 %all-to-all-done = bf16[8,12,8,128]{3,2,1,0:T(8,128)(2,1)S(1)} async-done(((bf16[8,12,8,128]{3,2,1,0:T(8,128)(2,1)}), bf16[8,12,8,128]{3,2,1,0:T(8,128)(2,1)S(1)}, u32[]{:S(2)}, u32[]{:S(2)}) %all-to-all-start) | async-done | bytes 196640 | tf_op jit(solution)/shard_map/all_to_all | solution.py:79
  28.3 1.0 broadcast_in_dim.28
  29.3 4.5 %all-to-all-start.1 = ((bf16[4,8,12,8,128]{4,3,2,1,0:T(8,128)(2,1)}), bf16[4,8,12,8,128]{4,3,2,1,0:T(8,128)(2,1)S(1)}, u32[]{:S(2)}, u32[]{:S(2)}) async-start(bf16[4,8,12,8,128]{4,3,2,1,0:T(8,128)(2,1)} %broadcast_in_dim.28), calls=%async_computation.1 | async-start | bytes 1572864 | tf_op jit(solution)/shard_map/all_to_all | solution.py:79
  33.8 0.2 copy.9.index_ref
  34.0 0.0 copy-start
  34.0 2.3 %copy-done = bf16[576,4096]{1,0:T(8,128)(2,1)S(1)} copy-done((bf16[576,4096]{1,0:T(8,128)(2,1)S(1)}, bf16[576,4096]{1,0:T(8,128)(2,1)}, u32[]{:S(2)}) %copy-start) | copy-done | bytes 4718616
  36.3 5.0 %shift.1.shifted_ref = bf16[576,4096]{1,0:T(8,128)(2,1)} custom-call(s32[576,1]{1,0:T(8,128)S(1)} %copy.9.index_ref, bf16[128,4096]{1,0:T(8,128)(2,1)S(1)} %maximum_maximum_fusion.table_ref, bf16[576,4096]{1,0:T(8,128)(2,1)S(1)} %copy-done), custom_call_target="tpu_custom_call" | custom-call | tf_op jit(solution)/shard_map/shift/pallas_call | solution.py:63
  41.3 2.0 %all-to-all-done.1 = bf16[4,8,12,8,128]{4,3,2,1,0:T(8,128)(2,1)S(1)} async-done(((bf16[4,8,12,8,128]{4,3,2,1,0:T(8,128)(2,1)}), bf16[4,8,12,8,128]{4,3,2,1,0:T(8,128)(2,1)S(1)}, u32[]{:S(2)}, u32[]{:S(2)}) %all-to-all-start.1) | async-done | bytes 786464 | tf_op jit(solution)/shard_map/all_to_all | solution.py:79
  43.3 1.9 %collective-permute-start = (bf16[4,8,12,8,128]{4,3,2,1,0:T(8,128)(2,1)S(1)}, bf16[4,8,12,8,128]{4,3,2,1,0:T(8,128)(2,1)S(1)}, u32[]{:S(2)}, u32[]{:S(2)}) collective-permute-start(bf16[4,8,12,8,128]{4,3,2,1,0:T(8,128)(2,1)S(1)} %all-to-all-done.1), channel_id=1, source_target_pairs={{0,8},{8,0},{1,9},{9,1},{2,10},{10,2},{3,11},{11,3},{4,12},{12,4},... | collective-permute-start | bytes 2359304 | tf_op jit(solution)/shard_map/ppermute | solution.py:88
  45.2 0.0 copy-done.1
  45.2 0.0 copy-done.2
  45.3 0.0 copy-done.3
  45.3 0.1 pad_add_fusion.place_ref
  45.4 2.1 %collective-permute-done = bf16[4,8,12,8,128]{4,3,2,1,0:T(8,128)(2,1)S(1)} collective-permute-done((bf16[4,8,12,8,128]{4,3,2,1,0:T(8,128)(2,1)S(1)}, bf16[4,8,12,8,128]{4,3,2,1,0:T(8,128)(2,1)S(1)}, u32[]{:S(2)}, u32[]{:S(2)}) %collective-permute-start) | collective-permute-done | bytes 786464 | tf_op jit(solution)/shard_map/ppermute | solution.py:88
  47.5 5.3 %scores.1 = (f32[192,576]{1,0:T(8,128)S(1)}, f32[8,2,576]{2,1,0:T(2,128)S(1)}) custom-call(s32[2]{0:T(128)S(1)} %pad_add_fusion.place_ref, bf16[8,4,12,8,128]{4,3,2,1,0:T(8,128)(2,1)S(1)} %bitcast.8, bf16[8,4,12,8,128]{4,3,2,1,0:T(8,128)(2,1)S(1)} %bitcast.9, bf16[576,4096]{1,0:T(8,128)(2,1)} %shift.1.shifted_ref, s32[1,576]{1,0:T(1,128)S(1)} %broadcast_in_dim.29.class_ref, ...), custom_call_target="tpu_custom_call" | custom-call | tf_op jit(solution)/shard_map/scores/pallas_call | solution.py:141
  52.8 25.1 %all_to_all.30.stats_ref = f32[8,2,576]{2,1,0:T(2,128)S(1)} all-to-all(f32[8,2,576]{2,1,0:T(2,128)S(1)} %get-tuple-element.16), channel_id=1, replica_groups=mesh['y'=4,'za'=2,'zb'=4,'c'=2,'zh'=2,'x'=4] {'zh','x'}, dimensions={0} | all-to-all | bytes 73728 | tf_op jit(solution)/shard_map/all_to_all | solution.py:79
  77.9 3.9 %sums.1 = (bf16[2,8,4,13,8,128]{5,4,3,2,1,0:T(8,128)(2,1)S(1)}, f32[1,576]{1,0:T(1,128)S(1)}) custom-call(f32[8,2,576]{2,1,0:T(2,128)S(1)} %all_to_all.30.stats_ref, f32[192,576]{1,0:T(8,128)S(1)} %get-tuple-element.17.scores_ref, bf16[576,4096]{1,0:T(8,128)(2,1)} %shift.1.shifted_ref), custom_call_target="tpu_custom_call" | custom-call | tf_op jit(solution)/shard_map/sums/pallas_call | solution.py:190
  81.7 5.1 %all_to_all.31 = bf16[2,8,4,13,8,128]{5,4,3,2,1,0:T(8,128)(2,1)S(1)} all-to-all(bf16[2,8,4,13,8,128]{5,4,3,2,1,0:T(8,128)(2,1)S(1)} %get-tuple-element.18), channel_id=1, replica_groups=mesh['y'=4,'za'=2,'zb'=4,'c'=2,'zh'=2,'x'=4] {'c'}, dimensions={0} | all-to-all | bytes 3407872 | tf_op jit(solution)/shard_map/all_to_all | solution.py:79
  86.8 0.6 reduce_sum.24
  87.4 16.0 %all_to_all.32 = bf16[4,8,13,8,128]{4,3,2,1,0:T(8,128)(2,1)S(1)} all-to-all(bf16[4,8,13,8,128]{4,3,2,1,0:T(8,128)(2,1)S(1)} %bitcast.10), channel_id=1, replica_groups=mesh['y'=4,'za'=2,'zb'=4,'c'=2,'zh'=2,'x'=4] {'y'}, dimensions={0} | all-to-all | bytes 1703936 | tf_op jit(solution)/shard_map/all_to_all | solution.py:79
  103.4 0.8 reduce_sum.25
  104.2 8.0 %all-to-all-start.5 = ((bf16[8,13,8,128]{3,2,1,0:T(8,128)(2,1)}), bf16[8,13,8,128]{3,2,1,0:T(8,128)(2,1)S(1)}, u32[]{:S(2)}, u32[]{:S(2)}) async-start(bf16[8,13,8,128]{3,2,1,0:T(8,128)(2,1)} %reduce_sum.25), calls=%async_computation.5 | async-start | bytes 425984 | tf_op jit(solution)/shard_map/all_to_all | solution.py:79
  112.2 0.6 reduce.2
  112.8 12.8 %all-to-all-done.5.pieces_ref = bf16[8,13,8,128]{3,2,1,0:T(8,128)(2,1)S(1)} async-done(((bf16[8,13,8,128]{3,2,1,0:T(8,128)(2,1)}), bf16[8,13,8,128]{3,2,1,0:T(8,128)(2,1)S(1)}, u32[]{:S(2)}, u32[]{:S(2)}) %all-to-all-start.5) | async-done | bytes 213024 | tf_op jit(solution)/shard_map/all_to_all | solution.py:79
  125.6 0.8 finish.1
  (9 shorter events, 0.0 us)
Async XLA Ops:
  2.1 26.2 %all-to-all-start = ((bf16[8,12,8,128]{3,2,1,0:T(8,128)(2,1)}), bf16[8,12,8,128]{3,2,1,0:T(8,128)(2,1)S(1)}, u32[]{:S(2)}, u32[]{:S(2)}) async-start(bf16[8,12,8,128]{3,2,1,0:T(8,128)(2,1)} %broadcast_in_dim.25), calls=%async_computation | async-start | bytes 393216 | tf_op jit(solution)/shard_map/all_to_all | solution.py:79
  29.3 14.0 %all-to-all-start.1 = ((bf16[4,8,12,8,128]{4,3,2,1,0:T(8,128)(2,1)}), bf16[4,8,12,8,128]{4,3,2,1,0:T(8,128)(2,1)S(1)}, u32[]{:S(2)}, u32[]{:S(2)}) async-start(bf16[4,8,12,8,128]{4,3,2,1,0:T(8,128)(2,1)} %broadcast_in_dim.28), calls=%async_computation.1 | async-start | bytes 1572864 | tf_op jit(solution)/shard_map/all_to_all | solution.py:79
  34.0 2.3 %copy-start = (bf16[576,4096]{1,0:T(8,128)(2,1)S(1)}, bf16[576,4096]{1,0:T(8,128)(2,1)}, u32[]{:S(2)}) copy-start(bf16[576,4096]{1,0:T(8,128)(2,1)} %image_ref.1) | copy-start | bytes 14155780
  36.3 8.9 %copy-start.1 = (s32[576]{0:T(1024)S(1)}, s32[576]{0:T(1024)}, u32[]{:S(2)}) copy-start(s32[576]{0:T(1024)} %param.8) | copy-start | bytes 6916
  36.3 8.9 %copy-start.2 = (s32[576]{0:T(1024)S(1)}, s32[576]{0:T(1024)}, u32[]{:S(2)}) copy-start(s32[576]{0:T(1024)} %param.9) | copy-start | bytes 6916
  36.3 8.9 %copy-start.3 = (f32[576]{0:T(1024)S(1)}, f32[576]{0:T(1024)}, u32[]{:S(2)}) copy-start(f32[576]{0:T(1024)} %param.10) | copy-start | bytes 6916
  43.3 4.2 %collective-permute-start = (bf16[4,8,12,8,128]{4,3,2,1,0:T(8,128)(2,1)S(1)}, bf16[4,8,12,8,128]{4,3,2,1,0:T(8,128)(2,1)S(1)}, u32[]{:S(2)}, u32[]{:S(2)}) collective-permute-start(bf16[4,8,12,8,128]{4,3,2,1,0:T(8,128)(2,1)S(1)} %all-to-all-done.1), channel_id=1, source_target_pairs={{0,8},{8,0},{1,9},{9,1},{2,10},{10,2},{3,11},{11,3},{4,12},{12,4},... | collective-permute-start | bytes 2359304 | tf_op jit(solution)/shard_map/ppermute | solution.py:88
  104.2 21.4 %all-to-all-start.5 = ((bf16[8,13,8,128]{3,2,1,0:T(8,128)(2,1)}), bf16[8,13,8,128]{3,2,1,0:T(8,128)(2,1)S(1)}, u32[]{:S(2)}, u32[]{:S(2)}) async-start(bf16[8,13,8,128]{3,2,1,0:T(8,128)(2,1)} %reduce_sum.25), calls=%async_computation.5 | async-start | bytes 425984 | tf_op jit(solution)/shard_map/all_to_all | solution.py:79

commit v4 on v3

--- a/solution.py
+++ b/solution.py
@@ -89,36 +89,50 @@
     return along_y.reshape(8, 4, TILES, K, 128), other.reshape(8, 4, TILES, K, 128), shifted
 
 
-def column_copies(source_ref, target_ref, arrived):
+def fill_table(source_ref, table_ref, core):
+    for zb in range(4):
+        for b in range(3):
+            part = 6 * zb + 3 * core + b
+            turn = part // 8
+            column = (part - 8 * turn) * 512
+            rows = pl.ds(pl.multiple_of(turn * 64, 64), 64)
+            for lanes in range(4):
+                tiles = source_ref[:, zb, 4 * b + lanes].reshape(64, 128)
+                table_ref[rows, pl.ds(pl.multiple_of(column + lanes * 128, 128), 128)] = tiles
+
+
+def load_kernel(place_ref, own_ref, shifted_ref, images_ref, table_ref, arrived):
     copies = []
     for q in range(8):
         columns = pl.ds(q * 512, 512)
-        copies.append(pltpu.make_async_copy(source_ref.at[:, columns], target_ref.at[:, columns], arrived.at[q]))
+        copies.append(pltpu.make_async_copy(shifted_ref.at[:, columns], images_ref.at[:, columns], arrived.at[q]))
         copies[-1].start()
-    return copies
-
-
-def score_kernel(place_ref, own_ref, other_ref, shifted_ref, class_ref, rotation_ref, precision_ref, scores_ref, stats_ref, table_ref, images_ref, arrived):
-    copies = column_copies(shifted_ref, images_ref, arrived)
-    core = place_ref[0]
-    for source, at in ((own_ref, core), (other_ref, 1 - core)):
-        for zb in range(4):
-            for b in range(3):
-                part = 6 * zb + 3 * at + b
-                turn = part // 8
-                column = (part - 8 * turn) * 512
-                rows = pl.ds(pl.multiple_of(turn * 64, 64), 64)
-                for lanes in range(4):
-                    tiles = source[:, zb, 4 * b + lanes].reshape(64, 128)
-                    table_ref[rows, pl.ds(pl.multiple_of(column + lanes * 128, 128), 128)] = tiles
+    fill_table(own_ref, table_ref, place_ref[0])
+    for copy in copies:
+        copy.wait()
+
+
+def load_own(place, own, shifted):
+    vmem = pl.BlockSpec(memory_space=pltpu.VMEM)
+    return pl.pallas_call(
+        load_kernel,
+        in_specs=[pl.BlockSpec(memory_space=pltpu.SMEM), vmem, pl.BlockSpec(memory_space=pltpu.HBM)],
+        out_specs=[vmem, vmem],
+        out_shape=[pltpu.VMEM((P_DEV, F), bf16), pltpu.VMEM((ROWS, F), bf16)],
+        scratch_shapes=[pltpu.SemaphoreType.DMA((8,))],
+        compiler_params=pltpu.CompilerParams(vmem_limit_bytes=16 << 20),
+        name="load",
+    )(place, own, pltpu.with_memory_space_constraint(shifted, pltpu.HBM))
+
+
+def score_kernel(place_ref, other_ref, half_ref, shifted_ref, class_ref, rotation_ref, precision_ref, scores_ref, stats_ref, table_ref):
+    fill_table(other_ref, table_ref, 1 - place_ref[0])
     half_norm = jnp.zeros((ROWS, 128), f32)
     for at in range(0, F, 128):
         piece = table_ref[:, at : at + 128].astype(f32)
         half_norm = half_norm + piece * piece
     half_norm = 0.5 * jnp.sum(half_norm, axis=1, keepdims=True)
-    for copy in copies:
-        copy.wait()
-    correlation = lax.dot_general(table_ref[...], images_ref[...], (((1,), (1,)), ((), ())), preferred_element_type=f32)
+    correlation = lax.dot_general(table_ref[...], shifted_ref[...], (((1,), (1,)), ((), ())), preferred_element_type=f32)
     row = lax.broadcasted_iota(jnp.int32, (ROWS, 1), 0)
     class_ids = place_ref[1] + row % K
     rotation_ids = (row // K) % 8 * 3 + row // 64
@@ -137,20 +151,21 @@
 
 def local_scores(own, other, shifted, prev_class, prev_rotation, precision):
     place = jnp.stack([lax.axis_index("c"), lax.axis_index(CLS) * K]).astype(jnp.int32)
+    images, half = load_own(place, own, shifted)
     vmem = pl.BlockSpec(memory_space=pltpu.VMEM)
-    return pl.pallas_call(
+    scores, stats, _ = pl.pallas_call(
         score_kernel,
-        in_specs=[pl.BlockSpec(memory_space=pltpu.SMEM), vmem, vmem, pl.BlockSpec(memory_space=pltpu.HBM)] + [vmem] * 3,
-        out_specs=[vmem, vmem],
-        out_shape=[jax.ShapeDtypeStruct((ROWS, P_DEV), f32), jax.ShapeDtypeStruct((8, 2, P_DEV), f32)],
-        scratch_shapes=[pltpu.VMEM((ROWS, F), bf16), pltpu.VMEM((P_DEV, F), bf16), pltpu.SemaphoreType.DMA((8,))],
+        in_specs=[pl.BlockSpec(memory_space=pltpu.SMEM)] + [vmem] * 6,
+        out_specs=[vmem, vmem, vmem],
+        out_shape=[jax.ShapeDtypeStruct((ROWS, P_DEV), f32), jax.ShapeDtypeStruct((8, 2, P_DEV), f32), pltpu.VMEM((ROWS, F), bf16)],
+        input_output_aliases={2: 2},
         compiler_params=pltpu.CompilerParams(vmem_limit_bytes=16 << 20),
         name="scores",
-    )(place, own, other, shifted, prev_class[None, :], prev_rotation[None, :], precision[None, :])
-
-
-def sum_kernel(stats_ref, scores_ref, shifted_ref, pieces_ref, evidence_ref, images_ref, arrived):
-    copies = column_copies(shifted_ref, images_ref, arrived)
+    )(place, other, half, images, prev_class[None, :], prev_rotation[None, :], precision[None, :])
+    return scores, stats, images
+
+
+def sum_kernel(stats_ref, scores_ref, shifted_ref, pieces_ref, evidence_ref):
     tops = [stats_ref[i, 0:1, :] for i in range(8)]
     top = tops[0]
     for i in range(1, 8):
@@ -175,8 +190,7 @@
             tile = jnp.where(lane == 3 + b, low[turn], tile)
         pieces_ref[j % 2, :, j // 2, TILES] = tile.astype(bf16)
     for q in range(8):
-        copies[q].wait()
-        numerator = jnp.dot(weights, images_ref[:, q * 512 : q * 512 + 512], preferred_element_type=f32)
+        numerator = jnp.dot(weights, shifted_ref[:, q * 512 : q * 512 + 512], preferred_element_type=f32)
         for turn in range(3):
             part = 8 * turn + q
             j, b = part // 3, part % 3
@@ -189,13 +203,12 @@
     vmem = pl.BlockSpec(memory_space=pltpu.VMEM)
     return pl.pallas_call(
         sum_kernel,
-        in_specs=[vmem, vmem, pl.BlockSpec(memory_space=pltpu.HBM)],
+        in_specs=[vmem, vmem, vmem],
         out_specs=[vmem, vmem],
         out_shape=[
             jax.ShapeDtypeStruct((2, 8, 4, TILES + 1, K, 128), bf16),
             jax.ShapeDtypeStruct((1, P_DEV), f32),
         ],
-        scratch_shapes=[pltpu.VMEM((P_DEV, F), bf16), pltpu.SemaphoreType.DMA((8,))],
         compiler_params=pltpu.CompilerParams(vmem_limit_bytes=16 << 20),
         name="sums",
     )(stats, scores, shifted)
@@ -230,10 +243,9 @@
 
 def on_device(particles, shift_index, prev_class, prev_rotation, precision, references):
     own, other, shifted = gather_table(references, particles, shift_index)
-    shifted = pltpu.with_memory_space_constraint(shifted, pltpu.HBM)
-    scores, stats = local_scores(own, other, shifted, prev_class, prev_rotation, precision)
+    scores, stats, images = local_scores(own, other, shifted, prev_class, prev_rotation, precision)
     stats = exchange(stats, CLS)
-    pieces, evidence = local_sums(stats, scores, shifted)
+    pieces, evidence = local_sums(stats, scores, images)
     return (scatter_sums(pieces), evidence.reshape(P_DEV))
 
 

time: 127 us -> 123 us (0.969)
  waiting for transfers between devices: 28.2 us -> 26.1 us
  Pallas kernels: 15 us -> 13.3 us
    pallas_call x1, Pallas kernels: 5.34 us -> 2.95 us  [local_scores(): pl.pallas_call(score_kernel, in_specs=[pl.BlockSpec(memory_space=pltpu.SM...]
    ppermute x1, waiting for transfers between devices: 2.09 us -> 0.01 us  [gather_table(): other = lax.ppermute(along_y, 'c', [(0, 1), (1, 0)])]
    pallas_call x1 -> x2, Pallas kernels: 3.86 us -> 4.54 us  [the longest x1 3.12 us: load_own(): pl.pallas_call(load_kernel, in_specs=[pl.BlockSpec(memory_space=pltpu.SME...]
  transfers between devices with their start and end apart: 4 -> 4, of which waited for: 4 -> 3; matrix products, arithmetic and copies ran while one was open for 2% -> 3% of each run, Pallas kernels for 4% -> 7%
where the time goes in v4:
time: 123 us
  blocking collectives  46.1 us (37%)
  starting transfers between devices  27 us (22%)
  waiting for transfers between devices  26.1 us (21%)
  Pallas kernels  13.3 us (11%)
  local copies, waits for them, and re-layouts  5.75 us (5%)
  other arithmetic  3.6 us (3%)
    all_to_all x3, blocking collectives, exchange(): return lax.all_to_all(array, axis, 0, 0, tiled=True)  46.1 us
    all_to_all x3, waiting for transfers between devices, exchange(): return lax.all_to_all(array, axis, 0, 0, tiled=True)  26.1 us
    all_to_all x3, starting transfers between devices, exchange(): return lax.all_to_all(array, axis, 0, 0, tiled=True)  25.1 us
    pallas_call x1, Pallas kernels, shift_particles(): pl.pallas_call(shift_kernel, grid=(P_DEV // ROW_BLOCK,), in_specs=[pl.Blo...  5.02 us
    pallas_call x1, Pallas kernels, load_own(): pl.pallas_call(load_kernel, in_specs=[pl.BlockSpec(memory_space=pltpu.SME...  3.12 us
    pallas_call x1, Pallas kernels, local_scores(): pl.pallas_call(score_kernel, in_specs=[pl.BlockSpec(memory_space=pltpu.SM...  2.95 us
  transfers between devices with their start and end apart: 4, of which 3 were waited for; matrix products, arithmetic and copies ran while one was open for 3% of the time, Pallas kernels for 7%

profile of v4, /device:TPU:32, one launch (start us, length us, event | category | flops | bytes accessed | tf_op | source)
XLA Modules:
  0.0 122.6 jit_solution(5576869907979149159)
XLA Ops:
  0.6 1.4 %broadcast_in_dim.25 = bf16[8,12,8,128]{3,2,1,0:T(8,128)(2,1)} broadcast(bf16[12,8,128]{2,1,0:T(8,128)(2,1)} %bitcast.11), dimensions={1,2,3} | broadcast | bytes 221184 | tf_op jit(solution)/shard_map/broadcast_in_dim | solution.py:84
  2.1 12.6 %all-to-all-start = ((bf16[8,12,8,128]{3,2,1,0:T(8,128)(2,1)}), bf16[8,12,8,128]{3,2,1,0:T(8,128)(2,1)S(1)}, u32[]{:S(2)}, u32[]{:S(2)}) async-start(bf16[8,12,8,128]{3,2,1,0:T(8,128)(2,1)} %broadcast_in_dim.25), calls=%async_computation | async-start | bytes 393216 | tf_op jit(solution)/shard_map/all_to_all | solution.py:79
  14.7 0.7 broadcast_in_dim.26
  15.4 1.1 fusion.5
  16.5 0.1 reduce-precision_convert_fusion.1
  16.6 0.1 pad.3.clone
  16.7 0.3 maximum_maximum_fusion.table_ref
  17.0 11.3 %all-to-all-done = bf16[8,12,8,128]{3,2,1,0:T(8,128)(2,1)S(1)} async-done(((bf16[8,12,8,128]{3,2,1,0:T(8,128)(2,1)}), bf16[8,12,8,128]{3,2,1,0:T(8,128)(2,1)S(1)}, u32[]{:S(2)}, u32[]{:S(2)}) %all-to-all-start) | async-done | bytes 196640 | tf_op jit(solution)/shard_map/all_to_all | solution.py:79
  28.3 1.0 broadcast_in_dim.28
  29.3 4.5 %all-to-all-start.1 = ((bf16[4,8,12,8,128]{4,3,2,1,0:T(8,128)(2,1)}), bf16[4,8,12,8,128]{4,3,2,1,0:T(8,128)(2,1)S(1)}, u32[]{:S(2)}, u32[]{:S(2)}) async-start(bf16[4,8,12,8,128]{4,3,2,1,0:T(8,128)(2,1)} %broadcast_in_dim.28), calls=%async_computation.1 | async-start | bytes 1572864 | tf_op jit(solution)/shard_map/all_to_all | solution.py:79
  33.8 0.2 copy.10.index_ref
  34.0 0.0 copy-start
  34.0 2.3 %copy-done = bf16[576,4096]{1,0:T(8,128)(2,1)S(1)} copy-done((bf16[576,4096]{1,0:T(8,128)(2,1)S(1)}, bf16[576,4096]{1,0:T(8,128)(2,1)}, u32[]{:S(2)}) %copy-start) | copy-done | bytes 4718616
  36.3 5.0 %shift.1.shifted_ref = bf16[576,4096]{1,0:T(8,128)(2,1)} custom-call(s32[576,1]{1,0:T(8,128)S(1)} %copy.10.index_ref, bf16[128,4096]{1,0:T(8,128)(2,1)S(1)} %maximum_maximum_fusion.table_ref, bf16[576,4096]{1,0:T(8,128)(2,1)S(1)} %copy-done), custom_call_target="tpu_custom_call" | custom-call | tf_op jit(solution)/shard_map/shift/pallas_call | solution.py:63
  41.3 2.0 %all-to-all-done.1 = bf16[4,8,12,8,128]{4,3,2,1,0:T(8,128)(2,1)S(1)} async-done(((bf16[4,8,12,8,128]{4,3,2,1,0:T(8,128)(2,1)}), bf16[4,8,12,8,128]{4,3,2,1,0:T(8,128)(2,1)S(1)}, u32[]{:S(2)}, u32[]{:S(2)}) %all-to-all-start.1) | async-done | bytes 786464 | tf_op jit(solution)/shard_map/all_to_all | solution.py:79
  43.3 1.9 %collective-permute-start = (bf16[4,8,12,8,128]{4,3,2,1,0:T(8,128)(2,1)S(1)}, bf16[4,8,12,8,128]{4,3,2,1,0:T(8,128)(2,1)S(1)}, u32[]{:S(2)}, u32[]{:S(2)}) collective-permute-start(bf16[4,8,12,8,128]{4,3,2,1,0:T(8,128)(2,1)S(1)} %all-to-all-done.1), channel_id=1, source_target_pairs={{0,8},{8,0},{1,9},{9,1},{2,10},{10,2},{3,11},{11,3},{4,12},{12,4},... | collective-permute-start | bytes 2359304 | tf_op jit(solution)/shard_map/ppermute | solution.py:88
  45.2 0.0 copy-done.1
  45.2 0.0 copy-done.2
  45.3 0.1 pad_add_fusion.place_ref
  45.4 3.1 %load.1 = (bf16[576,4096]{1,0:T(8,128)(2,1)S(1)}, bf16[192,4096]{1,0:T(8,128)(2,1)S(1)}) custom-call(s32[2]{0:T(128)S(1)} %pad_add_fusion.place_ref, bf16[8,4,12,8,128]{4,3,2,1,0:T(8,128)(2,1)S(1)} %bitcast.8, bf16[576,4096]{1,0:T(8,128)(2,1)} %shift.1.shifted_ref), custom_call_target="tpu_custom_call" | custom-call | tf_op jit(solution)/shard_map/load/pallas_call | solution.py:117
  48.5 0.0 collective-permute-done
  48.5 2.9 %scores.1 = (f32[192,576]{1,0:T(8,128)S(1)}, f32[8,2,576]{2,1,0:T(2,128)S(1)}, bf16[192,4096]{1,0:T(8,128)(2,1)S(1)}) custom-call(s32[2]{0:T(128)S(1)} %pad_add_fusion.place_ref, bf16[8,4,12,8,128]{4,3,2,1,0:T(8,128)(2,1)S(1)} %bitcast.9, bf16[192,4096]{1,0:T(8,128)(2,1)S(1)} %get-tuple-element.18.half_ref, ...), custom_call_target="tpu_custom_call", output_to_operand_aliasing={{2}: (2, {})} | custom-call | tf_op jit(solution)/shard_map/scores/pallas_call | solution.py:156
  51.4 24.8 %all_to_all.30.stats_ref = f32[8,2,576]{2,1,0:T(2,128)S(1)} all-to-all(f32[8,2,576]{2,1,0:T(2,128)S(1)} %get-tuple-element.20), channel_id=1, replica_groups=mesh['y'=4,'za'=2,'zb'=4,'c'=2,'zh'=2,'x'=4] {'zh','x'}, dimensions={0} | all-to-all | bytes 73728 | tf_op jit(solution)/shard_map/all_to_all | solution.py:79
  76.3 1.4 %sums.1 = (bf16[2,8,4,13,8,128]{5,4,3,2,1,0:T(8,128)(2,1)S(1)}, f32[1,576]{1,0:T(1,128)S(1)}) custom-call(f32[8,2,576]{2,1,0:T(2,128)S(1)} %all_to_all.30.stats_ref, f32[192,576]{1,0:T(8,128)S(1)} %get-tuple-element.21.scores_ref, bf16[576,4096]{1,0:T(8,128)(2,1)S(1)} %get-tuple-element.19.shifted_ref), custom_call_target="tpu_custom_call" | custom-call | tf_op jit(solution)/shard_map/sums/pallas_call | solution.py:204
  77.7 5.1 %all_to_all.31 = bf16[2,8,4,13,8,128]{5,4,3,2,1,0:T(8,128)(2,1)S(1)} all-to-all(bf16[2,8,4,13,8,128]{5,4,3,2,1,0:T(8,128)(2,1)S(1)} %get-tuple-element.22), channel_id=1, replica_groups=mesh['y'=4,'za'=2,'zb'=4,'c'=2,'zh'=2,'x'=4] {'c'}, dimensions={0} | all-to-all | bytes 3407872 | tf_op jit(solution)/shard_map/all_to_all | solution.py:79
  82.8 0.6 reduce_sum.24
  83.4 16.2 %all_to_all.32 = bf16[4,8,13,8,128]{4,3,2,1,0:T(8,128)(2,1)S(1)} all-to-all(bf16[4,8,13,8,128]{4,3,2,1,0:T(8,128)(2,1)S(1)} %bitcast.10), channel_id=1, replica_groups=mesh['y'=4,'za'=2,'zb'=4,'c'=2,'zh'=2,'x'=4] {'y'}, dimensions={0} | all-to-all | bytes 1703936 | tf_op jit(solution)/shard_map/all_to_all | solution.py:79
  99.6 0.8 reduce_sum.25
  100.4 8.0 %all-to-all-start.5 = ((bf16[8,13,8,128]{3,2,1,0:T(8,128)(2,1)}), bf16[8,13,8,128]{3,2,1,0:T(8,128)(2,1)S(1)}, u32[]{:S(2)}, u32[]{:S(2)}) async-start(bf16[8,13,8,128]{3,2,1,0:T(8,128)(2,1)} %reduce_sum.25), calls=%async_computation.5 | async-start | bytes 425984 | tf_op jit(solution)/shard_map/all_to_all | solution.py:79
  108.4 0.6 reduce.2
  109.0 12.8 %all-to-all-done.5.pieces_ref = bf16[8,13,8,128]{3,2,1,0:T(8,128)(2,1)S(1)} async-done(((bf16[8,13,8,128]{3,2,1,0:T(8,128)(2,1)}), bf16[8,13,8,128]{3,2,1,0:T(8,128)(2,1)S(1)}, u32[]{:S(2)}, u32[]{:S(2)}) %all-to-all-start.5) | async-done | bytes 213024 | tf_op jit(solution)/shard_map/all_to_all | solution.py:79
  121.8 0.8 finish.1
  (10 shorter events, 0.0 us)
Async XLA Ops:
  2.1 26.2 %all-to-all-start = ((bf16[8,12,8,128]{3,2,1,0:T(8,128)(2,1)}), bf16[8,12,8,128]{3,2,1,0:T(8,128)(2,1)S(1)}, u32[]{:S(2)}, u32[]{:S(2)}) async-start(bf16[8,12,8,128]{3,2,1,0:T(8,128)(2,1)} %broadcast_in_dim.25), calls=%async_computation | async-start | bytes 393216 | tf_op jit(solution)/shard_map/all_to_all | solution.py:79
  29.3 14.0 %all-to-all-start.1 = ((bf16[4,8,12,8,128]{4,3,2,1,0:T(8,128)(2,1)}), bf16[4,8,12,8,128]{4,3,2,1,0:T(8,128)(2,1)S(1)}, u32[]{:S(2)}, u32[]{:S(2)}) async-start(bf16[4,8,12,8,128]{4,3,2,1,0:T(8,128)(2,1)} %broadcast_in_dim.28), calls=%async_computation.1 | async-start | bytes 1572864 | tf_op jit(solution)/shard_map/all_to_all | solution.py:79
  34.0 2.3 %copy-start = (bf16[576,4096]{1,0:T(8,128)(2,1)S(1)}, bf16[576,4096]{1,0:T(8,128)(2,1)}, u32[]{:S(2)}) copy-start(bf16[576,4096]{1,0:T(8,128)(2,1)} %image_ref.1) | copy-start | bytes 14155780
  36.3 8.9 %copy-start.1 = (s32[576]{0:T(1024)S(1)}, s32[576]{0:T(1024)}, u32[]{:S(2)}) copy-start(s32[576]{0:T(1024)} %param.8) | copy-start | bytes 6916
  36.3 8.9 %copy-start.2 = (s32[576]{0:T(1024)S(1)}, s32[576]{0:T(1024)}, u32[]{:S(2)}) copy-start(s32[576]{0:T(1024)} %param.9) | copy-start | bytes 6916
  36.3 8.9 %copy-start.3 = (f32[576]{0:T(1024)S(1)}, f32[576]{0:T(1024)}, u32[]{:S(2)}) copy-start(f32[576]{0:T(1024)} %param.10) | copy-start | bytes 6916
  43.3 5.2 %collective-permute-start = (bf16[4,8,12,8,128]{4,3,2,1,0:T(8,128)(2,1)S(1)}, bf16[4,8,12,8,128]{4,3,2,1,0:T(8,128)(2,1)S(1)}, u32[]{:S(2)}, u32[]{:S(2)}) collective-permute-start(bf16[4,8,12,8,128]{4,3,2,1,0:T(8,128)(2,1)S(1)} %all-to-all-done.1), channel_id=1, source_target_pairs={{0,8},{8,0},{1,9},{9,1},{2,10},{10,2},{3,11},{11,3},{4,12},{12,4},... | collective-permute-start | bytes 2359304 | tf_op jit(solution)/shard_map/ppermute | solution.py:88
  100.4 21.4 %all-to-all-start.5 = ((bf16[8,13,8,128]{3,2,1,0:T(8,128)(2,1)}), bf16[8,13,8,128]{3,2,1,0:T(8,128)(2,1)S(1)}, u32[]{:S(2)}, u32[]{:S(2)}) async-start(bf16[8,13,8,128]{3,2,1,0:T(8,128)(2,1)} %reduce_sum.25), calls=%async_computation.5 | async-start | bytes 425984 | tf_op jit(solution)/shard_map/all_to_all | solution.py:79

commit v5 on v4

--- a/solution.py
+++ b/solution.py
@@ -19,6 +19,7 @@
 P_DEV = 576
 ROW_BLOCK = 96
 TILES = 12
+PIECES = 96
 
 bf16 = jnp.bfloat16
 f32 = jnp.float32
@@ -45,7 +46,8 @@
     return jnp.concatenate([high, middle, low, jnp.zeros((128 - 3 * SHIFTS, F), f32)], axis=0).astype(bf16)
 
 
-def shift_kernel(index_ref, table_ref, image_ref, out_ref):
+def shift_kernel(place_ref, index_ref, table_ref, image_ref, out_ref, send_ref):
+    core = place_ref[0]
     index = index_ref[...]
     lane = lax.broadcasted_iota(jnp.int32, (ROW_BLOCK, 128), 1)
     chosen = (lane == index) | (lane == index + SHIFTS) | (lane == index + 2 * SHIFTS)
@@ -55,38 +57,48 @@
         sine = jnp.dot(chosen, table_ref[:, H + at : H + at + 512], preferred_element_type=f32)
         real = image_ref[:, at : at + 512].astype(f32)
         imag = image_ref[:, H + at : H + at + 512].astype(f32)
-        out_ref[:, at : at + 512] = (real * cosine + imag * sine).astype(bf16)
-        out_ref[:, H + at : H + at + 512] = (imag * cosine - real * sine).astype(bf16)
-
-
-def shift_particles(particles, shift_index, table):
+        for value, start in ((real * cosine + imag * sine, at // 2), (imag * cosine - real * sine, (H + at) // 2)):
+            for m in range(2):
+                even = value[:, 256 * m : 256 * m + 128]
+                odd = value[:, 256 * m + 128 : 256 * m + 256]
+                column = start + 128 * m
+                out_ref[:, column : column + 128] = even.astype(bf16)
+                out_ref[:, H + column : H + column + 128] = odd.astype(bf16)
+                send_ref[:, column : column + 128] = jnp.where(core == 0, odd, even).astype(bf16)
+
+
+def shift_particles(particles, shift_index, table, place):
     return pl.pallas_call(
         shift_kernel,
         grid=(P_DEV // ROW_BLOCK,),
         in_specs=[
+            pl.BlockSpec(memory_space=pltpu.SMEM),
             pl.BlockSpec((ROW_BLOCK, 1), lambda i: (i, 0)),
             pl.BlockSpec((128, F), lambda i: (0, 0)),
             pl.BlockSpec((ROW_BLOCK, F), lambda i: (i, 0)),
         ],
-        out_specs=pl.BlockSpec((ROW_BLOCK, F), lambda i: (i, 0)),
-        out_shape=pltpu.HBM((P_DEV, F), bf16),
+        out_specs=[pl.BlockSpec((ROW_BLOCK, F), lambda i: (i, 0)), pl.BlockSpec((ROW_BLOCK, H), lambda i: (i, 0))],
+        out_shape=[pltpu.HBM((P_DEV, F), bf16), pltpu.HBM((P_DEV, H), bf16)],
         compiler_params=pltpu.CompilerParams(vmem_limit_bytes=16 << 20),
         name="shift",
-    )(shift_index, table, particles)
+    )(place, shift_index, table, pltpu.with_memory_space_constraint(particles, pltpu.HBM))
 
 
 def exchange(array, axis):
     return lax.all_to_all(array, axis, 0, 0, tiled=True)
 
 
-def gather_table(references, particles, shift_index):
+def gather_table(references, particles, shift_index, place):
     mine = references.reshape(K, TILES, 128).transpose(1, 0, 2)
-    along_z = exchange(jnp.broadcast_to(mine, (8, TILES, K, 128)), Z)
-    along_z, index, phases = lax.optimization_barrier((along_z, shift_index[:, None], phase_table()))
-    along_y = exchange(jnp.broadcast_to(along_z, (4, 8, TILES, K, 128)), "y")
-    along_y, shifted = lax.optimization_barrier((along_y, shift_particles(particles, index, phases)))
+    spread = jnp.broadcast_to(mine, (8, TILES, K, 128))
+    along_z = exchange(spread, Z)
+    shifted, send = shift_particles(particles, shift_index[:, None], phase_table(), place)
+    along_z, shifted, send = lax.optimization_barrier((along_z, shifted, send))
+    spread = jnp.broadcast_to(along_z, (4, 8, TILES, K, 128))
+    along_y = exchange(spread, "y")
+    received = lax.ppermute(send, "c", [(0, 1), (1, 0)])
     other = lax.ppermute(along_y, "c", [(0, 1), (1, 0)])
-    return along_y.reshape(8, 4, TILES, K, 128), other.reshape(8, 4, TILES, K, 128), shifted
+    return along_y.reshape(8, 4, TILES, K, 128), other.reshape(8, 4, TILES, K, 128), shifted, received
 
 
 def fill_table(source_ref, table_ref, core):
@@ -94,11 +106,12 @@
         for b in range(3):
             part = 6 * zb + 3 * core + b
             turn = part // 8
-            column = (part - 8 * turn) * 512
+            column = (part - 8 * turn) * 256
             rows = pl.ds(pl.multiple_of(turn * 64, 64), 64)
             for lanes in range(4):
                 tiles = source_ref[:, zb, 4 * b + lanes].reshape(64, 128)
-                table_ref[rows, pl.ds(pl.multiple_of(column + lanes * 128, 128), 128)] = tiles
+                start = pl.multiple_of(column + lanes % 2 * H + lanes // 2 * 128, 128)
+                table_ref[rows, pl.ds(start, 128)] = tiles
 
 
 def load_kernel(place_ref, own_ref, shifted_ref, images_ref, table_ref, arrived):
@@ -149,8 +162,7 @@
         stats_ref[at, 1:2, :] = mass
 
 
-def local_scores(own, other, shifted, prev_class, prev_rotation, precision):
-    place = jnp.stack([lax.axis_index("c"), lax.axis_index(CLS) * K]).astype(jnp.int32)
+def local_scores(place, own, other, shifted, prev_class, prev_rotation, precision):
     images, half = load_own(place, own, shifted)
     vmem = pl.BlockSpec(memory_space=pltpu.VMEM)
     scores, stats, _ = pl.pallas_call(
@@ -165,7 +177,7 @@
     return scores, stats, images
 
 
-def sum_kernel(stats_ref, scores_ref, shifted_ref, pieces_ref, evidence_ref):
+def weigh_kernel(stats_ref, scores_ref, weights_ref, mass_ref, evidence_ref):
     tops = [stats_ref[i, 0:1, :] for i in range(8)]
     top = tops[0]
     for i in range(1, 8):
@@ -175,78 +187,128 @@
         mass = mass + stats_ref[i, 1:2, :] * jnp.exp(tops[i] - top)
     evidence_ref[...] = top + jnp.log(mass)
     probs = jnp.exp(scores_ref[...] - top) * (1.0 / mass)
-    weights = probs.astype(bf16)
+    weights_ref[...] = probs.astype(bf16)
     occupancy = jnp.sum(probs, axis=1, keepdims=True)
     high = occupancy.astype(bf16).astype(f32)
     low = occupancy - high
-    lane = lax.broadcasted_iota(jnp.int32, (8, K, 128), 2)
-    high = [high[64 * turn : 64 * turn + 64].reshape(8, K, 1) for turn in range(3)]
-    low = [low[64 * turn : 64 * turn + 64].reshape(8, K, 1) for turn in range(3)]
-    for j in range(8):
-        tile = jnp.zeros((8, K, 128), f32)
-        for b in range(3):
-            turn = (3 * j + b) // 8
-            tile = jnp.where(lane == b, high[turn], tile)
-            tile = jnp.where(lane == 3 + b, low[turn], tile)
-        pieces_ref[j % 2, :, j // 2, TILES] = tile.astype(bf16)
+    lane = lax.broadcasted_iota(jnp.int32, (4, K, 128), 2)
+    tile = jnp.zeros((4, K, 128), f32)
+    for za in range(2):
+        for turn in range(3):
+            rows = slice(64 * turn, 64 * turn + 64)
+            spread_high = jnp.broadcast_to(high[rows].reshape(4, 2, K, 1)[:, za], (4, K, 128))
+            spread_low = jnp.broadcast_to(low[rows].reshape(4, 2, K, 1)[:, za], (4, K, 128))
+            for part in range(8 * turn, 8 * turn + 8):
+                at = 6 * (8 * za + part // 3) + part % 3
+                tile = jnp.where(lane == at, spread_high, tile)
+                tile = jnp.where(lane == at + 3, spread_low, tile)
+    mass_ref[...] = tile.astype(bf16)
+
+
+def weigh(stats, scores):
+    vmem = pl.BlockSpec(memory_space=pltpu.VMEM)
+    return pl.pallas_call(
+        weigh_kernel,
+        in_specs=[vmem, vmem],
+        out_specs=[vmem, vmem, vmem],
+        out_shape=[
+            jax.ShapeDtypeStruct((ROWS, P_DEV), bf16),
+            jax.ShapeDtypeStruct((4, K, 128), bf16),
+            jax.ShapeDtypeStruct((1, P_DEV), f32),
+        ],
+        compiler_params=pltpu.CompilerParams(vmem_limit_bytes=16 << 20),
+        name="weigh",
+    )(stats, scores)
+
+
+def sum_kernel(place_ref, weights_ref, mass_ref, shifted_ref, received_ref, pieces_ref):
+    core = place_ref[0]
+    own, other = weights_ref[core], weights_ref[1 - core]
     for q in range(8):
-        numerator = jnp.dot(weights, shifted_ref[:, q * 512 : q * 512 + 512], preferred_element_type=f32)
+        columns = pl.ds(pl.multiple_of(core * H + q * 256, 256), 256)
+        numerator = jnp.dot(own, shifted_ref[:, columns], preferred_element_type=f32)
+        numerator = numerator + jnp.dot(other, received_ref[:, q * 256 : q * 256 + 256], preferred_element_type=f32)
         for turn in range(3):
             part = 8 * turn + q
-            j, b = part // 3, part % 3
-            for lanes in range(4):
-                tile = numerator[64 * turn : 64 * turn + 64, 128 * lanes : 128 * lanes + 128]
-                pieces_ref[j % 2, :, j // 2, 4 * b + lanes] = tile.reshape(8, K, 128).astype(bf16)
-
-
-def local_sums(stats, scores, shifted):
+            for m in range(2):
+                tile = numerator[64 * turn : 64 * turn + 64, 128 * m : 128 * m + 128].reshape(4, 2, K, 128)
+                for za in range(2):
+                    at = 6 * (8 * za + part // 3) + 2 * (part % 3) + m
+                    pieces_ref[:, at] = tile[:, za].astype(bf16)
+    pieces_ref[:, PIECES] = mass_ref[...]
+
+
+def local_sums(place, weights, mass, shifted, received):
     vmem = pl.BlockSpec(memory_space=pltpu.VMEM)
     return pl.pallas_call(
         sum_kernel,
-        in_specs=[vmem, vmem, vmem],
-        out_specs=[vmem, vmem],
-        out_shape=[
-            jax.ShapeDtypeStruct((2, 8, 4, TILES + 1, K, 128), bf16),
-            jax.ShapeDtypeStruct((1, P_DEV), f32),
-        ],
+        in_specs=[pl.BlockSpec(memory_space=pltpu.SMEM)] + [vmem] * 4,
+        out_specs=vmem,
+        out_shape=jax.ShapeDtypeStruct((4, PIECES + 1, K, 128), bf16),
         compiler_params=pltpu.CompilerParams(vmem_limit_bytes=16 << 20),
         name="sums",
-    )(stats, scores, shifted)
-
-
-def finish_kernel(pieces_ref, out_ref):
+    )(place, weights, mass, shifted, received)
+
+
+def fold_kernel(pieces_ref, out_ref):
     total = pieces_ref[0].astype(f32)
-    for i in range(1, 8):
+    for i in range(1, 4):
         total = total + pieces_ref[i].astype(f32)
-    mass = total[TILES]
+    total = total.astype(bf16)
+    for i in range(16):
+        out_ref[i, 0:6] = total[6 * i : 6 * i + 6]
+        out_ref[i, 6] = total[PIECES]
+
+
+def finish_kernel(place_ref, pieces_ref, out_ref):
+    halves = []
+    for half in range(2):
+        total = pieces_ref[half].astype(f32)
+        for i in range(1, 8):
+            total = total + pieces_ref[2 * i + half].astype(f32)
+        halves.append(total)
+    mass = halves[0][6] + halves[1][6]
+    lane = lax.broadcasted_iota(jnp.int32, (K, 128), 1) - 6 * place_ref[2]
     for b in range(3):
-        scale = 1.0 / (mass[:, b : b + 1] + mass[:, 3 + b : 4 + b] + 1.0)
+        picked = jnp.where((lane == b) | (lane == b + 3), mass, 0.0)
+        scale = 1.0 / (jnp.sum(picked, axis=1, keepdims=True) + 1.0)
         for lanes in range(4):
             at = 4 * b + lanes
-            out_ref[:, at * 128 : at * 128 + 128] = total[at] * scale
-
-
-def scatter_sums(pieces):
-    pieces = exchange(pieces, "c").astype(f32)
-    pieces = jnp.sum(pieces, axis=0).astype(bf16)
-    pieces = pieces.reshape(4, 8, TILES + 1, K, 128)
-    pieces = exchange(pieces, "y").astype(f32)
-    pieces = jnp.sum(pieces, axis=0).astype(bf16)
-    pieces = exchange(pieces, Z)
+            out_ref[:, at * 128 : at * 128 + 128] = halves[lanes % 2][2 * b + lanes // 2] * scale
+
+
+def scatter_sums(place, pieces):
+    vmem = pl.BlockSpec(memory_space=pltpu.VMEM)
+    params = pltpu.CompilerParams(vmem_limit_bytes=16 << 20)
+    pieces = exchange(pieces, "y")
+    pieces = pl.pallas_call(
+        fold_kernel,
+        in_specs=[vmem],
+        out_specs=vmem,
+        out_shape=jax.ShapeDtypeStruct((16, 7, K, 128), bf16),
+        compiler_params=params,
+        name="fold",
+    )(pieces)
+    pieces = exchange(pieces, Z + ("c",))
     return pl.pallas_call(
         finish_kernel,
+        in_specs=[pl.BlockSpec(memory_space=pltpu.SMEM), vmem],
+        out_specs=vmem,
         out_shape=jax.ShapeDtypeStruct((K, TILES * 128), f32),
-        compiler_params=pltpu.CompilerParams(vmem_limit_bytes=16 << 20),
+        compiler_params=params,
         name="finish",
-    )(pieces.reshape(8, TILES + 1, K, 128))
+    )(place, pieces)
 
 
 def on_device(particles, shift_index, prev_class, prev_rotation, precision, references):
-    own, other, shifted = gather_table(references, particles, shift_index)
-    scores, stats, images = local_scores(own, other, shifted, prev_class, prev_rotation, precision)
+    place = jnp.stack([lax.axis_index("c"), lax.axis_index(CLS) * K, lax.axis_index(Z + ("c",))]).astype(jnp.int32)
+    own, other, shifted, received = gather_table(references, particles, shift_index, place)
+    scores, stats, images = local_scores(place, own, other, shifted, prev_class, prev_rotation, precision)
     stats = exchange(stats, CLS)
-    pieces, evidence = local_sums(stats, scores, images)
-    return (scatter_sums(pieces), evidence.reshape(P_DEV))
+    weights, mass, evidence = weigh(stats, scores)
+    weights = lax.all_gather(weights, "c", axis=0)
+    pieces = local_sums(place, weights, mass, images, received)
+    return (scatter_sums(place, pieces), evidence.reshape(P_DEV))
 
 
 def solution(mesh):

time: 123 us -> 127 us (1.033)
  the two profiles are of different devices: /device:TPU:32 before, /device:TPU:1 now
where the time goes in v5:
time: 127 us
  blocking collectives  57.3 us (45%)
  starting transfers between devices  29.9 us (24%)
  Pallas kernels  18.6 us (15%)
  waiting for transfers between devices  15.5 us (12%)
  local copies, waits for them, and re-layouts  2.48 us (2%)
  other arithmetic  2.18 us (2%)
    all_to_all x3, blocking collectives, exchange(): return lax.all_to_all(array, axis, 0, 0, tiled=True)  54.1 us
    all_to_all x2, starting transfers between devices, exchange(): return lax.all_to_all(array, axis, 0, 0, tiled=True)  21.2 us
    all_to_all x2, waiting for transfers between devices, exchange(): return lax.all_to_all(array, axis, 0, 0, tiled=True)  15.5 us
    pallas_call x1, Pallas kernels, shift_particles(): pl.pallas_call(shift_kernel, grid=(P_DEV // ROW_BLOCK,), in_specs=[pl.Blo...  8.25 us
    ppermute x1, starting transfers between devices, gather_table(): received = lax.ppermute(send, 'c', [(0, 1), (1, 0)])  5.64 us
    all_gather x1, blocking collectives, on_device(): weights = lax.all_gather(weights, 'c', axis=0)  3.15 us
    pallas_call x1, Pallas kernels, load_own(): pl.pallas_call(load_kernel, in_specs=[pl.BlockSpec(memory_space=pltpu.SME...  3.13 us
    ppermute x1, starting transfers between devices, gather_table(): other = lax.ppermute(along_y, 'c', [(0, 1), (1, 0)])  3.01 us
  transfers between devices with their start and end apart: 4, of which 2 were waited for; matrix products, arithmetic and copies ran while one was open for 3% of the time, Pallas kernels for 12%

profile of v5, /device:TPU:1, one launch (start us, length us, event | category | flops | bytes accessed | tf_op | source)
XLA Modules:
  0.0 126.7 jit_solution(15491931803232179715)
XLA Ops:
  0.6 1.4 %broadcast_in_dim.25 = bf16[8,12,8,128]{3,2,1,0:T(8,128)(2,1)} broadcast(bf16[12,8,128]{2,1,0:T(8,128)(2,1)} %bitcast.12), dimensions={1,2,3} | broadcast | bytes 221184 | tf_op jit(solution)/shard_map/broadcast_in_dim | solution.py:93
  2.1 13.1 %all-to-all-start = ((bf16[8,12,8,128]{3,2,1,0:T(8,128)(2,1)}), bf16[8,12,8,128]{3,2,1,0:T(8,128)(2,1)S(1)}, u32[]{:S(2)}, u32[]{:S(2)}) async-start(bf16[8,12,8,128]{3,2,1,0:T(8,128)(2,1)} %broadcast_in_dim.25), calls=%async_computation | async-start | bytes 393216 | tf_op jit(solution)/shard_map/all_to_all | solution.py:88
  15.2 0.8 broadcast_in_dim.32.index_ref
  16.0 1.1 fusion.5
  17.1 0.1 reduce-precision_convert_fusion.1
  17.3 0.1 pad.3.clone
  17.3 0.1 pad_add_fusion.place_ref
  17.4 0.3 maximum_maximum_fusion.table_ref
  17.7 8.2 %shift.1 = (bf16[576,4096]{1,0:T(8,128)(2,1)}, bf16[576,2048]{1,0:T(8,128)(2,1)}) custom-call(s32[3]{0:T(128)S(1)} %pad_add_fusion.place_ref, s32[576,1]{1,0:T(8,128)S(1)} %broadcast_in_dim.32.index_ref, bf16[128,4096]{1,0:T(8,128)(2,1)S(1)} %maximum_maximum_fusion.table_ref, bf16[576,4096]{1,0:T(8,128)(2,1)} %image_ref.1), custom_call_target="tpu_custom_call" | custom-call | tf_op jit(solution)/shard_map/shift/pallas_call | solution.py:71
  25.9 0.0 copy-start
  25.9 0.3 all-to-all-done
  26.3 5.6 %collective-permute-start.1 = (bf16[576,2048]{1,0:T(8,128)(2,1)}, bf16[576,2048]{1,0:T(8,128)(2,1)S(1)}, u32[]{:S(2)}, u32[]{:S(2)}) collective-permute-start(bf16[576,2048]{1,0:T(8,128)(2,1)} %get-tuple-element.24), channel_id=1, source_target_pairs={{0,8},{8,0},{1,9},{9,1},{2,10},{10,2},{3,11},{11,3},{4,12},{12,4},... | collective-permute-start | bytes 7077896 | tf_op jit(solution)/shard_map/ppermute | solution.py:99
  31.9 0.1 broadcast_in_dim.28
  32.0 16.1 %all_to_all.25 = bf16[4,8,12,8,128]{4,3,2,1,0:T(8,128)(2,1)S(1)} all-to-all(bf16[4,8,12,8,128]{4,3,2,1,0:T(8,128)(2,1)S(1)} %broadcast_in_dim.28), channel_id=1, replica_groups=mesh['y'=4,'za'=2,'zb'=4,'c'=2,'zh'=2,'x'=4] {'y'}, dimensions={0} | all-to-all | bytes 1572864 | tf_op jit(solution)/shard_map/all_to_all | solution.py:88
  48.1 3.0 %collective-permute-start = (bf16[4,8,12,8,128]{4,3,2,1,0:T(8,128)(2,1)S(1)}, bf16[4,8,12,8,128]{4,3,2,1,0:T(8,128)(2,1)S(1)}, u32[]{:S(2)}, u32[]{:S(2)}) collective-permute-start(bf16[4,8,12,8,128]{4,3,2,1,0:T(8,128)(2,1)S(1)} %all_to_all.25), channel_id=1, source_target_pairs={{0,8},{8,0},{1,9},{9,1},{2,10},{10,2},{3,11},{11,3},{4,12},{12,4},... | collective-permute-start | bytes 2359304 | tf_op jit(solution)/shard_map/ppermute | solution.py:100
  51.2 0.0 copy-done
  51.2 0.0 copy-done.1
  51.2 0.0 copy-done.2
  51.2 3.1 %load.1 = (bf16[576,4096]{1,0:T(8,128)(2,1)S(1)}, bf16[192,4096]{1,0:T(8,128)(2,1)S(1)}) custom-call(s32[3]{0:T(128)S(1)} %pad_add_fusion.place_ref, bf16[8,4,12,8,128]{4,3,2,1,0:T(8,128)(2,1)S(1)} %bitcast.9, bf16[576,4096]{1,0:T(8,128)(2,1)} %get-tuple-element.17.shifted_ref), custom_call_target="tpu_custom_call" | custom-call | tf_op jit(solution)/shard_map/load/pallas_call | solution.py:130
  54.4 0.0 collective-permute-done
  54.4 3.0 %scores.1 = (f32[192,576]{1,0:T(8,128)S(1)}, f32[8,2,576]{2,1,0:T(2,128)S(1)}, bf16[192,4096]{1,0:T(8,128)(2,1)S(1)}) custom-call(s32[3]{0:T(128)S(1)} %pad_add_fusion.place_ref, bf16[8,4,12,8,128]{4,3,2,1,0:T(8,128)(2,1)S(1)} %bitcast.11, bf16[192,4096]{1,0:T(8,128)(2,1)S(1)} %get-tuple-element.18.half_ref, ...), custom_call_target="tpu_custom_call", output_to_operand_aliasing={{2}: (2, {})} | custom-call | tf_op jit(solution)/shard_map/scores/pallas_call | solution.py:168
  57.4 23.5 %all_to_all.26.stats_ref = f32[8,2,576]{2,1,0:T(2,128)S(1)} all-to-all(f32[8,2,576]{2,1,0:T(2,128)S(1)} %get-tuple-element.20), channel_id=1, replica_groups=mesh['y'=4,'za'=2,'zb'=4,'c'=2,'zh'=2,'x'=4] {'zh','x'}, dimensions={0} | all-to-all | bytes 73728 | tf_op jit(solution)/shard_map/all_to_all | solution.py:88
  80.9 0.2 weigh.1
  81.1 3.2 %all-gather = bf16[384,576]{1,0:T(8,128)(2,1)S(1)} all-gather(bf16[192,576]{1,0:T(8,128)(2,1)S(1)} %get-tuple-element.22), channel_id=2, replica_groups=mesh['y'=4,'za'=2,'zb'=4,'c'=2,'zh'=2,'x'=4] {'c'}, dimensions={0}, use_global_device_ids=true | all-gather | bytes 663552 | tf_op jit(solution)/shard_map/all_gather | solution.py:309
  84.3 0.0 collective-permute-done.1.received_ref
  84.3 1.9 %sums.1 = bf16[4,97,8,128]{3,2,1,0:T(8,128)(2,1)S(1)} custom-call(s32[3]{0:T(128)S(1)} %pad_add_fusion.place_ref, bf16[2,192,576]{2,1,0:T(8,128)(2,1)S(1)} %bitcast.10, bf16[4,8,128]{2,1,0:T(8,128)(2,1)S(1)} %get-tuple-element.23.mass_ref, bf16[576,4096]{1,0:T(8,128)(2,1)S(1)} %get-tuple-element.19.shifted_ref, ...), custom_call_target="tpu_custom_call" | custom-call | tf_op jit(solution)/shard_map/sums/pallas_call | solution.py:243
  86.2 14.5 %all_to_all.27.pieces_ref = bf16[4,97,8,128]{3,2,1,0:T(8,128)(2,1)S(1)} all-to-all(bf16[4,97,8,128]{3,2,1,0:T(8,128)(2,1)S(1)} %sums.1), channel_id=1, replica_groups=mesh['y'=4,'za'=2,'zb'=4,'c'=2,'zh'=2,'x'=4] {'y'}, dimensions={0} | all-to-all | bytes 1589248 | tf_op jit(solution)/shard_map/all_to_all | solution.py:88
  100.7 0.8 fold.1
  101.5 8.1 %all-to-all-start.4 = ((bf16[16,7,8,128]{3,2,1,0:T(8,128)(2,1)}), bf16[16,7,8,128]{3,2,1,0:T(8,128)(2,1)S(1)}, u32[]{:S(2)}, u32[]{:S(2)}) async-start(bf16[16,7,8,128]{3,2,1,0:T(8,128)(2,1)} %fold.1), calls=%async_computation.4 | async-start | bytes 458752 | tf_op jit(solution)/shard_map/all_to_all | solution.py:88
  109.7 0.6 reduce
  110.3 15.2 %all-to-all-done.4.pieces_ref = bf16[16,7,8,128]{3,2,1,0:T(8,128)(2,1)S(1)} async-done(((bf16[16,7,8,128]{3,2,1,0:T(8,128)(2,1)}), bf16[16,7,8,128]{3,2,1,0:T(8,128)(2,1)S(1)}, u32[]{:S(2)}, u32[]{:S(2)}) %all-to-all-start.4) | async-done | bytes 229408 | tf_op jit(solution)/shard_map/all_to_all | solution.py:88
  125.5 1.3 finish.1
  (8 shorter events, 0.0 us)
Async XLA Ops:
  2.1 24.2 %all-to-all-start = ((bf16[8,12,8,128]{3,2,1,0:T(8,128)(2,1)}), bf16[8,12,8,128]{3,2,1,0:T(8,128)(2,1)S(1)}, u32[]{:S(2)}, u32[]{:S(2)}) async-start(bf16[8,12,8,128]{3,2,1,0:T(8,128)(2,1)} %broadcast_in_dim.25), calls=%async_computation | async-start | bytes 393216 | tf_op jit(solution)/shard_map/all_to_all | solution.py:88
  25.9 25.2 %copy-start = (s32[576]{0:T(1024)S(1)}, s32[576]{0:T(1024)}, u32[]{:S(2)}) copy-start(s32[576]{0:T(1024)} %param.8) | copy-start | bytes 6916
  25.9 25.2 %copy-start.1 = (s32[576]{0:T(1024)S(1)}, s32[576]{0:T(1024)}, u32[]{:S(2)}) copy-start(s32[576]{0:T(1024)} %param.9) | copy-start | bytes 6916
  25.9 25.3 %copy-start.2 = (f32[576]{0:T(1024)S(1)}, f32[576]{0:T(1024)}, u32[]{:S(2)}) copy-start(f32[576]{0:T(1024)} %param.10) | copy-start | bytes 6916
  26.3 58.0 %collective-permute-start.1 = (bf16[576,2048]{1,0:T(8,128)(2,1)}, bf16[576,2048]{1,0:T(8,128)(2,1)S(1)}, u32[]{:S(2)}, u32[]{:S(2)}) collective-permute-start(bf16[576,2048]{1,0:T(8,128)(2,1)} %get-tuple-element.24), channel_id=1, source_target_pairs={{0,8},{8,0},{1,9},{9,1},{2,10},{10,2},{3,11},{11,3},{4,12},{12,4},... | collective-permute-start | bytes 7077896 | tf_op jit(solution)/shard_map/ppermute | solution.py:99
  48.1 6.2 %collective-permute-start = (bf16[4,8,12,8,128]{4,3,2,1,0:T(8,128)(2,1)S(1)}, bf16[4,8,12,8,128]{4,3,2,1,0:T(8,128)(2,1)S(1)}, u32[]{:S(2)}, u32[]{:S(2)}) collective-permute-start(bf16[4,8,12,8,128]{4,3,2,1,0:T(8,128)(2,1)S(1)} %all_to_all.25), channel_id=1, source_target_pairs={{0,8},{8,0},{1,9},{9,1},{2,10},{10,2},{3,11},{11,3},{4,12},{12,4},... | collective-permute-start | bytes 2359304 | tf_op jit(solution)/shard_map/ppermute | solution.py:100
  101.5 23.9 %all-to-all-start.4 = ((bf16[16,7,8,128]{3,2,1,0:T(8,128)(2,1)}), bf16[16,7,8,128]{3,2,1,0:T(8,128)(2,1)S(1)}, u32[]{:S(2)}, u32[]{:S(2)}) async-start(bf16[16,7,8,128]{3,2,1,0:T(8,128)(2,1)} %fold.1), calls=%async_computation.4 | async-start | bytes 458752 | tf_op jit(solution)/shard_map/all_to_all | solution.py:88

commit v6 on v4

--- a/solution.py
+++ b/solution.py
@@ -1,3 +1,4 @@
+import functools
 import math
 
 import jax
@@ -19,6 +20,7 @@
 P_DEV = 576
 ROW_BLOCK = 96
 TILES = 12
+PIECES = 96
 
 bf16 = jnp.bfloat16
 f32 = jnp.float32
@@ -149,8 +151,7 @@
         stats_ref[at, 1:2, :] = mass
 
 
-def local_scores(own, other, shifted, prev_class, prev_rotation, precision):
-    place = jnp.stack([lax.axis_index("c"), lax.axis_index(CLS) * K]).astype(jnp.int32)
+def local_scores(place, own, other, shifted, prev_class, prev_rotation, precision):
     images, half = load_own(place, own, shifted)
     vmem = pl.BlockSpec(memory_space=pltpu.VMEM)
     scores, stats, _ = pl.pallas_call(
@@ -165,7 +166,7 @@
     return scores, stats, images
 
 
-def sum_kernel(stats_ref, scores_ref, shifted_ref, pieces_ref, evidence_ref):
+def sum_kernel(place_ref, stats_ref, scores_ref, shifted_ref, keep_ref, send_ref, evidence_ref):
     tops = [stats_ref[i, 0:1, :] for i in range(8)]
     top = tops[0]
     for i in range(1, 8):
@@ -173,80 +174,116 @@
     mass = jnp.zeros_like(top)
     for i in range(8):
         mass = mass + stats_ref[i, 1:2, :] * jnp.exp(tops[i] - top)
-    evidence_ref[...] = top + jnp.log(mass)
+    evidence_ref[...] = (top + jnp.log(mass)).reshape(P_DEV)
     probs = jnp.exp(scores_ref[...] - top) * (1.0 / mass)
     weights = probs.astype(bf16)
     occupancy = jnp.sum(probs, axis=1, keepdims=True)
     high = occupancy.astype(bf16).astype(f32)
     low = occupancy - high
-    lane = lax.broadcasted_iota(jnp.int32, (8, K, 128), 2)
-    high = [high[64 * turn : 64 * turn + 64].reshape(8, K, 1) for turn in range(3)]
-    low = [low[64 * turn : 64 * turn + 64].reshape(8, K, 1) for turn in range(3)]
-    for j in range(8):
-        tile = jnp.zeros((8, K, 128), f32)
-        for b in range(3):
-            turn = (3 * j + b) // 8
-            tile = jnp.where(lane == b, high[turn], tile)
-            tile = jnp.where(lane == 3 + b, low[turn], tile)
-        pieces_ref[j % 2, :, j // 2, TILES] = tile.astype(bf16)
-    for q in range(8):
-        numerator = jnp.dot(weights, shifted_ref[:, q * 512 : q * 512 + 512], preferred_element_type=f32)
+    lane = lax.broadcasted_iota(jnp.int32, (4, K, 128), 2)
+    masses = [jnp.zeros((4, K, 128), f32), jnp.zeros((4, K, 128), f32)]
+    for za in range(2):
         for turn in range(3):
-            part = 8 * turn + q
-            j, b = part // 3, part % 3
-            for lanes in range(4):
-                tile = numerator[64 * turn : 64 * turn + 64, 128 * lanes : 128 * lanes + 128]
-                pieces_ref[j % 2, :, j // 2, 4 * b + lanes] = tile.reshape(8, K, 128).astype(bf16)
-
-
-def local_sums(stats, scores, shifted):
+            rows = slice(64 * turn, 64 * turn + 64)
+            spread_high = jnp.broadcast_to(high[rows].reshape(4, 2, K, 1)[:, za], (4, K, 128))
+            spread_low = jnp.broadcast_to(low[rows].reshape(4, 2, K, 1)[:, za], (4, K, 128))
+            for part in range(8 * turn, 8 * turn + 8):
+                zb, to, b = part // 6, part // 3 % 2, part % 3
+                at = 6 * (4 * za + zb) + b
+                masses[to] = jnp.where(lane == at, spread_high, masses[to])
+                masses[to] = jnp.where(lane == at + 3, spread_low, masses[to])
+
+    def pack(core):
+        for q in range(8):
+            numerator = jnp.dot(weights, shifted_ref[:, q * 512 : q * 512 + 512], preferred_element_type=f32)
+            for turn in range(3):
+                part = 8 * turn + q
+                zb, to, b = part // 6, part // 3 % 2, part % 3
+                for lanes in range(4):
+                    tile = numerator[64 * turn : 64 * turn + 64, 128 * lanes : 128 * lanes + 128].reshape(4, 2, K, 128)
+                    for za in range(2):
+                        at = 12 * (4 * za + zb) + 4 * b + lanes
+                        if to == core:
+                            keep_ref[:, at] = tile[:, za]
+                        else:
+                            send_ref[:, at] = tile[:, za].astype(bf16)
+        keep_ref[:, PIECES] = masses[core]
+        send_ref[:, PIECES] = masses[1 - core].astype(bf16)
+
+    for core in range(2):
+        pl.when(place_ref[0] == core)(functools.partial(pack, core))
+
+
+def local_sums(place, stats, scores, shifted):
     vmem = pl.BlockSpec(memory_space=pltpu.VMEM)
     return pl.pallas_call(
         sum_kernel,
-        in_specs=[vmem, vmem, vmem],
-        out_specs=[vmem, vmem],
+        in_specs=[pl.BlockSpec(memory_space=pltpu.SMEM)] + [vmem] * 3,
+        out_specs=[vmem, vmem, vmem],
         out_shape=[
-            jax.ShapeDtypeStruct((2, 8, 4, TILES + 1, K, 128), bf16),
-            jax.ShapeDtypeStruct((1, P_DEV), f32),
+            jax.ShapeDtypeStruct((4, PIECES + 1, K, 128), f32),
+            jax.ShapeDtypeStruct((4, PIECES + 1, K, 128), bf16),
+            jax.ShapeDtypeStruct((P_DEV,), f32),
         ],
         compiler_params=pltpu.CompilerParams(vmem_limit_bytes=16 << 20),
         name="sums",
-    )(stats, scores, shifted)
-
-
-def finish_kernel(pieces_ref, out_ref):
+    )(place, stats, scores, shifted)
+
+
+def fold_kernel(pieces_ref, out_ref):
+    total = pieces_ref[0].astype(f32)
+    for i in range(1, 4):
+        total = total + pieces_ref[i].astype(f32)
+    total = total.astype(bf16)
+    for i in range(8):
+        out_ref[i, 0:TILES] = total[TILES * i : TILES * i + TILES]
+        out_ref[i, TILES] = total[PIECES]
+
+
+def finish_kernel(place_ref, pieces_ref, out_ref):
     total = pieces_ref[0].astype(f32)
     for i in range(1, 8):
         total = total + pieces_ref[i].astype(f32)
-    mass = total[TILES]
+    lane = lax.broadcasted_iota(jnp.int32, (K, 128), 1) - 6 * place_ref[2]
     for b in range(3):
-        scale = 1.0 / (mass[:, b : b + 1] + mass[:, 3 + b : 4 + b] + 1.0)
+        picked = jnp.where((lane == b) | (lane == b + 3), total[TILES], 0.0)
+        scale = 1.0 / (jnp.sum(picked, axis=1, keepdims=True) + 1.0)
         for lanes in range(4):
             at = 4 * b + lanes
             out_ref[:, at * 128 : at * 128 + 128] = total[at] * scale
 
 
-def scatter_sums(pieces):
-    pieces = exchange(pieces, "c").astype(f32)
-    pieces = jnp.sum(pieces, axis=0).astype(bf16)
-    pieces = pieces.reshape(4, 8, TILES + 1, K, 128)
-    pieces = exchange(pieces, "y").astype(f32)
-    pieces = jnp.sum(pieces, axis=0).astype(bf16)
+def scatter_sums(place, keep, send):
+    vmem = pl.BlockSpec(memory_space=pltpu.VMEM)
+    params = pltpu.CompilerParams(vmem_limit_bytes=16 << 20)
+    received = lax.ppermute(send, "c", [(0, 1), (1, 0)])
+    pieces = exchange((keep + received.astype(f32)).astype(bf16), "y")
+    pieces = pl.pallas_call(
+        fold_kernel,
+        in_specs=[vmem],
+        out_specs=vmem,
+        out_shape=jax.ShapeDtypeStruct((8, TILES + 1, K, 128), bf16),
+        compiler_params=params,
+        name="fold",
+    )(pieces)
     pieces = exchange(pieces, Z)
     return pl.pallas_call(
         finish_kernel,
+        in_specs=[pl.BlockSpec(memory_space=pltpu.SMEM), vmem],
+        out_specs=vmem,
         out_shape=jax.ShapeDtypeStruct((K, TILES * 128), f32),
-        compiler_params=pltpu.CompilerParams(vmem_limit_bytes=16 << 20),
+        compiler_params=params,
         name="finish",
-    )(pieces.reshape(8, TILES + 1, K, 128))
+    )(place, pieces)
 
 
 def on_device(particles, shift_index, prev_class, prev_rotation, precision, references):
+    place = jnp.stack([lax.axis_index("c"), lax.axis_index(CLS) * K, lax.axis_index(Z)]).astype(jnp.int32)
     own, other, shifted = gather_table(references, particles, shift_index)
-    scores, stats, images = local_scores(own, other, shifted, prev_class, prev_rotation, precision)
+    scores, stats, images = local_scores(place, own, other, shifted, prev_class, prev_rotation, precision)
     stats = exchange(stats, CLS)
-    pieces, evidence = local_sums(stats, scores, images)
-    return (scatter_sums(pieces), evidence.reshape(P_DEV))
+    keep, send, evidence = local_sums(place, stats, scores, images)
+    return (scatter_sums(place, keep, send), evidence)
 
 
 def solution(mesh):

time: 123 us -> 122 us (level)
  blocking collectives: 46.1 us -> 61.9 us
  waiting for transfers between devices: 26.1 us -> 15.5 us
  starting transfers between devices: 27 us -> 20.9 us
  Pallas kernels: 13.3 us -> 15.2 us
  other arithmetic: 3.6 us -> 1.76 us
    all_to_all x3, blocking collectives: 46.1 us -> 61.9 us  [exchange(): return lax.all_to_all(array, axis, 0, 0, tiled=True)]
    all_to_all x3 -> x2, waiting for transfers between devices: 26.1 us -> 13.2 us  [exchange(): return lax.all_to_all(array, axis, 0, 0, tiled=True)]
    all_to_all x3 -> x2, starting transfers between devices: 25.1 us -> 17.1 us  [exchange(): return lax.all_to_all(array, axis, 0, 0, tiled=True)]
    ppermute x0 -> x1, waiting for transfers between devices: none -> 2.26 us  [scatter_sums(): received = lax.ppermute(send, 'c', [(0, 1), (1, 0)])]
    ppermute x0 -> x1, starting transfers between devices: none -> 1.91 us  [scatter_sums(): received = lax.ppermute(send, 'c', [(0, 1), (1, 0)])]
    pallas_call x2 -> x3, Pallas kernels: 2.2 us -> 4.1 us  [the longest x1 2.74 us: local_sums(): pl.pallas_call(sum_kernel, in_specs=[pl.BlockSpec(memory_space=pltpu.SMEM...]
    reduce_sum x2 -> x0, other arithmetic: 1.41 us -> none  [scatter_sums(): pieces = jnp.sum(pieces, axis=0).astype(bf16)]
  transfers between devices with their start and end apart: 4 -> 4, of which waited for: 3 -> 3; matrix products, arithmetic and copies ran while one was open for 3% -> 2% of each run, Pallas kernels for 7% -> 7%
where the time goes in v6:
time: 122 us
  blocking collectives  61.9 us (51%)
  starting transfers between devices  20.9 us (17%)
  waiting for transfers between devices  15.5 us (13%)
  Pallas kernels  15.2 us (12%)
  local copies, waits for them, and re-layouts  5.74 us (5%)
  other arithmetic  1.76 us (1%)
    all_to_all x3, blocking collectives, exchange(): return lax.all_to_all(array, axis, 0, 0, tiled=True)  61.9 us
    all_to_all x2, starting transfers between devices, exchange(): return lax.all_to_all(array, axis, 0, 0, tiled=True)  17.1 us
    all_to_all x2, waiting for transfers between devices, exchange(): return lax.all_to_all(array, axis, 0, 0, tiled=True)  13.2 us
    pallas_call x1, Pallas kernels, shift_particles(): pl.pallas_call(shift_kernel, grid=(P_DEV // ROW_BLOCK,), in_specs=[pl.Blo...  5.06 us
    pallas_call x1, Pallas kernels, load_own(): pl.pallas_call(load_kernel, in_specs=[pl.BlockSpec(memory_space=pltpu.SME...  3.12 us
    pallas_call x1, Pallas kernels, local_scores(): pl.pallas_call(score_kernel, in_specs=[pl.BlockSpec(memory_space=pltpu.SM...  2.94 us
    pallas_call x1, Pallas kernels, local_sums(): pl.pallas_call(sum_kernel, in_specs=[pl.BlockSpec(memory_space=pltpu.SMEM...  2.74 us
  transfers between devices with their start and end apart: 4, of which 3 were waited for; matrix products, arithmetic and copies ran while one was open for 2% of the time, Pallas kernels for 7%

profile of v6, /device:TPU:32, one launch (start us, length us, event | category | flops | bytes accessed | tf_op | source)
XLA Modules:
  0.0 121.8 jit_solution(9812109982012105838)
XLA Ops:
  0.6 1.4 %broadcast_in_dim.25 = bf16[8,12,8,128]{3,2,1,0:T(8,128)(2,1)} broadcast(bf16[12,8,128]{2,1,0:T(8,128)(2,1)} %bitcast.10), dimensions={1,2,3} | broadcast | bytes 221184 | tf_op jit(solution)/shard_map/broadcast_in_dim | solution.py:86
  2.1 12.6 %all-to-all-start = ((bf16[8,12,8,128]{3,2,1,0:T(8,128)(2,1)}), bf16[8,12,8,128]{3,2,1,0:T(8,128)(2,1)S(1)}, u32[]{:S(2)}, u32[]{:S(2)}) async-start(bf16[8,12,8,128]{3,2,1,0:T(8,128)(2,1)} %broadcast_in_dim.25), calls=%async_computation | async-start | bytes 393216 | tf_op jit(solution)/shard_map/all_to_all | solution.py:81
  14.7 0.7 broadcast_in_dim.26
  15.4 1.1 fusion.5
  16.5 0.1 reduce-precision_convert_fusion.1
  16.7 0.1 pad.3.clone
  16.7 0.3 maximum_maximum_fusion.table_ref
  17.0 11.3 %all-to-all-done = bf16[8,12,8,128]{3,2,1,0:T(8,128)(2,1)S(1)} async-done(((bf16[8,12,8,128]{3,2,1,0:T(8,128)(2,1)}), bf16[8,12,8,128]{3,2,1,0:T(8,128)(2,1)S(1)}, u32[]{:S(2)}, u32[]{:S(2)}) %all-to-all-start) | async-done | bytes 196640 | tf_op jit(solution)/shard_map/all_to_all | solution.py:81
  28.3 1.0 broadcast_in_dim.28
  29.3 4.5 %all-to-all-start.1 = ((bf16[4,8,12,8,128]{4,3,2,1,0:T(8,128)(2,1)}), bf16[4,8,12,8,128]{4,3,2,1,0:T(8,128)(2,1)S(1)}, u32[]{:S(2)}, u32[]{:S(2)}) async-start(bf16[4,8,12,8,128]{4,3,2,1,0:T(8,128)(2,1)} %broadcast_in_dim.28), calls=%async_computation.1 | async-start | bytes 1572864 | tf_op jit(solution)/shard_map/all_to_all | solution.py:81
  33.8 0.2 copy.9.index_ref
  33.9 0.0 copy-start
  34.0 2.3 %copy-done = bf16[576,4096]{1,0:T(8,128)(2,1)S(1)} copy-done((bf16[576,4096]{1,0:T(8,128)(2,1)S(1)}, bf16[576,4096]{1,0:T(8,128)(2,1)}, u32[]{:S(2)}) %copy-start) | copy-done | bytes 4718616
  36.3 5.1 %shift.1.shifted_ref = bf16[576,4096]{1,0:T(8,128)(2,1)} custom-call(s32[576,1]{1,0:T(8,128)S(1)} %copy.9.index_ref, bf16[128,4096]{1,0:T(8,128)(2,1)S(1)} %maximum_maximum_fusion.table_ref, bf16[576,4096]{1,0:T(8,128)(2,1)S(1)} %copy-done), custom_call_target="tpu_custom_call" | custom-call | tf_op jit(solution)/shard_map/shift/pallas_call | solution.py:65
  41.4 1.9 %all-to-all-done.1 = bf16[4,8,12,8,128]{4,3,2,1,0:T(8,128)(2,1)S(1)} async-done(((bf16[4,8,12,8,128]{4,3,2,1,0:T(8,128)(2,1)}), bf16[4,8,12,8,128]{4,3,2,1,0:T(8,128)(2,1)S(1)}, u32[]{:S(2)}, u32[]{:S(2)}) %all-to-all-start.1) | async-done | bytes 786464 | tf_op jit(solution)/shard_map/all_to_all | solution.py:81
  43.3 1.9 %collective-permute-start = (bf16[4,8,12,8,128]{4,3,2,1,0:T(8,128)(2,1)S(1)}, bf16[4,8,12,8,128]{4,3,2,1,0:T(8,128)(2,1)S(1)}, u32[]{:S(2)}, u32[]{:S(2)}) collective-permute-start(bf16[4,8,12,8,128]{4,3,2,1,0:T(8,128)(2,1)S(1)} %all-to-all-done.1), channel_id=1, source_target_pairs={{0,8},{8,0},{1,9},{9,1},{2,10},{10,2},{3,11},{11,3},{4,12},{12,4},... | collective-permute-start | bytes 2359304 | tf_op jit(solution)/shard_map/ppermute | solution.py:90
  45.2 0.0 copy-done.1
  45.2 0.0 copy-done.2
  45.2 0.0 copy-done.3
  45.3 0.1 pad_add_fusion.place_ref
  45.4 3.1 %load.1 = (bf16[576,4096]{1,0:T(8,128)(2,1)S(1)}, bf16[192,4096]{1,0:T(8,128)(2,1)S(1)}) custom-call(s32[3]{0:T(128)S(1)} %pad_add_fusion.place_ref, bf16[8,4,12,8,128]{4,3,2,1,0:T(8,128)(2,1)S(1)} %bitcast.8, bf16[576,4096]{1,0:T(8,128)(2,1)} %shift.1.shifted_ref), custom_call_target="tpu_custom_call" | custom-call | tf_op jit(solution)/shard_map/load/pallas_call | solution.py:119
  48.5 0.0 collective-permute-done
  48.5 2.9 %scores.1 = (f32[192,576]{1,0:T(8,128)S(1)}, f32[8,2,576]{2,1,0:T(2,128)S(1)}, bf16[192,4096]{1,0:T(8,128)(2,1)S(1)}) custom-call(s32[3]{0:T(128)S(1)} %pad_add_fusion.place_ref, bf16[8,4,12,8,128]{4,3,2,1,0:T(8,128)(2,1)S(1)} %bitcast.9, bf16[192,4096]{1,0:T(8,128)(2,1)S(1)} %get-tuple-element.19.half_ref, ...), custom_call_target="tpu_custom_call", output_to_operand_aliasing={{2}: (2, {})} | custom-call | tf_op jit(solution)/shard_map/scores/pallas_call | solution.py:157
  51.4 24.8 %all_to_all.25.stats_ref = f32[8,2,576]{2,1,0:T(2,128)S(1)} all-to-all(f32[8,2,576]{2,1,0:T(2,128)S(1)} %get-tuple-element.21), channel_id=1, replica_groups=mesh['y'=4,'za'=2,'zb'=4,'c'=2,'zh'=2,'x'=4] {'zh','x'}, dimensions={0} | all-to-all | bytes 73728 | tf_op jit(solution)/shard_map/all_to_all | solution.py:81
  76.3 2.7 %sums.1 = (f32[4,97,8,128]{3,2,1,0:T(8,128)S(1)}, bf16[4,97,8,128]{3,2,1,0:T(8,128)(2,1)S(1)}, f32[576]{0:T(1024)}) custom-call(s32[3]{0:T(128)S(1)} %pad_add_fusion.place_ref, f32[8,2,576]{2,1,0:T(2,128)S(1)} %all_to_all.25.stats_ref, f32[192,576]{1,0:T(8,128)S(1)} %get-tuple-element.22.scores_ref, bf16[576,4096]{1,0:T(8,128)(2,1)S(1)} %get-tuple-element.20.shifted_ref), custom_call_target="tpu_custom_call" | custom-call | tf_op jit(solution)/shard_map/sums/pallas_call | solution.py:219
  79.0 1.9 %collective-permute-start.1 = (bf16[4,97,8,128]{3,2,1,0:T(8,128)(2,1)S(1)}, bf16[4,97,8,128]{3,2,1,0:T(8,128)(2,1)S(1)}, u32[]{:S(2)}, u32[]{:S(2)}) collective-permute-start(bf16[4,97,8,128]{3,2,1,0:T(8,128)(2,1)S(1)} %get-tuple-element.24), channel_id=1, source_target_pairs={{0,8},{8,0},{1,9},{9,1},{2,10},{10,2},{3,11},{11,3},{4,12},{12,4},... | collective-permute-start | bytes 2383880 | tf_op jit(solution)/shard_map/ppermute | solution.py:259
  80.9 2.3 %collective-permute-done.1 = bf16[4,97,8,128]{3,2,1,0:T(8,128)(2,1)S(1)} collective-permute-done((bf16[4,97,8,128]{3,2,1,0:T(8,128)(2,1)S(1)}, bf16[4,97,8,128]{3,2,1,0:T(8,128)(2,1)S(1)}, u32[]{:S(2)}, u32[]{:S(2)}) %collective-permute-start.1) | collective-permute-done | bytes 794656 | tf_op jit(solution)/shard_map/ppermute | solution.py:259
  83.2 0.2 add_convert_fusion
  83.4 15.6 %all_to_all.26.pieces_ref = bf16[4,97,8,128]{3,2,1,0:T(8,128)(2,1)S(1)} all-to-all(bf16[4,97,8,128]{3,2,1,0:T(8,128)(2,1)S(1)} %add_convert_fusion), channel_id=1, replica_groups=mesh['y'=4,'za'=2,'zb'=4,'c'=2,'zh'=2,'x'=4] {'y'}, dimensions={0} | all-to-all | bytes 1589248 | tf_op jit(solution)/shard_map/all_to_all | solution.py:81
  99.0 0.1 fold.1
  99.1 21.5 %all_to_all.27.pieces_ref = bf16[8,13,8,128]{3,2,1,0:T(8,128)(2,1)S(1)} all-to-all(bf16[8,13,8,128]{3,2,1,0:T(8,128)(2,1)S(1)} %fold.1), channel_id=1, replica_groups=mesh['y'=4,'za'=2,'zb'=4,'c'=2,'zh'=2,'x'=4] {'za','zb'}, dimensions={0} | all-to-all | bytes 425984 | tf_op jit(solution)/shard_map/all_to_all | solution.py:81
  120.6 1.3 %finish.1 = f32[8,1536]{1,0:T(8,128)} custom-call(s32[3]{0:T(128)S(1)} %pad_add_fusion.place_ref, bf16[8,13,8,128]{3,2,1,0:T(8,128)(2,1)S(1)} %all_to_all.27.pieces_ref), custom_call_target="tpu_custom_call" | custom-call | tf_op jit(solution)/shard_map/finish/pallas_call | solution.py:270
  (9 shorter events, 0.0 us)
Async XLA Ops:
  2.1 26.2 %all-to-all-start = ((bf16[8,12,8,128]{3,2,1,0:T(8,128)(2,1)}), bf16[8,12,8,128]{3,2,1,0:T(8,128)(2,1)S(1)}, u32[]{:S(2)}, u32[]{:S(2)}) async-start(bf16[8,12,8,128]{3,2,1,0:T(8,128)(2,1)} %broadcast_in_dim.25), calls=%async_computation | async-start | bytes 393216 | tf_op jit(solution)/shard_map/all_to_all | solution.py:81
  29.3 14.0 %all-to-all-start.1 = ((bf16[4,8,12,8,128]{4,3,2,1,0:T(8,128)(2,1)}), bf16[4,8,12,8,128]{4,3,2,1,0:T(8,128)(2,1)S(1)}, u32[]{:S(2)}, u32[]{:S(2)}) async-start(bf16[4,8,12,8,128]{4,3,2,1,0:T(8,128)(2,1)} %broadcast_in_dim.28), calls=%async_computation.1 | async-start | bytes 1572864 | tf_op jit(solution)/shard_map/all_to_all | solution.py:81
  33.9 2.3 %copy-start = (bf16[576,4096]{1,0:T(8,128)(2,1)S(1)}, bf16[576,4096]{1,0:T(8,128)(2,1)}, u32[]{:S(2)}) copy-start(bf16[576,4096]{1,0:T(8,128)(2,1)} %image_ref.1) | copy-start | bytes 14155780
  36.3 8.9 %copy-start.1 = (s32[576]{0:T(1024)S(1)}, s32[576]{0:T(1024)}, u32[]{:S(2)}) copy-start(s32[576]{0:T(1024)} %param.8) | copy-start | bytes 6916
  36.3 8.9 %copy-start.2 = (s32[576]{0:T(1024)S(1)}, s32[576]{0:T(1024)}, u32[]{:S(2)}) copy-start(s32[576]{0:T(1024)} %param.9) | copy-start | bytes 6916
  36.3 9.0 %copy-start.3 = (f32[576]{0:T(1024)S(1)}, f32[576]{0:T(1024)}, u32[]{:S(2)}) copy-start(f32[576]{0:T(1024)} %param.10) | copy-start | bytes 6916
  43.3 5.2 %collective-permute-start = (bf16[4,8,12,8,128]{4,3,2,1,0:T(8,128)(2,1)S(1)}, bf16[4,8,12,8,128]{4,3,2,1,0:T(8,128)(2,1)S(1)}, u32[]{:S(2)}, u32[]{:S(2)}) collective-permute-start(bf16[4,8,12,8,128]{4,3,2,1,0:T(8,128)(2,1)S(1)} %all-to-all-done.1), channel_id=1, source_target_pairs={{0,8},{8,0},{1,9},{9,1},{2,10},{10,2},{3,11},{11,3},{4,12},{12,4},... | collective-permute-start | bytes 2359304 | tf_op jit(solution)/shard_map/ppermute | solution.py:90
  79.0 4.2 %collective-permute-start.1 = (bf16[4,97,8,128]{3,2,1,0:T(8,128)(2,1)S(1)}, bf16[4,97,8,128]{3,2,1,0:T(8,128)(2,1)S(1)}, u32[]{:S(2)}, u32[]{:S(2)}) collective-permute-start(bf16[4,97,8,128]{3,2,1,0:T(8,128)(2,1)S(1)} %get-tuple-element.24), channel_id=1, source_target_pairs={{0,8},{8,0},{1,9},{9,1},{2,10},{10,2},{3,11},{11,3},{4,12},{12,4},... | collective-permute-start | bytes 2383880 | tf_op jit(solution)/shard_map/ppermute | solution.py:259

commit v7 on v6

--- a/solution.py
+++ b/solution.py
@@ -1,8 +1,9 @@
-import functools
 import math
 
 import jax
 import jax.numpy as jnp
+import ml_dtypes
+import numpy as np
 from jax import lax
 from jax.experimental import pallas as pl
 from jax.experimental.pallas import tpu as pltpu
@@ -18,7 +19,7 @@
 SHIFTS = 25
 SIDE = 5
 P_DEV = 576
-ROW_BLOCK = 96
+ROW_BLOCK = 288
 TILES = 12
 PIECES = 96
 
@@ -31,20 +32,18 @@
 
 
 def phase_table():
-    frequency = jnp.arange(H, dtype=jnp.int32)
-    freq_x = frequency % BOX - BOX // 2
-    freq_y = frequency // BOX
-    shift = jnp.arange(SHIFTS, dtype=jnp.int32)
-    step_x = shift % SIDE - 2
-    step_y = shift // SIDE - 2
-    phase = (freq_x[None, :] * step_x[:, None] + freq_y[None, :] * step_y[:, None]) % BOX
-    angle = phase.astype(f32) * (2.0 * math.pi / BOX)
-    exact = jnp.concatenate([jnp.cos(angle), jnp.sin(angle)], axis=1)
-    high = lax.reduce_precision(exact, 8, 7)
-    rest = exact - high
-    middle = lax.reduce_precision(rest, 8, 7)
-    low = rest - middle
-    return jnp.concatenate([high, middle, low, jnp.zeros((128 - 3 * SHIFTS, F), f32)], axis=0).astype(bf16)
+    frequency = np.arange(H)
+    shift = np.arange(SHIFTS)
+    step_x, step_y = shift % SIDE - 2, shift // SIDE - 2
+    phase = (np.outer(step_x, frequency % BOX - BOX // 2) + np.outer(step_y, frequency // BOX)) % BOX
+    angle = phase * (2.0 * math.pi / BOX)
+    rest = np.concatenate([np.cos(angle), np.sin(angle)], axis=1).astype(np.float32)
+    terms = []
+    for _ in range(3):
+        terms.append(rest.astype(ml_dtypes.bfloat16))
+        rest = rest - terms[-1].astype(np.float32)
+    terms.append(np.zeros((128 - 3 * SHIFTS, F), ml_dtypes.bfloat16))
+    return jnp.asarray(np.concatenate(terms, axis=0))
 
 
 def shift_kernel(index_ref, table_ref, image_ref, out_ref):
@@ -74,7 +73,7 @@
         out_shape=pltpu.HBM((P_DEV, F), bf16),
         compiler_params=pltpu.CompilerParams(vmem_limit_bytes=16 << 20),
         name="shift",
-    )(shift_index, table, particles)
+    )(shift_index, table, pltpu.with_memory_space_constraint(particles, pltpu.HBM))
 
 
 def exchange(array, axis):
@@ -84,9 +83,9 @@
 def gather_table(references, particles, shift_index):
     mine = references.reshape(K, TILES, 128).transpose(1, 0, 2)
     along_z = exchange(jnp.broadcast_to(mine, (8, TILES, K, 128)), Z)
-    along_z, index, phases = lax.optimization_barrier((along_z, shift_index[:, None], phase_table()))
+    along_z, index = lax.optimization_barrier((along_z, shift_index))
     along_y = exchange(jnp.broadcast_to(along_z, (4, 8, TILES, K, 128)), "y")
-    along_y, shifted = lax.optimization_barrier((along_y, shift_particles(particles, index, phases)))
+    along_y, shifted = lax.optimization_barrier((along_y, shift_particles(particles, index[:, None], phase_table())))
     other = lax.ppermute(along_y, "c", [(0, 1), (1, 0)])
     return along_y.reshape(8, 4, TILES, K, 128), other.reshape(8, 4, TILES, K, 128), shifted
 
@@ -193,25 +192,27 @@
                 masses[to] = jnp.where(lane == at, spread_high, masses[to])
                 masses[to] = jnp.where(lane == at + 3, spread_low, masses[to])
 
-    def pack(core):
-        for q in range(8):
-            numerator = jnp.dot(weights, shifted_ref[:, q * 512 : q * 512 + 512], preferred_element_type=f32)
-            for turn in range(3):
-                part = 8 * turn + q
-                zb, to, b = part // 6, part // 3 % 2, part % 3
-                for lanes in range(4):
-                    tile = numerator[64 * turn : 64 * turn + 64, 128 * lanes : 128 * lanes + 128].reshape(4, 2, K, 128)
-                    for za in range(2):
-                        at = 12 * (4 * za + zb) + 4 * b + lanes
-                        if to == core:
-                            keep_ref[:, at] = tile[:, za]
-                        else:
-                            send_ref[:, at] = tile[:, za].astype(bf16)
-        keep_ref[:, PIECES] = masses[core]
-        send_ref[:, PIECES] = masses[1 - core].astype(bf16)
-
-    for core in range(2):
-        pl.when(place_ref[0] == core)(functools.partial(pack, core))
+    swap = place_ref[0] == 1
+    numerators = {}
+    for q in range(8):
+        numerator = jnp.dot(weights, shifted_ref[:, q * 512 : q * 512 + 512], preferred_element_type=f32)
+        for turn in range(3):
+            numerators[8 * turn + q] = numerator[64 * turn : 64 * turn + 64]
+    for part in range(24):
+        if part // 3 % 2:
+            continue
+        zb, b = part // 6, part % 3
+        first, second = numerators[part], numerators[part + 3]
+        keep = jnp.where(swap, second, first)
+        send = jnp.where(swap, first, second)
+        for lanes in range(4):
+            columns = slice(128 * lanes, 128 * lanes + 128)
+            for za in range(2):
+                at = 12 * (4 * za + zb) + 4 * b + lanes
+                keep_ref[:, at] = keep[:, columns].reshape(4, 2, K, 128)[:, za]
+                send_ref[:, at] = send[:, columns].reshape(4, 2, K, 128)[:, za].astype(bf16)
+    keep_ref[:, PIECES] = jnp.where(swap, masses[1], masses[0])
+    send_ref[:, PIECES] = jnp.where(swap, masses[0], masses[1]).astype(bf16)
 
 
 def local_sums(place, stats, scores, shifted):

time: 122 us -> 121 us (level)
  blocking collectives: 61.9 us -> 88.1 us
  starting transfers between devices: 20.9 us -> 8.28 us
  waiting for transfers between devices: 15.5 us -> 5.41 us
  local copies, waits for them, and re-layouts: 5.74 us -> 1.96 us
  other arithmetic: 1.76 us -> 0.25 us
    all_to_all x3 -> x4, blocking collectives: 61.9 us -> 88.1 us  [exchange(): return lax.all_to_all(array, axis, 0, 0, tiled=True)]
    all_to_all x2 -> x1, starting transfers between devices: 17.1 us -> 4.46 us  [exchange(): return lax.all_to_all(array, axis, 0, 0, tiled=True)]
    all_to_all x2 -> x1, waiting for transfers between devices: 13.2 us -> 3.14 us  [exchange(): return lax.all_to_all(array, axis, 0, 0, tiled=True)]
    unnamed x8 -> x10, local copies, waits for them, and re-layouts: 2.35 us -> 0.03 us
  transfers between devices with their start and end apart: 4 -> 3, of which waited for: 3 -> 2; matrix products, arithmetic and copies ran while one was open for 2% -> 0% of each run, Pallas kernels for 7% -> 8%
where the time goes in v7:
time: 121 us
  blocking collectives  88.1 us (73%)
  Pallas kernels  16.1 us (13%)
  starting transfers between devices  8.28 us (7%)
  waiting for transfers between devices  5.41 us (4%)
  local copies, waits for them, and re-layouts  1.96 us (2%)
    all_to_all x4, blocking collectives, exchange(): return lax.all_to_all(array, axis, 0, 0, tiled=True)  88.1 us
    pallas_call x1, Pallas kernels, shift_particles(): pl.pallas_call(shift_kernel, grid=(P_DEV // ROW_BLOCK,), in_specs=[pl.Blo...  6.16 us
    all_to_all x1, starting transfers between devices, exchange(): return lax.all_to_all(array, axis, 0, 0, tiled=True)  4.46 us
    all_to_all x1, waiting for transfers between devices, exchange(): return lax.all_to_all(array, axis, 0, 0, tiled=True)  3.14 us
    pallas_call x1, Pallas kernels, load_own(): pl.pallas_call(load_kernel, in_specs=[pl.BlockSpec(memory_space=pltpu.SME...  3.12 us
    pallas_call x1, Pallas kernels, local_scores(): pl.pallas_call(score_kernel, in_specs=[pl.BlockSpec(memory_space=pltpu.SM...  2.95 us
    pallas_call x1, Pallas kernels, local_sums(): pl.pallas_call(sum_kernel, in_specs=[pl.BlockSpec(memory_space=pltpu.SMEM...  2.48 us
  transfers between devices with their start and end apart: 3, of which 2 were waited for; matrix products, arithmetic and copies ran while one was open for 0% of the time, Pallas kernels for 8%

profile of v7, /device:TPU:32, one launch (start us, length us, event | category | flops | bytes accessed | tf_op | source)
XLA Modules:
  0.0 120.8 jit_solution(2344076006629372515)
XLA Ops:
  0.6 0.0 copy-start.1
  0.6 0.8 broadcast_in_dim.18
  1.4 0.0 copy-start
  1.4 26.2 %all_to_all.25 = bf16[8,12,8,128]{3,2,1,0:T(8,128)(2,1)S(1)} all-to-all(bf16[8,12,8,128]{3,2,1,0:T(8,128)(2,1)S(1)} %broadcast_in_dim.18), channel_id=1, replica_groups=mesh['y'=4,'za'=2,'zb'=4,'c'=2,'zh'=2,'x'=4] {'za','zb'}, dimensions={0} | all-to-all | bytes 393216 | tf_op jit(solution)/shard_map/all_to_all | solution.py:80
  27.6 1.0 broadcast_in_dim.19
  28.6 4.5 %all-to-all-start.1 = ((bf16[4,8,12,8,128]{4,3,2,1,0:T(8,128)(2,1)}), bf16[4,8,12,8,128]{4,3,2,1,0:T(8,128)(2,1)S(1)}, u32[]{:S(2)}, u32[]{:S(2)}) async-start(bf16[4,8,12,8,128]{4,3,2,1,0:T(8,128)(2,1)} %broadcast_in_dim.19), calls=%async_computation.1 | async-start | bytes 1572864 | tf_op jit(solution)/shard_map/all_to_all | solution.py:80
  33.1 0.0 copy-done.1
  33.1 0.1 broadcast_in_dim.24.index_ref
  33.2 0.0 copy-done
  33.2 0.0 copy-start.2
  33.2 0.0 copy-start.3
  33.2 0.0 copy-start.4
  33.3 6.2 %shift.1.shifted_ref = bf16[576,4096]{1,0:T(8,128)(2,1)} custom-call(s32[576,1]{1,0:T(8,128)S(1)} %broadcast_in_dim.24.index_ref, bf16[128,4096]{1,0:T(8,128)(2,1)S(1)} %copy-done, bf16[576,4096]{1,0:T(8,128)(2,1)} %image_ref.1), custom_call_target="tpu_custom_call" | custom-call | tf_op jit(solution)/shard_map/shift/pallas_call | solution.py:64
  39.4 3.1 %all-to-all-done.1 = bf16[4,8,12,8,128]{4,3,2,1,0:T(8,128)(2,1)S(1)} async-done(((bf16[4,8,12,8,128]{4,3,2,1,0:T(8,128)(2,1)}), bf16[4,8,12,8,128]{4,3,2,1,0:T(8,128)(2,1)S(1)}, u32[]{:S(2)}, u32[]{:S(2)}) %all-to-all-start.1) | async-done | bytes 786464 | tf_op jit(solution)/shard_map/all_to_all | solution.py:80
  42.6 1.9 %collective-permute-start = (bf16[4,8,12,8,128]{4,3,2,1,0:T(8,128)(2,1)S(1)}, bf16[4,8,12,8,128]{4,3,2,1,0:T(8,128)(2,1)S(1)}, u32[]{:S(2)}, u32[]{:S(2)}) collective-permute-start(bf16[4,8,12,8,128]{4,3,2,1,0:T(8,128)(2,1)S(1)} %all-to-all-done.1), channel_id=1, source_target_pairs={{0,8},{8,0},{1,9},{9,1},{2,10},{10,2},{3,11},{11,3},{4,12},{12,4},... | collective-permute-start | bytes 2359304 | tf_op jit(solution)/shard_map/ppermute | solution.py:89
  44.5 0.0 copy-done.2
  44.5 0.0 copy-done.3
  44.5 0.0 copy-done.4
  44.6 0.1 pad_add_fusion.place_ref
  44.6 3.1 %load.1 = (bf16[576,4096]{1,0:T(8,128)(2,1)S(1)}, bf16[192,4096]{1,0:T(8,128)(2,1)S(1)}) custom-call(s32[3]{0:T(128)S(1)} %pad_add_fusion.place_ref, bf16[8,4,12,8,128]{4,3,2,1,0:T(8,128)(2,1)S(1)} %bitcast.8, bf16[576,4096]{1,0:T(8,128)(2,1)} %shift.1.shifted_ref), custom_call_target="tpu_custom_call" | custom-call | tf_op jit(solution)/shard_map/load/pallas_call | solution.py:118
  47.8 0.0 collective-permute-done
  47.8 2.9 %scores.1 = (f32[192,576]{1,0:T(8,128)S(1)}, f32[8,2,576]{2,1,0:T(2,128)S(1)}, bf16[192,4096]{1,0:T(8,128)(2,1)S(1)}) custom-call(s32[3]{0:T(128)S(1)} %pad_add_fusion.place_ref, bf16[8,4,12,8,128]{4,3,2,1,0:T(8,128)(2,1)S(1)} %bitcast.9, bf16[192,4096]{1,0:T(8,128)(2,1)S(1)} %get-tuple-element.17.half_ref, ...), custom_call_target="tpu_custom_call", output_to_operand_aliasing={{2}: (2, {})} | custom-call | tf_op jit(solution)/shard_map/scores/pallas_call | solution.py:156
  50.7 24.8 %all_to_all.26.stats_ref = f32[8,2,576]{2,1,0:T(2,128)S(1)} all-to-all(f32[8,2,576]{2,1,0:T(2,128)S(1)} %get-tuple-element.19), channel_id=1, replica_groups=mesh['y'=4,'za'=2,'zb'=4,'c'=2,'zh'=2,'x'=4] {'zh','x'}, dimensions={0} | all-to-all | bytes 73728 | tf_op jit(solution)/shard_map/all_to_all | solution.py:80
  75.6 2.5 %sums.1 = (f32[4,97,8,128]{3,2,1,0:T(8,128)S(1)}, bf16[4,97,8,128]{3,2,1,0:T(8,128)(2,1)S(1)}, f32[576]{0:T(1024)}) custom-call(s32[3]{0:T(128)S(1)} %pad_add_fusion.place_ref, f32[8,2,576]{2,1,0:T(2,128)S(1)} %all_to_all.26.stats_ref, f32[192,576]{1,0:T(8,128)S(1)} %get-tuple-element.20.scores_ref, bf16[576,4096]{1,0:T(8,128)(2,1)S(1)} %get-tuple-element.18.shifted_ref), custom_call_target="tpu_custom_call" | custom-call | tf_op jit(solution)/shard_map/sums/pallas_call | solution.py:220
  78.0 1.9 %collective-permute-start.1 = (bf16[4,97,8,128]{3,2,1,0:T(8,128)(2,1)S(1)}, bf16[4,97,8,128]{3,2,1,0:T(8,128)(2,1)S(1)}, u32[]{:S(2)}, u32[]{:S(2)}) collective-permute-start(bf16[4,97,8,128]{3,2,1,0:T(8,128)(2,1)S(1)} %get-tuple-element.22), channel_id=1, source_target_pairs={{0,8},{8,0},{1,9},{9,1},{2,10},{10,2},{3,11},{11,3},{4,12},{12,4},... | collective-permute-start | bytes 2383880 | tf_op jit(solution)/shard_map/ppermute | solution.py:260
  80.0 2.3 %collective-permute-done.1 = bf16[4,97,8,128]{3,2,1,0:T(8,128)(2,1)S(1)} collective-permute-done((bf16[4,97,8,128]{3,2,1,0:T(8,128)(2,1)S(1)}, bf16[4,97,8,128]{3,2,1,0:T(8,128)(2,1)S(1)}, u32[]{:S(2)}, u32[]{:S(2)}) %collective-permute-start.1) | collective-permute-done | bytes 794656 | tf_op jit(solution)/shard_map/ppermute | solution.py:260
  82.2 0.2 add_convert_fusion
  82.4 15.4 %all_to_all.27.pieces_ref = bf16[4,97,8,128]{3,2,1,0:T(8,128)(2,1)S(1)} all-to-all(bf16[4,97,8,128]{3,2,1,0:T(8,128)(2,1)S(1)} %add_convert_fusion), channel_id=1, replica_groups=mesh['y'=4,'za'=2,'zb'=4,'c'=2,'zh'=2,'x'=4] {'y'}, dimensions={0} | all-to-all | bytes 1589248 | tf_op jit(solution)/shard_map/all_to_all | solution.py:80
  97.8 0.1 fold.1
  97.9 21.7 %all_to_all.28.pieces_ref = bf16[8,13,8,128]{3,2,1,0:T(8,128)(2,1)S(1)} all-to-all(bf16[8,13,8,128]{3,2,1,0:T(8,128)(2,1)S(1)} %fold.1), channel_id=1, replica_groups=mesh['y'=4,'za'=2,'zb'=4,'c'=2,'zh'=2,'x'=4] {'za','zb'}, dimensions={0} | all-to-all | bytes 425984 | tf_op jit(solution)/shard_map/all_to_all | solution.py:80
  119.6 1.3 %finish.1 = f32[8,1536]{1,0:T(8,128)} custom-call(s32[3]{0:T(128)S(1)} %pad_add_fusion.place_ref, bf16[8,13,8,128]{3,2,1,0:T(8,128)(2,1)S(1)} %all_to_all.28.pieces_ref), custom_call_target="tpu_custom_call" | custom-call | tf_op jit(solution)/shard_map/finish/pallas_call | solution.py:271
  (3 shorter events, 0.0 us)
Async XLA Ops:
  0.6 32.4 %copy-start.1 = (s32[576]{0:T(1024)S(1)}, s32[576]{0:T(1024)}, u32[]{:S(2)}) copy-start(s32[576]{0:T(1024)} %param.8) | copy-start | bytes 6916
  1.4 31.8 %copy-start = (bf16[128,4096]{1,0:T(8,128)(2,1)S(1)}, bf16[128,4096]{1,0:T(8,128)(2,1)}, u32[]{:S(2)}) copy-start(bf16[128,4096]{1,0:T(8,128)(2,1)} %constant.26.clone.table_ref) | copy-start | bytes 3145732
  28.6 14.0 %all-to-all-start.1 = ((bf16[4,8,12,8,128]{4,3,2,1,0:T(8,128)(2,1)}), bf16[4,8,12,8,128]{4,3,2,1,0:T(8,128)(2,1)S(1)}, u32[]{:S(2)}, u32[]{:S(2)}) async-start(bf16[4,8,12,8,128]{4,3,2,1,0:T(8,128)(2,1)} %broadcast_in_dim.19), calls=%async_computation.1 | async-start | bytes 1572864 | tf_op jit(solution)/shard_map/all_to_all | solution.py:80
  33.2 11.3 %copy-start.2 = (s32[576]{0:T(1024)S(1)}, s32[576]{0:T(1024)}, u32[]{:S(2)}) copy-start(s32[576]{0:T(1024)} %param.9) | copy-start | bytes 6916
  33.2 11.3 %copy-start.3 = (s32[576]{0:T(1024)S(1)}, s32[576]{0:T(1024)}, u32[]{:S(2)}) copy-start(s32[576]{0:T(1024)} %param.10) | copy-start | bytes 6916
  33.2 11.3 %copy-start.4 = (f32[576]{0:T(1024)S(1)}, f32[576]{0:T(1024)}, u32[]{:S(2)}) copy-start(f32[576]{0:T(1024)} %param.11) | copy-start | bytes 6916
  42.6 5.2 %collective-permute-start = (bf16[4,8,12,8,128]{4,3,2,1,0:T(8,128)(2,1)S(1)}, bf16[4,8,12,8,128]{4,3,2,1,0:T(8,128)(2,1)S(1)}, u32[]{:S(2)}, u32[]{:S(2)}) collective-permute-start(bf16[4,8,12,8,128]{4,3,2,1,0:T(8,128)(2,1)S(1)} %all-to-all-done.1), channel_id=1, source_target_pairs={{0,8},{8,0},{1,9},{9,1},{2,10},{10,2},{3,11},{11,3},{4,12},{12,4},... | collective-permute-start | bytes 2359304 | tf_op jit(solution)/shard_map/ppermute | solution.py:89
  78.0 4.2 %collective-permute-start.1 = (bf16[4,97,8,128]{3,2,1,0:T(8,128)(2,1)S(1)}, bf16[4,97,8,128]{3,2,1,0:T(8,128)(2,1)S(1)}, u32[]{:S(2)}, u32[]{:S(2)}) collective-permute-start(bf16[4,97,8,128]{3,2,1,0:T(8,128)(2,1)S(1)} %get-tuple-element.22), channel_id=1, source_target_pairs={{0,8},{8,0},{1,9},{9,1},{2,10},{10,2},{3,11},{11,3},{4,12},{12,4},... | collective-permute-start | bytes 2383880 | tf_op jit(solution)/shard_map/ppermute | solution.py:260

commit v8 on v7

--- a/solution.py
+++ b/solution.py
@@ -102,32 +102,32 @@
                 table_ref[rows, pl.ds(pl.multiple_of(column + lanes * 128, 128), 128)] = tiles
 
 
-def load_kernel(place_ref, own_ref, shifted_ref, images_ref, table_ref, arrived):
+def load_kernel(own_ref, shifted_ref, images_ref, table_ref, arrived):
     copies = []
     for q in range(8):
         columns = pl.ds(q * 512, 512)
         copies.append(pltpu.make_async_copy(shifted_ref.at[:, columns], images_ref.at[:, columns], arrived.at[q]))
         copies[-1].start()
-    fill_table(own_ref, table_ref, place_ref[0])
+    fill_table(own_ref, table_ref, lax.axis_index("c"))
     for copy in copies:
         copy.wait()
 
 
-def load_own(place, own, shifted):
+def load_own(own, shifted):
     vmem = pl.BlockSpec(memory_space=pltpu.VMEM)
     return pl.pallas_call(
         load_kernel,
-        in_specs=[pl.BlockSpec(memory_space=pltpu.SMEM), vmem, pl.BlockSpec(memory_space=pltpu.HBM)],
+        in_specs=[vmem, pl.BlockSpec(memory_space=pltpu.HBM)],
         out_specs=[vmem, vmem],
         out_shape=[pltpu.VMEM((P_DEV, F), bf16), pltpu.VMEM((ROWS, F), bf16)],
         scratch_shapes=[pltpu.SemaphoreType.DMA((8,))],
         compiler_params=pltpu.CompilerParams(vmem_limit_bytes=16 << 20),
         name="load",
-    )(place, own, pltpu.with_memory_space_constraint(shifted, pltpu.HBM))
-
-
-def score_kernel(place_ref, other_ref, half_ref, shifted_ref, class_ref, rotation_ref, precision_ref, scores_ref, stats_ref, table_ref):
-    fill_table(other_ref, table_ref, 1 - place_ref[0])
+    )(own, pltpu.with_memory_space_constraint(shifted, pltpu.HBM))
+
+
+def score_kernel(other_ref, half_ref, shifted_ref, class_ref, rotation_ref, precision_ref, scores_ref, stats_ref, table_ref):
+    fill_table(other_ref, table_ref, 1 - lax.axis_index("c"))
     half_norm = jnp.zeros((ROWS, 128), f32)
     for at in range(0, F, 128):
         piece = table_ref[:, at : at + 128].astype(f32)
@@ -135,7 +135,7 @@
     half_norm = 0.5 * jnp.sum(half_norm, axis=1, keepdims=True)
     correlation = lax.dot_general(table_ref[...], shifted_ref[...], (((1,), (1,)), ((), ())), preferred_element_type=f32)
     row = lax.broadcasted_iota(jnp.int32, (ROWS, 1), 0)
-    class_ids = place_ref[1] + row % K
+    class_ids = lax.axis_index(CLS) * K + row % K
     rotation_ids = (row // K) % 8 * 3 + row // 64
     distance = jnp.abs(rotation_ids - rotation_ref[...])
     distance = jnp.minimum(distance, R - distance).astype(f32)
@@ -150,22 +150,22 @@
         stats_ref[at, 1:2, :] = mass
 
 
-def local_scores(place, own, other, shifted, prev_class, prev_rotation, precision):
-    images, half = load_own(place, own, shifted)
+def local_scores(own, other, shifted, prev_class, prev_rotation, precision):
+    images, half = load_own(own, shifted)
     vmem = pl.BlockSpec(memory_space=pltpu.VMEM)
     scores, stats, _ = pl.pallas_call(
         score_kernel,
-        in_specs=[pl.BlockSpec(memory_space=pltpu.SMEM)] + [vmem] * 6,
+        in_specs=[vmem] * 6,
         out_specs=[vmem, vmem, vmem],
         out_shape=[jax.ShapeDtypeStruct((ROWS, P_DEV), f32), jax.ShapeDtypeStruct((8, 2, P_DEV), f32), pltpu.VMEM((ROWS, F), bf16)],
-        input_output_aliases={2: 2},
+        input_output_aliases={1: 2},
         compiler_params=pltpu.CompilerParams(vmem_limit_bytes=16 << 20),
         name="scores",
-    )(place, other, half, images, prev_class[None, :], prev_rotation[None, :], precision[None, :])
+    )(other, half, images, prev_class[None, :], prev_rotation[None, :], precision[None, :])
     return scores, stats, images
 
 
-def sum_kernel(place_ref, stats_ref, scores_ref, shifted_ref, keep_ref, send_ref, evidence_ref):
+def sum_kernel(stats_ref, scores_ref, shifted_ref, keep_ref, send_ref, evidence_ref):
     tops = [stats_ref[i, 0:1, :] for i in range(8)]
     top = tops[0]
     for i in range(1, 8):
@@ -192,7 +192,7 @@
                 masses[to] = jnp.where(lane == at, spread_high, masses[to])
                 masses[to] = jnp.where(lane == at + 3, spread_low, masses[to])
 
-    swap = place_ref[0] == 1
+    swap = lax.axis_index("c") == 1
     numerators = {}
     for q in range(8):
         numerator = jnp.dot(weights, shifted_ref[:, q * 512 : q * 512 + 512], preferred_element_type=f32)
@@ -215,11 +215,11 @@
     send_ref[:, PIECES] = jnp.where(swap, masses[0], masses[1]).astype(bf16)
 
 
-def local_sums(place, stats, scores, shifted):
+def local_sums(stats, scores, shifted):
     vmem = pl.BlockSpec(memory_space=pltpu.VMEM)
     return pl.pallas_call(
         sum_kernel,
-        in_specs=[pl.BlockSpec(memory_space=pltpu.SMEM)] + [vmem] * 3,
+        in_specs=[vmem] * 3,
         out_specs=[vmem, vmem, vmem],
         out_shape=[
             jax.ShapeDtypeStruct((4, PIECES + 1, K, 128), f32),
@@ -228,7 +228,7 @@
         ],
         compiler_params=pltpu.CompilerParams(vmem_limit_bytes=16 << 20),
         name="sums",
-    )(place, stats, scores, shifted)
+    )(stats, scores, shifted)
 
 
 def fold_kernel(pieces_ref, out_ref):
@@ -241,11 +241,11 @@
         out_ref[i, TILES] = total[PIECES]
 
 
-def finish_kernel(place_ref, pieces_ref, out_ref):
+def finish_kernel(pieces_ref, out_ref):
     total = pieces_ref[0].astype(f32)
     for i in range(1, 8):
         total = total + pieces_ref[i].astype(f32)
-    lane = lax.broadcasted_iota(jnp.int32, (K, 128), 1) - 6 * place_ref[2]
+    lane = lax.broadcasted_iota(jnp.int32, (K, 128), 1) - 6 * lax.axis_index(Z)
     for b in range(3):
         picked = jnp.where((lane == b) | (lane == b + 3), total[TILES], 0.0)
         scale = 1.0 / (jnp.sum(picked, axis=1, keepdims=True) + 1.0)
@@ -254,7 +254,7 @@
             out_ref[:, at * 128 : at * 128 + 128] = total[at] * scale
 
 
-def scatter_sums(place, keep, send):
+def scatter_sums(keep, send):
     vmem = pl.BlockSpec(memory_space=pltpu.VMEM)
     params = pltpu.CompilerParams(vmem_limit_bytes=16 << 20)
     received = lax.ppermute(send, "c", [(0, 1), (1, 0)])
@@ -270,21 +270,20 @@
     pieces = exchange(pieces, Z)
     return pl.pallas_call(
         finish_kernel,
-        in_specs=[pl.BlockSpec(memory_space=pltpu.SMEM), vmem],
+        in_specs=[vmem],
         out_specs=vmem,
         out_shape=jax.ShapeDtypeStruct((K, TILES * 128), f32),
         compiler_params=params,
         name="finish",
-    )(place, pieces)
+    )(pieces)
 
 
 def on_device(particles, shift_index, prev_class, prev_rotation, precision, references):
-    place = jnp.stack([lax.axis_index("c"), lax.axis_index(CLS) * K, lax.axis_index(Z)]).astype(jnp.int32)
     own, other, shifted = gather_table(references, particles, shift_index)
-    scores, stats, images = local_scores(place, own, other, shifted, prev_class, prev_rotation, precision)
+    scores, stats, images = local_scores(own, other, shifted, prev_class, prev_rotation, precision)
     stats = exchange(stats, CLS)
-    keep, send, evidence = local_sums(place, stats, scores, images)
-    return (scatter_sums(place, keep, send), evidence)
+    keep, send, evidence = local_sums(stats, scores, images)
+    return (scatter_sums(keep, send), evidence)
 
 
 def solution(mesh):

time: 121 us -> 119 us (0.983)
  Pallas kernels: 16.1 us -> 13.9 us
    pallas_call x4, Pallas kernels: 9.8 us -> 7.59 us  [the longest x1 2.56 us: load_own(): pl.pallas_call(load_kernel, in_specs=[vmem, pl.BlockSpec(memory_space=plt...]
  transfers between devices with their start and end apart: 3 -> 3, of which waited for: 2 -> 2; matrix products, arithmetic and copies ran while one was open for 0% -> 0% of each run, Pallas kernels for 8% -> 7%
where the time goes in v8:
time: 119 us
  blocking collectives  88.1 us (74%)
  Pallas kernels  13.9 us (12%)
  starting transfers between devices  8.28 us (7%)
  waiting for transfers between devices  5.41 us (5%)
  local copies, waits for them, and re-layouts  1.96 us (2%)
    all_to_all x4, blocking collectives, exchange(): return lax.all_to_all(array, axis, 0, 0, tiled=True)  88.1 us
    pallas_call x1, Pallas kernels, shift_particles(): pl.pallas_call(shift_kernel, grid=(P_DEV // ROW_BLOCK,), in_specs=[pl.Blo...  6.16 us
    all_to_all x1, starting transfers between devices, exchange(): return lax.all_to_all(array, axis, 0, 0, tiled=True)  4.46 us
    all_to_all x1, waiting for transfers between devices, exchange(): return lax.all_to_all(array, axis, 0, 0, tiled=True)  3.14 us
    pallas_call x1, Pallas kernels, load_own(): pl.pallas_call(load_kernel, in_specs=[vmem, pl.BlockSpec(memory_space=plt...  2.56 us
  transfers between devices with their start and end apart: 3, of which 2 were waited for; matrix products, arithmetic and copies ran while one was open for 0% of the time, Pallas kernels for 7%

profile of v8, /device:TPU:32, one launch (start us, length us, event | category | flops | bytes accessed | tf_op | source)
XLA Modules:
  0.0 118.5 jit_solution(7054462999471355399)
XLA Ops:
  0.6 0.0 copy-start.1
  0.6 0.8 broadcast_in_dim.18
  1.4 0.0 copy-start
  1.4 26.2 %all_to_all.25 = bf16[8,12,8,128]{3,2,1,0:T(8,128)(2,1)S(1)} all-to-all(bf16[8,12,8,128]{3,2,1,0:T(8,128)(2,1)S(1)} %broadcast_in_dim.18), channel_id=1, replica_groups=mesh['y'=4,'za'=2,'zb'=4,'c'=2,'zh'=2,'x'=4] {'za','zb'}, dimensions={0} | all-to-all | bytes 393216 | tf_op jit(solution)/shard_map/all_to_all | solution.py:80
  27.6 1.0 broadcast_in_dim.19
  28.6 4.5 %all-to-all-start.1 = ((bf16[4,8,12,8,128]{4,3,2,1,0:T(8,128)(2,1)}), bf16[4,8,12,8,128]{4,3,2,1,0:T(8,128)(2,1)S(1)}, u32[]{:S(2)}, u32[]{:S(2)}) async-start(bf16[4,8,12,8,128]{4,3,2,1,0:T(8,128)(2,1)} %broadcast_in_dim.19), calls=%async_computation.1 | async-start | bytes 1572864 | tf_op jit(solution)/shard_map/all_to_all | solution.py:80
  33.1 0.0 copy-done.1
  33.1 0.1 broadcast_in_dim.24.index_ref
  33.2 0.0 copy-done
  33.2 0.0 copy-start.2
  33.2 0.0 copy-start.3
  33.2 0.0 copy-start.4
  33.3 6.2 %shift.1.shifted_ref = bf16[576,4096]{1,0:T(8,128)(2,1)} custom-call(s32[576,1]{1,0:T(8,128)S(1)} %broadcast_in_dim.24.index_ref, bf16[128,4096]{1,0:T(8,128)(2,1)S(1)} %copy-done, bf16[576,4096]{1,0:T(8,128)(2,1)} %image_ref.1), custom_call_target="tpu_custom_call" | custom-call | tf_op jit(solution)/shard_map/shift/pallas_call | solution.py:64
  39.4 3.1 %all-to-all-done.1 = bf16[4,8,12,8,128]{4,3,2,1,0:T(8,128)(2,1)S(1)} async-done(((bf16[4,8,12,8,128]{4,3,2,1,0:T(8,128)(2,1)}), bf16[4,8,12,8,128]{4,3,2,1,0:T(8,128)(2,1)S(1)}, u32[]{:S(2)}, u32[]{:S(2)}) %all-to-all-start.1) | async-done | bytes 786464 | tf_op jit(solution)/shard_map/all_to_all | solution.py:80
  42.6 1.9 %collective-permute-start = (bf16[4,8,12,8,128]{4,3,2,1,0:T(8,128)(2,1)S(1)}, bf16[4,8,12,8,128]{4,3,2,1,0:T(8,128)(2,1)S(1)}, u32[]{:S(2)}, u32[]{:S(2)}) collective-permute-start(bf16[4,8,12,8,128]{4,3,2,1,0:T(8,128)(2,1)S(1)} %all-to-all-done.1), channel_id=1, source_target_pairs={{0,8},{8,0},{1,9},{9,1},{2,10},{10,2},{3,11},{11,3},{4,12},{12,4},... | collective-permute-start | bytes 2359304 | tf_op jit(solution)/shard_map/ppermute | solution.py:89
  44.5 0.0 copy-done.2
  44.5 0.0 copy-done.3
  44.5 0.0 copy-done.4
  44.5 2.6 %load.1 = (bf16[576,4096]{1,0:T(8,128)(2,1)S(1)}, bf16[192,4096]{1,0:T(8,128)(2,1)S(1)}) custom-call(bf16[8,4,12,8,128]{4,3,2,1,0:T(8,128)(2,1)S(1)} %bitcast.5, bf16[576,4096]{1,0:T(8,128)(2,1)} %shift.1.shifted_ref), custom_call_target="tpu_custom_call" | custom-call | tf_op jit(solution)/shard_map/load/pallas_call | solution.py:118
  47.1 0.0 collective-permute-done
  47.1 2.4 %scores.1 = (f32[192,576]{1,0:T(8,128)S(1)}, f32[8,2,576]{2,1,0:T(2,128)S(1)}, bf16[192,4096]{1,0:T(8,128)(2,1)S(1)}) custom-call(bf16[8,4,12,8,128]{4,3,2,1,0:T(8,128)(2,1)S(1)} %bitcast.6, bf16[192,4096]{1,0:T(8,128)(2,1)S(1)} %get-tuple-element.17.half_ref, bf16[576,4096]{1,0:T(8,128)(2,1)S(1)} %get-tuple-element.18.shifted_ref, ...), custom_call_target="tpu_custom_call", output_to_operand_aliasing={{2}: (1, {})} | custom-call | tf_op jit(solution)/shard_map/scores/pallas_call | solution.py:156
  49.5 24.8 %all_to_all.26.stats_ref = f32[8,2,576]{2,1,0:T(2,128)S(1)} all-to-all(f32[8,2,576]{2,1,0:T(2,128)S(1)} %get-tuple-element.19), channel_id=1, replica_groups=mesh['y'=4,'za'=2,'zb'=4,'c'=2,'zh'=2,'x'=4] {'zh','x'}, dimensions={0} | all-to-all | bytes 73728 | tf_op jit(solution)/shard_map/all_to_all | solution.py:80
  74.3 1.9 %sums.1 = (f32[4,97,8,128]{3,2,1,0:T(8,128)S(1)}, bf16[4,97,8,128]{3,2,1,0:T(8,128)(2,1)S(1)}, f32[576]{0:T(1024)}) custom-call(f32[8,2,576]{2,1,0:T(2,128)S(1)} %all_to_all.26.stats_ref, f32[192,576]{1,0:T(8,128)S(1)} %get-tuple-element.20.scores_ref, bf16[576,4096]{1,0:T(8,128)(2,1)S(1)} %get-tuple-element.18.shifted_ref), custom_call_target="tpu_custom_call" | custom-call | tf_op jit(solution)/shard_map/sums/pallas_call | solution.py:220
  76.3 1.9 %collective-permute-start.1 = (bf16[4,97,8,128]{3,2,1,0:T(8,128)(2,1)S(1)}, bf16[4,97,8,128]{3,2,1,0:T(8,128)(2,1)S(1)}, u32[]{:S(2)}, u32[]{:S(2)}) collective-permute-start(bf16[4,97,8,128]{3,2,1,0:T(8,128)(2,1)S(1)} %get-tuple-element.22), channel_id=1, source_target_pairs={{0,8},{8,0},{1,9},{9,1},{2,10},{10,2},{3,11},{11,3},{4,12},{12,4},... | collective-permute-start | bytes 2383880 | tf_op jit(solution)/shard_map/ppermute | solution.py:260
  78.2 2.3 %collective-permute-done.1 = bf16[4,97,8,128]{3,2,1,0:T(8,128)(2,1)S(1)} collective-permute-done((bf16[4,97,8,128]{3,2,1,0:T(8,128)(2,1)S(1)}, bf16[4,97,8,128]{3,2,1,0:T(8,128)(2,1)S(1)}, u32[]{:S(2)}, u32[]{:S(2)}) %collective-permute-start.1) | collective-permute-done | bytes 794656 | tf_op jit(solution)/shard_map/ppermute | solution.py:260
  80.5 0.2 add_convert_fusion
  80.6 15.4 %all_to_all.27.pieces_ref = bf16[4,97,8,128]{3,2,1,0:T(8,128)(2,1)S(1)} all-to-all(bf16[4,97,8,128]{3,2,1,0:T(8,128)(2,1)S(1)} %add_convert_fusion), channel_id=1, replica_groups=mesh['y'=4,'za'=2,'zb'=4,'c'=2,'zh'=2,'x'=4] {'y'}, dimensions={0} | all-to-all | bytes 1589248 | tf_op jit(solution)/shard_map/all_to_all | solution.py:80
  96.0 0.1 fold.1
  96.1 21.7 %all_to_all.28.pieces_ref = bf16[8,13,8,128]{3,2,1,0:T(8,128)(2,1)S(1)} all-to-all(bf16[8,13,8,128]{3,2,1,0:T(8,128)(2,1)S(1)} %fold.1), channel_id=1, replica_groups=mesh['y'=4,'za'=2,'zb'=4,'c'=2,'zh'=2,'x'=4] {'za','zb'}, dimensions={0} | all-to-all | bytes 425984 | tf_op jit(solution)/shard_map/all_to_all | solution.py:80
  117.8 0.7 finish.1
  (3 shorter events, 0.0 us)
Async XLA Ops:
  0.6 32.4 %copy-start.1 = (s32[576]{0:T(1024)S(1)}, s32[576]{0:T(1024)}, u32[]{:S(2)}) copy-start(s32[576]{0:T(1024)} %param.8) | copy-start | bytes 6916
  1.4 31.8 %copy-start = (bf16[128,4096]{1,0:T(8,128)(2,1)S(1)}, bf16[128,4096]{1,0:T(8,128)(2,1)}, u32[]{:S(2)}) copy-start(bf16[128,4096]{1,0:T(8,128)(2,1)} %constant.2.clone.table_ref) | copy-start | bytes 3145732
  28.6 14.0 %all-to-all-start.1 = ((bf16[4,8,12,8,128]{4,3,2,1,0:T(8,128)(2,1)}), bf16[4,8,12,8,128]{4,3,2,1,0:T(8,128)(2,1)S(1)}, u32[]{:S(2)}, u32[]{:S(2)}) async-start(bf16[4,8,12,8,128]{4,3,2,1,0:T(8,128)(2,1)} %broadcast_in_dim.19), calls=%async_computation.1 | async-start | bytes 1572864 | tf_op jit(solution)/shard_map/all_to_all | solution.py:80
  33.2 11.3 %copy-start.2 = (s32[576]{0:T(1024)S(1)}, s32[576]{0:T(1024)}, u32[]{:S(2)}) copy-start(s32[576]{0:T(1024)} %param.9) | copy-start | bytes 6916
  33.2 11.3 %copy-start.3 = (s32[576]{0:T(1024)S(1)}, s32[576]{0:T(1024)}, u32[]{:S(2)}) copy-start(s32[576]{0:T(1024)} %param.10) | copy-start | bytes 6916
  33.2 11.3 %copy-start.4 = (f32[576]{0:T(1024)S(1)}, f32[576]{0:T(1024)}, u32[]{:S(2)}) copy-start(f32[576]{0:T(1024)} %param.11) | copy-start | bytes 6916
  42.6 4.6 %collective-permute-start = (bf16[4,8,12,8,128]{4,3,2,1,0:T(8,128)(2,1)S(1)}, bf16[4,8,12,8,128]{4,3,2,1,0:T(8,128)(2,1)S(1)}, u32[]{:S(2)}, u32[]{:S(2)}) collective-permute-start(bf16[4,8,12,8,128]{4,3,2,1,0:T(8,128)(2,1)S(1)} %all-to-all-done.1), channel_id=1, source_target_pairs={{0,8},{8,0},{1,9},{9,1},{2,10},{10,2},{3,11},{11,3},{4,12},{12,4},... | collective-permute-start | bytes 2359304 | tf_op jit(solution)/shard_map/ppermute | solution.py:89
  76.3 4.2 %collective-permute-start.1 = (bf16[4,97,8,128]{3,2,1,0:T(8,128)(2,1)S(1)}, bf16[4,97,8,128]{3,2,1,0:T(8,128)(2,1)S(1)}, u32[]{:S(2)}, u32[]{:S(2)}) collective-permute-start(bf16[4,97,8,128]{3,2,1,0:T(8,128)(2,1)S(1)} %get-tuple-element.22), channel_id=1, source_target_pairs={{0,8},{8,0},{1,9},{9,1},{2,10},{10,2},{3,11},{11,3},{4,12},{12,4},... | collective-permute-start | bytes 2383880 | tf_op jit(solution)/shard_map/ppermute | solution.py:260

commit v9 on v8

--- a/solution.py
+++ b/solution.py
@@ -83,9 +83,9 @@
 def gather_table(references, particles, shift_index):
     mine = references.reshape(K, TILES, 128).transpose(1, 0, 2)
     along_z = exchange(jnp.broadcast_to(mine, (8, TILES, K, 128)), Z)
-    along_z, index = lax.optimization_barrier((along_z, shift_index))
+    shifted = shift_particles(particles, shift_index[:, None], phase_table())
+    along_z, shifted = lax.optimization_barrier((along_z, shifted))
     along_y = exchange(jnp.broadcast_to(along_z, (4, 8, TILES, K, 128)), "y")
-    along_y, shifted = lax.optimization_barrier((along_y, shift_particles(particles, index[:, None], phase_table())))
     other = lax.ppermute(along_y, "c", [(0, 1), (1, 0)])
     return along_y.reshape(8, 4, TILES, K, 128), other.reshape(8, 4, TILES, K, 128), shifted
 
@@ -133,7 +133,7 @@
         piece = table_ref[:, at : at + 128].astype(f32)
         half_norm = half_norm + piece * piece
     half_norm = 0.5 * jnp.sum(half_norm, axis=1, keepdims=True)
-    correlation = lax.dot_general(table_ref[...], shifted_ref[...], (((1,), (1,)), ((), ())), preferred_element_type=f32)
+    correlation = lax.dot_general(shifted_ref[...], table_ref[...], (((1,), (1,)), ((), ())), preferred_element_type=f32).T
     row = lax.broadcasted_iota(jnp.int32, (ROWS, 1), 0)
     class_ids = lax.axis_index(CLS) * K + row % K
     rotation_ids = (row // K) % 8 * 3 + row // 64

time: 119 us -> 118 us (level)
  blocking collectives: 88.1 us -> 75.7 us
  starting transfers between devices: 8.28 us -> 16.4 us
  waiting for transfers between devices: 5.41 us -> 7.65 us
  local copies, waits for them, and re-layouts: 1.96 us -> 3.64 us
    all_to_all x4, blocking collectives: 88.1 us -> 75.7 us  [exchange(): return lax.all_to_all(array, axis, 0, 0, tiled=True)]
    all_to_all x1, starting transfers between devices: 4.46 us -> 12.6 us  [exchange(): return lax.all_to_all(array, axis, 0, 0, tiled=True)]
    all_to_all x1, waiting for transfers between devices: 3.14 us -> 5.38 us  [exchange(): return lax.all_to_all(array, axis, 0, 0, tiled=True)]
    unnamed x10 -> x8, local copies, waits for them, and re-layouts: 0.03 us -> 1.23 us
  transfers between devices with their start and end apart: 3 -> 3, of which waited for: 2 -> 2; matrix products, arithmetic and copies ran while one was open for 0% -> 1% of each run, Pallas kernels for 7% -> 7%
where the time goes in v9:
time: 118 us
  blocking collectives  75.7 us (64%)
  starting transfers between devices  16.4 us (14%)
  Pallas kernels  13.5 us (11%)
  waiting for transfers between devices  7.65 us (6%)
  local copies, waits for them, and re-layouts  3.64 us (3%)
    all_to_all x4, blocking collectives, exchange(): return lax.all_to_all(array, axis, 0, 0, tiled=True)  75.7 us
    all_to_all x1, starting transfers between devices, exchange(): return lax.all_to_all(array, axis, 0, 0, tiled=True)  12.6 us
    pallas_call x1, Pallas kernels, shift_particles(): pl.pallas_call(shift_kernel, grid=(P_DEV // ROW_BLOCK,), in_specs=[pl.Blo...  6.16 us
    all_to_all x1, waiting for transfers between devices, exchange(): return lax.all_to_all(array, axis, 0, 0, tiled=True)  5.38 us
    pallas_call x1, Pallas kernels, load_own(): pl.pallas_call(load_kernel, in_specs=[vmem, pl.BlockSpec(memory_space=plt...  2.56 us
  transfers between devices with their start and end apart: 3, of which 2 were waited for; matrix products, arithmetic and copies ran while one was open for 1% of the time, Pallas kernels for 7%

profile of v9, /device:TPU:32, one launch (start us, length us, event | category | flops | bytes accessed | tf_op | source)
XLA Modules:
  0.0 117.9 jit_solution(854207753805047901)
XLA Ops:
  0.6 1.5 %broadcast_in_dim.18 = bf16[8,12,8,128]{3,2,1,0:T(8,128)(2,1)} broadcast(bf16[12,8,128]{2,1,0:T(8,128)(2,1)} %bitcast.7), dimensions={1,2,3} | broadcast | bytes 221184 | tf_op jit(solution)/shard_map/broadcast_in_dim | solution.py:85
  2.1 12.6 %all-to-all-start = ((bf16[8,12,8,128]{3,2,1,0:T(8,128)(2,1)}), bf16[8,12,8,128]{3,2,1,0:T(8,128)(2,1)S(1)}, u32[]{:S(2)}, u32[]{:S(2)}) async-start(bf16[8,12,8,128]{3,2,1,0:T(8,128)(2,1)} %broadcast_in_dim.18), calls=%async_computation | async-start | bytes 393216 | tf_op jit(solution)/shard_map/all_to_all | solution.py:80
  14.7 0.8 broadcast_in_dim.24.index_ref
  15.6 0.0 copy-start
  15.6 1.2 %copy-done = bf16[128,4096]{1,0:T(8,128)(2,1)S(1)} copy-done((bf16[128,4096]{1,0:T(8,128)(2,1)S(1)}, bf16[128,4096]{1,0:T(8,128)(2,1)}, u32[]{:S(2)}) %copy-start) | copy-done | bytes 1048600
  16.8 6.2 %shift.1.shifted_ref = bf16[576,4096]{1,0:T(8,128)(2,1)} custom-call(s32[576,1]{1,0:T(8,128)S(1)} %broadcast_in_dim.24.index_ref, bf16[128,4096]{1,0:T(8,128)(2,1)S(1)} %copy-done, bf16[576,4096]{1,0:T(8,128)(2,1)} %image_ref.1), custom_call_target="tpu_custom_call" | custom-call | tf_op jit(solution)/shard_map/shift/pallas_call | solution.py:64
  22.9 0.0 copy-start.1
  22.9 0.0 copy-start.2
  22.9 0.0 copy-start.3
  22.9 5.4 %all-to-all-done = bf16[8,12,8,128]{3,2,1,0:T(8,128)(2,1)S(1)} async-done(((bf16[8,12,8,128]{3,2,1,0:T(8,128)(2,1)}), bf16[8,12,8,128]{3,2,1,0:T(8,128)(2,1)S(1)}, u32[]{:S(2)}, u32[]{:S(2)}) %all-to-all-start) | async-done | bytes 196640 | tf_op jit(solution)/shard_map/all_to_all | solution.py:80
  28.3 0.1 broadcast_in_dim.20
  28.4 13.8 %all_to_all.25 = bf16[4,8,12,8,128]{4,3,2,1,0:T(8,128)(2,1)S(1)} all-to-all(bf16[4,8,12,8,128]{4,3,2,1,0:T(8,128)(2,1)S(1)} %broadcast_in_dim.20), channel_id=1, replica_groups=mesh['y'=4,'za'=2,'zb'=4,'c'=2,'zh'=2,'x'=4] {'y'}, dimensions={0} | all-to-all | bytes 1572864 | tf_op jit(solution)/shard_map/all_to_all | solution.py:80
  42.2 1.9 %collective-permute-start = (bf16[4,8,12,8,128]{4,3,2,1,0:T(8,128)(2,1)S(1)}, bf16[4,8,12,8,128]{4,3,2,1,0:T(8,128)(2,1)S(1)}, u32[]{:S(2)}, u32[]{:S(2)}) collective-permute-start(bf16[4,8,12,8,128]{4,3,2,1,0:T(8,128)(2,1)S(1)} %all_to_all.25), channel_id=1, source_target_pairs={{0,8},{8,0},{1,9},{9,1},{2,10},{10,2},{3,11},{11,3},{4,12},{12,4},... | collective-permute-start | bytes 2359304 | tf_op jit(solution)/shard_map/ppermute | solution.py:89
  44.1 0.0 copy-done.1
  44.1 0.0 copy-done.2
  44.2 0.0 copy-done.3
  44.2 2.6 %load.1 = (bf16[576,4096]{1,0:T(8,128)(2,1)S(1)}, bf16[192,4096]{1,0:T(8,128)(2,1)S(1)}) custom-call(bf16[8,4,12,8,128]{4,3,2,1,0:T(8,128)(2,1)S(1)} %bitcast.5, bf16[576,4096]{1,0:T(8,128)(2,1)} %shift.1.shifted_ref), custom_call_target="tpu_custom_call" | custom-call | tf_op jit(solution)/shard_map/load/pallas_call | solution.py:118
  46.8 0.0 collective-permute-done
  46.8 2.1 %scores.1 = (f32[192,576]{1,0:T(8,128)S(1)}, f32[8,2,576]{2,1,0:T(2,128)S(1)}, bf16[192,4096]{1,0:T(8,128)(2,1)S(1)}) custom-call(bf16[8,4,12,8,128]{4,3,2,1,0:T(8,128)(2,1)S(1)} %bitcast.6, bf16[192,4096]{1,0:T(8,128)(2,1)S(1)} %get-tuple-element.13.half_ref, bf16[576,4096]{1,0:T(8,128)(2,1)S(1)} %get-tuple-element.14.shifted_ref, ...), custom_call_target="tpu_custom_call", output_to_operand_aliasing={{2}: (1, {})} | custom-call | tf_op jit(solution)/shard_map/scores/pallas_call | solution.py:156
  48.8 24.8 %all_to_all.26.stats_ref = f32[8,2,576]{2,1,0:T(2,128)S(1)} all-to-all(f32[8,2,576]{2,1,0:T(2,128)S(1)} %get-tuple-element.15), channel_id=1, replica_groups=mesh['y'=4,'za'=2,'zb'=4,'c'=2,'zh'=2,'x'=4] {'zh','x'}, dimensions={0} | all-to-all | bytes 73728 | tf_op jit(solution)/shard_map/all_to_all | solution.py:80
  73.7 1.9 %sums.1 = (f32[4,97,8,128]{3,2,1,0:T(8,128)S(1)}, bf16[4,97,8,128]{3,2,1,0:T(8,128)(2,1)S(1)}, f32[576]{0:T(1024)}) custom-call(f32[8,2,576]{2,1,0:T(2,128)S(1)} %all_to_all.26.stats_ref, f32[192,576]{1,0:T(8,128)S(1)} %get-tuple-element.16.scores_ref, bf16[576,4096]{1,0:T(8,128)(2,1)S(1)} %get-tuple-element.14.shifted_ref), custom_call_target="tpu_custom_call" | custom-call | tf_op jit(solution)/shard_map/sums/pallas_call | solution.py:220
  75.6 1.9 %collective-permute-start.1 = (bf16[4,97,8,128]{3,2,1,0:T(8,128)(2,1)S(1)}, bf16[4,97,8,128]{3,2,1,0:T(8,128)(2,1)S(1)}, u32[]{:S(2)}, u32[]{:S(2)}) collective-permute-start(bf16[4,97,8,128]{3,2,1,0:T(8,128)(2,1)S(1)} %get-tuple-element.18), channel_id=1, source_target_pairs={{0,8},{8,0},{1,9},{9,1},{2,10},{10,2},{3,11},{11,3},{4,12},{12,4},... | collective-permute-start | bytes 2383880 | tf_op jit(solution)/shard_map/ppermute | solution.py:260
  77.5 2.3 %collective-permute-done.1 = bf16[4,97,8,128]{3,2,1,0:T(8,128)(2,1)S(1)} collective-permute-done((bf16[4,97,8,128]{3,2,1,0:T(8,128)(2,1)S(1)}, bf16[4,97,8,128]{3,2,1,0:T(8,128)(2,1)S(1)}, u32[]{:S(2)}, u32[]{:S(2)}) %collective-permute-start.1) | collective-permute-done | bytes 794656 | tf_op jit(solution)/shard_map/ppermute | solution.py:260
  79.8 0.2 add_convert_fusion
  80.0 15.4 %all_to_all.27.pieces_ref = bf16[4,97,8,128]{3,2,1,0:T(8,128)(2,1)S(1)} all-to-all(bf16[4,97,8,128]{3,2,1,0:T(8,128)(2,1)S(1)} %add_convert_fusion), channel_id=1, replica_groups=mesh['y'=4,'za'=2,'zb'=4,'c'=2,'zh'=2,'x'=4] {'y'}, dimensions={0} | all-to-all | bytes 1589248 | tf_op jit(solution)/shard_map/all_to_all | solution.py:80
  95.3 0.1 fold.1
  95.4 21.7 %all_to_all.28.pieces_ref = bf16[8,13,8,128]{3,2,1,0:T(8,128)(2,1)S(1)} all-to-all(bf16[8,13,8,128]{3,2,1,0:T(8,128)(2,1)S(1)} %fold.1), channel_id=1, replica_groups=mesh['y'=4,'za'=2,'zb'=4,'c'=2,'zh'=2,'x'=4] {'za','zb'}, dimensions={0} | all-to-all | bytes 425984 | tf_op jit(solution)/shard_map/all_to_all | solution.py:80
  117.1 0.7 finish.1
  (3 shorter events, 0.0 us)
Async XLA Ops:
  2.1 26.2 %all-to-all-start = ((bf16[8,12,8,128]{3,2,1,0:T(8,128)(2,1)}), bf16[8,12,8,128]{3,2,1,0:T(8,128)(2,1)S(1)}, u32[]{:S(2)}, u32[]{:S(2)}) async-start(bf16[8,12,8,128]{3,2,1,0:T(8,128)(2,1)} %broadcast_in_dim.18), calls=%async_computation | async-start | bytes 393216 | tf_op jit(solution)/shard_map/all_to_all | solution.py:80
  15.6 1.2 %copy-start = (bf16[128,4096]{1,0:T(8,128)(2,1)S(1)}, bf16[128,4096]{1,0:T(8,128)(2,1)}, u32[]{:S(2)}) copy-start(bf16[128,4096]{1,0:T(8,128)(2,1)} %constant.2.clone.table_ref) | copy-start | bytes 3145732
  22.9 21.2 %copy-start.1 = (s32[576]{0:T(1024)S(1)}, s32[576]{0:T(1024)}, u32[]{:S(2)}) copy-start(s32[576]{0:T(1024)} %param.9) | copy-start | bytes 6916
  22.9 21.2 %copy-start.2 = (s32[576]{0:T(1024)S(1)}, s32[576]{0:T(1024)}, u32[]{:S(2)}) copy-start(s32[576]{0:T(1024)} %param.10) | copy-start | bytes 6916
  22.9 21.2 %copy-start.3 = (f32[576]{0:T(1024)S(1)}, f32[576]{0:T(1024)}, u32[]{:S(2)}) copy-start(f32[576]{0:T(1024)} %param.11) | copy-start | bytes 6916
  42.2 4.6 %collective-permute-start = (bf16[4,8,12,8,128]{4,3,2,1,0:T(8,128)(2,1)S(1)}, bf16[4,8,12,8,128]{4,3,2,1,0:T(8,128)(2,1)S(1)}, u32[]{:S(2)}, u32[]{:S(2)}) collective-permute-start(bf16[4,8,12,8,128]{4,3,2,1,0:T(8,128)(2,1)S(1)} %all_to_all.25), channel_id=1, source_target_pairs={{0,8},{8,0},{1,9},{9,1},{2,10},{10,2},{3,11},{11,3},{4,12},{12,4},... | collective-permute-start | bytes 2359304 | tf_op jit(solution)/shard_map/ppermute | solution.py:89
  75.6 4.2 %collective-permute-start.1 = (bf16[4,97,8,128]{3,2,1,0:T(8,128)(2,1)S(1)}, bf16[4,97,8,128]{3,2,1,0:T(8,128)(2,1)S(1)}, u32[]{:S(2)}, u32[]{:S(2)}) collective-permute-start(bf16[4,97,8,128]{3,2,1,0:T(8,128)(2,1)S(1)} %get-tuple-element.18), channel_id=1, source_target_pairs={{0,8},{8,0},{1,9},{9,1},{2,10},{10,2},{3,11},{11,3},{4,12},{12,4},... | collective-permute-start | bytes 2383880 | tf_op jit(solution)/shard_map/ppermute | solution.py:260

commit v10 on v8

--- a/solution.py
+++ b/solution.py
@@ -133,7 +133,7 @@
         piece = table_ref[:, at : at + 128].astype(f32)
         half_norm = half_norm + piece * piece
     half_norm = 0.5 * jnp.sum(half_norm, axis=1, keepdims=True)
-    correlation = lax.dot_general(table_ref[...], shifted_ref[...], (((1,), (1,)), ((), ())), preferred_element_type=f32)
+    correlation = lax.dot_general(shifted_ref[...], table_ref[...], (((1,), (1,)), ((), ())), preferred_element_type=f32).T
     row = lax.broadcasted_iota(jnp.int32, (ROWS, 1), 0)
     class_ids = lax.axis_index(CLS) * K + row % K
     rotation_ids = (row // K) % 8 * 3 + row // 64

time: 119 us -> 119 us (level)
  no operation moved by 1% of the time
where the time goes in v10:
time: 119 us; the launch traced here: 118 us
  blocking collectives  88.1 us (74%)
  Pallas kernels  13.5 us (11%)
  starting transfers between devices  8.28 us (7%)
  waiting for transfers between devices  5.41 us (5%)
  local copies, waits for them, and re-layouts  1.96 us (2%)
    all_to_all x4, blocking collectives, exchange(): return lax.all_to_all(array, axis, 0, 0, tiled=True)  88.1 us
    pallas_call x1, Pallas kernels, shift_particles(): pl.pallas_call(shift_kernel, grid=(P_DEV // ROW_BLOCK,), in_specs=[pl.Blo...  6.16 us
    all_to_all x1, starting transfers between devices, exchange(): return lax.all_to_all(array, axis, 0, 0, tiled=True)  4.46 us
    all_to_all x1, waiting for transfers between devices, exchange(): return lax.all_to_all(array, axis, 0, 0, tiled=True)  3.14 us
    pallas_call x1, Pallas kernels, load_own(): pl.pallas_call(load_kernel, in_specs=[vmem, pl.BlockSpec(memory_space=plt...  2.56 us
  transfers between devices with their start and end apart: 3, of which 2 were waited for; matrix products, arithmetic and copies ran while one was open for 0% of the time, Pallas kernels for 7%

profile of v10, /device:TPU:32, one launch (start us, length us, event | category | flops | bytes accessed | tf_op | source)
XLA Modules:
  0.0 118.2 jit_solution(7302338759169379161)
XLA Ops:
  0.6 0.0 copy-start.1
  0.6 0.8 broadcast_in_dim.18
  1.4 0.0 copy-start
  1.4 26.2 %all_to_all.25 = bf16[8,12,8,128]{3,2,1,0:T(8,128)(2,1)S(1)} all-to-all(bf16[8,12,8,128]{3,2,1,0:T(8,128)(2,1)S(1)} %broadcast_in_dim.18), channel_id=1, replica_groups=mesh['y'=4,'za'=2,'zb'=4,'c'=2,'zh'=2,'x'=4] {'za','zb'}, dimensions={0} | all-to-all | bytes 393216 | tf_op jit(solution)/shard_map/all_to_all | solution.py:80
  27.6 1.0 broadcast_in_dim.19
  28.6 4.5 %all-to-all-start.1 = ((bf16[4,8,12,8,128]{4,3,2,1,0:T(8,128)(2,1)}), bf16[4,8,12,8,128]{4,3,2,1,0:T(8,128)(2,1)S(1)}, u32[]{:S(2)}, u32[]{:S(2)}) async-start(bf16[4,8,12,8,128]{4,3,2,1,0:T(8,128)(2,1)} %broadcast_in_dim.19), calls=%async_computation.1 | async-start | bytes 1572864 | tf_op jit(solution)/shard_map/all_to_all | solution.py:80
  33.1 0.0 copy-done.1
  33.1 0.1 broadcast_in_dim.24.index_ref
  33.2 0.0 copy-done
  33.2 0.0 copy-start.2
  33.2 0.0 copy-start.3
  33.2 0.0 copy-start.4
  33.3 6.2 %shift.1.shifted_ref = bf16[576,4096]{1,0:T(8,128)(2,1)} custom-call(s32[576,1]{1,0:T(8,128)S(1)} %broadcast_in_dim.24.index_ref, bf16[128,4096]{1,0:T(8,128)(2,1)S(1)} %copy-done, bf16[576,4096]{1,0:T(8,128)(2,1)} %image_ref.1), custom_call_target="tpu_custom_call" | custom-call | tf_op jit(solution)/shard_map/shift/pallas_call | solution.py:64
  39.4 3.1 %all-to-all-done.1 = bf16[4,8,12,8,128]{4,3,2,1,0:T(8,128)(2,1)S(1)} async-done(((bf16[4,8,12,8,128]{4,3,2,1,0:T(8,128)(2,1)}), bf16[4,8,12,8,128]{4,3,2,1,0:T(8,128)(2,1)S(1)}, u32[]{:S(2)}, u32[]{:S(2)}) %all-to-all-start.1) | async-done | bytes 786464 | tf_op jit(solution)/shard_map/all_to_all | solution.py:80
  42.6 1.9 %collective-permute-start = (bf16[4,8,12,8,128]{4,3,2,1,0:T(8,128)(2,1)S(1)}, bf16[4,8,12,8,128]{4,3,2,1,0:T(8,128)(2,1)S(1)}, u32[]{:S(2)}, u32[]{:S(2)}) collective-permute-start(bf16[4,8,12,8,128]{4,3,2,1,0:T(8,128)(2,1)S(1)} %all-to-all-done.1), channel_id=1, source_target_pairs={{0,8},{8,0},{1,9},{9,1},{2,10},{10,2},{3,11},{11,3},{4,12},{12,4},... | collective-permute-start | bytes 2359304 | tf_op jit(solution)/shard_map/ppermute | solution.py:89
  44.5 0.0 copy-done.2
  44.5 0.0 copy-done.3
  44.5 0.0 copy-done.4
  44.5 2.6 %load.1 = (bf16[576,4096]{1,0:T(8,128)(2,1)S(1)}, bf16[192,4096]{1,0:T(8,128)(2,1)S(1)}) custom-call(bf16[8,4,12,8,128]{4,3,2,1,0:T(8,128)(2,1)S(1)} %bitcast.5, bf16[576,4096]{1,0:T(8,128)(2,1)} %shift.1.shifted_ref), custom_call_target="tpu_custom_call" | custom-call | tf_op jit(solution)/shard_map/load/pallas_call | solution.py:118
  47.1 0.0 collective-permute-done
  47.1 2.1 %scores.1 = (f32[192,576]{1,0:T(8,128)S(1)}, f32[8,2,576]{2,1,0:T(2,128)S(1)}, bf16[192,4096]{1,0:T(8,128)(2,1)S(1)}) custom-call(bf16[8,4,12,8,128]{4,3,2,1,0:T(8,128)(2,1)S(1)} %bitcast.6, bf16[192,4096]{1,0:T(8,128)(2,1)S(1)} %get-tuple-element.17.half_ref, bf16[576,4096]{1,0:T(8,128)(2,1)S(1)} %get-tuple-element.18.shifted_ref, ...), custom_call_target="tpu_custom_call", output_to_operand_aliasing={{2}: (1, {})} | custom-call | tf_op jit(solution)/shard_map/scores/pallas_call | solution.py:156
  49.2 24.8 %all_to_all.26.stats_ref = f32[8,2,576]{2,1,0:T(2,128)S(1)} all-to-all(f32[8,2,576]{2,1,0:T(2,128)S(1)} %get-tuple-element.19), channel_id=1, replica_groups=mesh['y'=4,'za'=2,'zb'=4,'c'=2,'zh'=2,'x'=4] {'zh','x'}, dimensions={0} | all-to-all | bytes 73728 | tf_op jit(solution)/shard_map/all_to_all | solution.py:80
  74.0 1.9 %sums.1 = (f32[4,97,8,128]{3,2,1,0:T(8,128)S(1)}, bf16[4,97,8,128]{3,2,1,0:T(8,128)(2,1)S(1)}, f32[576]{0:T(1024)}) custom-call(f32[8,2,576]{2,1,0:T(2,128)S(1)} %all_to_all.26.stats_ref, f32[192,576]{1,0:T(8,128)S(1)} %get-tuple-element.20.scores_ref, bf16[576,4096]{1,0:T(8,128)(2,1)S(1)} %get-tuple-element.18.shifted_ref), custom_call_target="tpu_custom_call" | custom-call | tf_op jit(solution)/shard_map/sums/pallas_call | solution.py:220
  76.0 1.9 %collective-permute-start.1 = (bf16[4,97,8,128]{3,2,1,0:T(8,128)(2,1)S(1)}, bf16[4,97,8,128]{3,2,1,0:T(8,128)(2,1)S(1)}, u32[]{:S(2)}, u32[]{:S(2)}) collective-permute-start(bf16[4,97,8,128]{3,2,1,0:T(8,128)(2,1)S(1)} %get-tuple-element.22), channel_id=1, source_target_pairs={{0,8},{8,0},{1,9},{9,1},{2,10},{10,2},{3,11},{11,3},{4,12},{12,4},... | collective-permute-start | bytes 2383880 | tf_op jit(solution)/shard_map/ppermute | solution.py:260
  77.9 2.3 %collective-permute-done.1 = bf16[4,97,8,128]{3,2,1,0:T(8,128)(2,1)S(1)} collective-permute-done((bf16[4,97,8,128]{3,2,1,0:T(8,128)(2,1)S(1)}, bf16[4,97,8,128]{3,2,1,0:T(8,128)(2,1)S(1)}, u32[]{:S(2)}, u32[]{:S(2)}) %collective-permute-start.1) | collective-permute-done | bytes 794656 | tf_op jit(solution)/shard_map/ppermute | solution.py:260
  80.1 0.2 add_convert_fusion
  80.3 15.4 %all_to_all.27.pieces_ref = bf16[4,97,8,128]{3,2,1,0:T(8,128)(2,1)S(1)} all-to-all(bf16[4,97,8,128]{3,2,1,0:T(8,128)(2,1)S(1)} %add_convert_fusion), channel_id=1, replica_groups=mesh['y'=4,'za'=2,'zb'=4,'c'=2,'zh'=2,'x'=4] {'y'}, dimensions={0} | all-to-all | bytes 1589248 | tf_op jit(solution)/shard_map/all_to_all | solution.py:80
  95.7 0.1 fold.1
  95.8 21.7 %all_to_all.28.pieces_ref = bf16[8,13,8,128]{3,2,1,0:T(8,128)(2,1)S(1)} all-to-all(bf16[8,13,8,128]{3,2,1,0:T(8,128)(2,1)S(1)} %fold.1), channel_id=1, replica_groups=mesh['y'=4,'za'=2,'zb'=4,'c'=2,'zh'=2,'x'=4] {'za','zb'}, dimensions={0} | all-to-all | bytes 425984 | tf_op jit(solution)/shard_map/all_to_all | solution.py:80
  117.5 0.7 finish.1
  (3 shorter events, 0.0 us)
Async XLA Ops:
  0.6 32.4 %copy-start.1 = (s32[576]{0:T(1024)S(1)}, s32[576]{0:T(1024)}, u32[]{:S(2)}) copy-start(s32[576]{0:T(1024)} %param.8) | copy-start | bytes 6916
  1.4 31.8 %copy-start = (bf16[128,4096]{1,0:T(8,128)(2,1)S(1)}, bf16[128,4096]{1,0:T(8,128)(2,1)}, u32[]{:S(2)}) copy-start(bf16[128,4096]{1,0:T(8,128)(2,1)} %constant.2.clone.table_ref) | copy-start | bytes 3145732
  28.6 14.0 %all-to-all-start.1 = ((bf16[4,8,12,8,128]{4,3,2,1,0:T(8,128)(2,1)}), bf16[4,8,12,8,128]{4,3,2,1,0:T(8,128)(2,1)S(1)}, u32[]{:S(2)}, u32[]{:S(2)}) async-start(bf16[4,8,12,8,128]{4,3,2,1,0:T(8,128)(2,1)} %broadcast_in_dim.19), calls=%async_computation.1 | async-start | bytes 1572864 | tf_op jit(solution)/shard_map/all_to_all | solution.py:80
  33.2 11.3 %copy-start.2 = (s32[576]{0:T(1024)S(1)}, s32[576]{0:T(1024)}, u32[]{:S(2)}) copy-start(s32[576]{0:T(1024)} %param.9) | copy-start | bytes 6916
  33.2 11.3 %copy-start.3 = (s32[576]{0:T(1024)S(1)}, s32[576]{0:T(1024)}, u32[]{:S(2)}) copy-start(s32[576]{0:T(1024)} %param.10) | copy-start | bytes 6916
  33.2 11.3 %copy-start.4 = (f32[576]{0:T(1024)S(1)}, f32[576]{0:T(1024)}, u32[]{:S(2)}) copy-start(f32[576]{0:T(1024)} %param.11) | copy-start | bytes 6916
  42.6 4.6 %collective-permute-start = (bf16[4,8,12,8,128]{4,3,2,1,0:T(8,128)(2,1)S(1)}, bf16[4,8,12,8,128]{4,3,2,1,0:T(8,128)(2,1)S(1)}, u32[]{:S(2)}, u32[]{:S(2)}) collective-permute-start(bf16[4,8,12,8,128]{4,3,2,1,0:T(8,128)(2,1)S(1)} %all-to-all-done.1), channel_id=1, source_target_pairs={{0,8},{8,0},{1,9},{9,1},{2,10},{10,2},{3,11},{11,3},{4,12},{12,4},... | collective-permute-start | bytes 2359304 | tf_op jit(solution)/shard_map/ppermute | solution.py:89
  76.0 4.2 %collective-permute-start.1 = (bf16[4,97,8,128]{3,2,1,0:T(8,128)(2,1)S(1)}, bf16[4,97,8,128]{3,2,1,0:T(8,128)(2,1)S(1)}, u32[]{:S(2)}, u32[]{:S(2)}) collective-permute-start(bf16[4,97,8,128]{3,2,1,0:T(8,128)(2,1)S(1)} %get-tuple-element.22), channel_id=1, source_target_pairs={{0,8},{8,0},{1,9},{9,1},{2,10},{10,2},{3,11},{11,3},{4,12},{12,4},... | collective-permute-start | bytes 2383880 | tf_op jit(solution)/shard_map/ppermute | solution.py:260
